TPU v7x, 32 devices: a whole 2x2x4 slice. The times are simulated.
32 devices in a mesh: batch: 8 (over y, x, core), kv: 4 (over z).
Axes of the slice: x: 2, y: 2, z: 4, core: 2. Of those that a mesh axis runs over, the one named last changes fastest.
Arguments:
- inputs: bfloat16 [8, 1024, 1024], P('batch'), may hold values from -6 to 6
- memory: bfloat16 [8, 1024, 1024], P('batch'), may hold values from -6 to 6
- out_grad: bfloat16 [8, 1024, 1024], P('batch'), may hold values from -6 to 6
- gain_self: bfloat16 [1024], replicated, may hold values from 0.5 to 1.5
- self_query: bfloat16 [1024, 1024], P(None, 'kv'), may hold values from -0.046875 to 0.046875
- self_key: bfloat16 [1024, 512], P(None, 'kv'), may hold values from -0.1875 to 0.1875
- self_value: bfloat16 [1024, 512], P(None, 'kv'), may hold values from -0.1875 to 0.1875
- self_output: bfloat16 [1024, 1024], P('kv'), may hold values from -0.75 to 0.75
- self_table: bfloat16 [32, 16], P(None, 'kv'), may hold values from -4 to 4
- gain_cross: bfloat16 [1024], replicated, may hold values from 0.5 to 1.5
- cross_query: bfloat16 [1024, 1024], P(None, 'kv'), may hold values from -0.046875 to 0.046875
- cross_key: bfloat16 [1024, 512], P(None, 'kv'), may hold values from -0.1875 to 0.1875
- cross_value: bfloat16 [1024, 512], P(None, 'kv'), may hold values from -0.1875 to 0.1875
- cross_output: bfloat16 [1024, 1024], P('kv'), may hold values from -0.75 to 0.75
- cross_table: bfloat16 [32, 16], P(None, 'kv'), may hold values from -4 to 4
- gain_ffn: bfloat16 [1024], replicated, may hold values from 0.5 to 1.5
- ffn_gate: bfloat16 [1024, 2816], P(None, 'kv'), may hold values from -0.1875 to 0.1875
- ffn_up: bfloat16 [1024, 2816], P(None, 'kv'), may hold values from -0.1875 to 0.1875
- ffn_down: bfloat16 [2816, 1024], P('kv'), may hold values from -0.109375 to 0.109375
Outputs:
- layer_out: bfloat16 [8, 1024, 1024], P('batch')
- input_grad: float32 [8, 1024, 1024], P('batch')
- memory_grad: float32 [8, 1024, 1024], P('batch', None, 'kv')
- grad_gain_self: float32 [1024], replicated
- grad_self_query: float32 [1024, 1024], P(None, 'kv')
- grad_self_key: float32 [1024, 512], P(None, 'kv')
- grad_self_value: float32 [1024, 512], P(None, 'kv')
- grad_self_output: float32 [1024, 1024], P('kv')
- grad_self_table: float32 [32, 16], P(None, 'kv')
- grad_gain_cross: float32 [1024], replicated
- grad_cross_query: float32 [1024, 1024], P(None, 'kv')
- grad_cross_key: float32 [1024, 512], P(None, 'kv')
- grad_cross_value: float32 [1024, 512], P(None, 'kv')
- grad_cross_output: float32 [1024, 1024], P('kv')
- grad_cross_table: float32 [32, 16], P(None, 'kv')
- grad_gain_ffn: float32 [1024], replicated
- grad_ffn_gate: float32 [1024, 2816], P(None, 'kv')
- grad_ffn_up: float32 [1024, 2816], P(None, 'kv')
- grad_ffn_down: float32 [2816, 1024], P('kv')
All inputs are finite; a program needn't handle non-finite values.
Results may differ from a plain program's by a relative error of at most 0.034.
The roundings to bfloat16 on the way count: a program that leaves them out, or rounds other values in their place, can miss the bound.
Values sent between devices are 32-bit elements; how exact they have to be, the bound alone decides.
No kernel may reach another device: no remote copies, remote signals or barrier semaphores. Data moves between devices by JAX's collectives and lax.ppermute only.
A program may use at most 192 MiB of HBM per device.

v0:
```python
import math

import jax
import jax.numpy as jnp
import numpy as np
from jax import lax
from jax.sharding import PartitionSpec as P

DH = 64
MAXDIST = 128


eps = 1e-06
masked_value = -1e30


def bucket_ids(extent, offset, buckets, reach):
    relative = np.arange(extent) - offset
    base_id = np.zeros(extent, np.int64)
    distance = np.maximum(-relative, 0)
    exact_end = buckets // 2
    scaled = np.log(np.maximum(distance, 1) / exact_end) / math.log(reach / exact_end)
    far_id = np.minimum(
        exact_end + np.floor(scaled * (buckets - exact_end)).astype(np.int64), buckets - 1
    )
    return np.where(distance < exact_end, distance, far_id) + base_id


def bucket_starts(extent, per_side):
    side_ids = bucket_ids(extent, extent - 1, per_side, MAXDIST)[::-1]
    starts = []
    for level in range(1, per_side):
        if side_ids[-1] >= level:
            starts.append(int(np.argmax(side_ids >= level)))
        else:
            starts.append(extent + 1)
    return starts


def block_buckets(start_row, block_rows, seq_len, key_len, two_sided, buckets):
    per_side = buckets // 2 if two_sided else buckets
    starts = bucket_starts(seq_len + key_len, per_side)
    query_pos = start_row + jnp.arange(block_rows, dtype=jnp.int32)
    key_pos = jnp.arange(key_len, dtype=jnp.int32)
    relative = key_pos[None, :] - query_pos[:, None]
    if two_sided:
        distance = jnp.abs(relative)
        level_ids = jnp.where(relative > 0, per_side, 0).astype(jnp.int32)
    else:
        distance = jnp.maximum(-relative, 0)
        level_ids = jnp.zeros(relative.shape, jnp.int32)
    for first_distance in starts:
        level_ids = level_ids + (distance >= first_distance).astype(jnp.int32)
    return (level_ids[:, :, None] == jnp.arange(buckets, dtype=jnp.int32)[None, None, :]).astype(
        jnp.bfloat16
    )


def norm_rows(hidden, gain_vec):
    inv_scale = lax.rsqrt(jnp.mean(hidden * hidden, axis=-1, keepdims=True) + eps)
    return hidden * inv_scale * gain_vec


def inner_rows(left_mat, right_mat):
    return lax.dot_general(
        left_mat, right_mat, (((0,), (0,)), ((), ())), preferred_element_type=jnp.float32
    )


def outer_cols(left_mat, right_mat):
    return lax.dot_general(
        left_mat, right_mat, (((1,), (1,)), ((), ())), preferred_element_type=jnp.float32
    )


def block_scores(query_block, key_block, bias_block, start_row, causal):
    block_rows = query_block.shape[0]
    groups_here = query_block.shape[1]
    per_group = query_block.shape[2]
    key_len = key_block.shape[0]
    scores = jnp.einsum(
        "qgrd,kgd->grqk", query_block, key_block, preferred_element_type=jnp.float32
    )
    scores = scores + bias_block.reshape(groups_here, per_group, block_rows, key_len)
    if causal:
        query_pos = start_row + jnp.arange(block_rows, dtype=jnp.int32)
        keep_mask = jnp.arange(key_len, dtype=jnp.int32)[None, :] <= query_pos[:, None]
        scores = jnp.where(keep_mask, scores, masked_value)
    return scores


def attend_forward(queries, key_rows, value_rows, bias_table, seq_len, two_sided, causal):
    rows_all, head_cols = queries.shape
    key_len = key_rows.shape[0] // (rows_all // seq_len)
    groups_here = key_rows.shape[1] // DH
    per_group = head_cols // (groups_here * DH)
    block_rows = min(512, seq_len)
    blocks = rows_all // block_rows

    def one_block(block_index):
        row_start = block_index * block_rows
        start_row = row_start % seq_len
        query_block = lax.dynamic_slice_in_dim(queries, row_start, block_rows, 0).reshape(
            block_rows, groups_here, per_group, DH
        )
        key_block = key_rows.reshape(key_len, groups_here, DH)
        value_block = value_rows.reshape(key_len, groups_here, DH)
        onehot = block_buckets(
            start_row, block_rows, seq_len, key_len, two_sided, bias_table.shape[0]
        )
        bias_block = jnp.einsum(
            "qkb,bh->hqk", onehot, bias_table, preferred_element_type=jnp.float32
        )
        scores = block_scores(query_block, key_block, bias_block, start_row, causal)
        row_max = jnp.max(scores, axis=-1, keepdims=True)
        weights = jnp.exp(scores - row_max)
        row_total = jnp.sum(weights, axis=-1, keepdims=True)
        prob_low = (weights / row_total).astype(jnp.bfloat16)
        mixed_heads = jnp.einsum(
            "grqk,kgd->qgrd", prob_low, value_block, preferred_element_type=jnp.float32
        )
        log_total = (row_max + jnp.log(row_total))[..., 0]
        return (mixed_heads.reshape(block_rows, head_cols).astype(jnp.bfloat16), log_total)

    mixed_heads, log_total = lax.map(one_block, jnp.arange(blocks, dtype=jnp.int32))
    return (mixed_heads.reshape(rows_all, head_cols), log_total)


def attend_backward(
    queries, key_rows, value_rows, mixed_grad, log_total, bias_table, seq_len, two_sided, causal
):
    rows_all, head_cols = queries.shape
    key_len = key_rows.shape[0] // (rows_all // seq_len)
    groups_here = key_rows.shape[1] // DH
    per_group = head_cols // (groups_here * DH)
    heads_here = groups_here * per_group
    block_rows = min(512, seq_len)
    blocks = rows_all // block_rows

    def one_block(sums, block_index):
        key_grad, value_grad, table_grad = sums
        row_start = block_index * block_rows
        start_row = row_start % seq_len
        query_block = lax.dynamic_slice_in_dim(queries, row_start, block_rows, 0).reshape(
            block_rows, groups_here, per_group, DH
        )
        grad_block = lax.dynamic_slice_in_dim(mixed_grad, row_start, block_rows, 0).reshape(
            block_rows, groups_here, per_group, DH
        )
        key_block = key_rows.reshape(key_len, groups_here, DH)
        value_block = value_rows.reshape(key_len, groups_here, DH)
        onehot = block_buckets(
            start_row, block_rows, seq_len, key_len, two_sided, bias_table.shape[0]
        )
        bias_block = jnp.einsum(
            "qkb,bh->hqk", onehot, bias_table, preferred_element_type=jnp.float32
        )
        scores = block_scores(query_block, key_block, bias_block, start_row, causal)
        block_total = lax.dynamic_index_in_dim(log_total, block_index, 0, keepdims=False)
        prob_high = jnp.exp(scores - block_total[..., None])
        prob_low = prob_high.astype(jnp.bfloat16)
        prob_grad = jnp.einsum(
            "qgrd,kgd->grqk", grad_block, value_block, preferred_element_type=jnp.float32
        )
        row_dot = jnp.sum(prob_high * prob_grad, axis=-1, keepdims=True)
        score_grad = (prob_high * (prob_grad - row_dot)).astype(jnp.bfloat16)
        query_grad = jnp.einsum(
            "grqk,kgd->qgrd", score_grad, key_block, preferred_element_type=jnp.float32
        )
        key_part = jnp.einsum(
            "grqk,qgrd->kgd", score_grad, query_block, preferred_element_type=jnp.float32
        ).reshape(key_len, groups_here * DH)
        value_part = jnp.einsum(
            "grqk,qgrd->kgd", prob_low, grad_block, preferred_element_type=jnp.float32
        ).reshape(key_len, groups_here * DH)
        key_grad = key_grad + key_part
        value_grad = value_grad + value_part
        head_grad = score_grad.reshape(heads_here, block_rows, key_len)
        table_grad = table_grad + jnp.einsum(
            "hqk,qkb->bh", head_grad, onehot, preferred_element_type=jnp.float32
        )
        return (
            (key_grad, value_grad, table_grad),
            query_grad.reshape(block_rows, head_cols).astype(jnp.bfloat16),
        )

    start_sums = (
        jnp.zeros(key_rows.shape, jnp.float32),
        jnp.zeros(value_rows.shape, jnp.float32),
        jnp.zeros(bias_table.shape, jnp.float32),
    )
    sums, query_grads = lax.scan(one_block, start_sums, jnp.arange(blocks, dtype=jnp.int32))
    return (
        query_grads.reshape(rows_all, head_cols),
        sums[0].astype(jnp.bfloat16),
        sums[1].astype(jnp.bfloat16),
        sums[2],
    )


def gate_times_up(gate_value, up_value):
    return jax.nn.gelu(gate_value, approximate=True) * up_value


def on_device(
    inputs,
    memory,
    out_grad,
    gain_self,
    self_query,
    self_key,
    self_value,
    self_output,
    self_table,
    gain_cross,
    cross_query,
    cross_key,
    cross_value,
    cross_output,
    cross_table,
    gain_ffn,
    ffn_gate,
    ffn_up,
    ffn_down,
):
    seq_len = inputs.shape[1]
    model_width = inputs.shape[2]
    rows_here = inputs.shape[0] * seq_len
    flat_in = inputs.reshape(rows_here, model_width).astype(jnp.float32)
    flat_mem = memory.reshape(memory.shape[0] * memory.shape[1], model_width)
    gain_one = gain_self.astype(jnp.float32)
    gain_two = gain_cross.astype(jnp.float32)
    gain_three = gain_ffn.astype(jnp.float32)
    attn_in = norm_rows(flat_in, gain_one).astype(jnp.bfloat16)
    queries = jnp.dot(attn_in, self_query, preferred_element_type=jnp.float32).astype(jnp.bfloat16)
    self_keys = jnp.dot(attn_in, self_key, preferred_element_type=jnp.float32).astype(jnp.bfloat16)
    self_values = jnp.dot(attn_in, self_value, preferred_element_type=jnp.float32).astype(
        jnp.bfloat16
    )
    mixed_self, total_self = attend_forward(
        queries, self_keys, self_values, self_table, seq_len, False, True
    )
    after_self = flat_in + lax.psum(
        jnp.dot(mixed_self, self_output, preferred_element_type=jnp.float32), "kv"
    )
    cross_in = norm_rows(after_self, gain_two).astype(jnp.bfloat16)
    cross_q = jnp.dot(cross_in, cross_query, preferred_element_type=jnp.float32).astype(
        jnp.bfloat16
    )
    cross_k = jnp.dot(flat_mem, cross_key, preferred_element_type=jnp.float32).astype(jnp.bfloat16)
    cross_v = jnp.dot(flat_mem, cross_value, preferred_element_type=jnp.float32).astype(
        jnp.bfloat16
    )
    mixed_cross, total_cross = attend_forward(
        cross_q, cross_k, cross_v, cross_table, seq_len, True, False
    )
    after_cross = after_self + lax.psum(
        jnp.dot(mixed_cross, cross_output, preferred_element_type=jnp.float32), "kv"
    )
    ffn_in = norm_rows(after_cross, gain_three).astype(jnp.bfloat16)
    gate_pre = jnp.dot(ffn_in, ffn_gate, preferred_element_type=jnp.float32)
    up_pre = jnp.dot(ffn_in, ffn_up, preferred_element_type=jnp.float32)
    hidden = gate_times_up(gate_pre, up_pre).astype(jnp.bfloat16)
    result = after_cross + lax.psum(
        jnp.dot(hidden, ffn_down, preferred_element_type=jnp.float32), "kv"
    )
    layer_out = result.astype(jnp.bfloat16).reshape(inputs.shape)
    grad_out = out_grad.reshape(rows_here, model_width).astype(jnp.float32)
    branch_grad = grad_out.astype(jnp.bfloat16)
    grad_down = inner_rows(hidden, branch_grad)
    hidden_grad = outer_cols(branch_grad, ffn_down)
    gate_grad, up_grad = jax.vjp(gate_times_up, gate_pre, up_pre)[1](hidden_grad)
    gate_low = gate_grad.astype(jnp.bfloat16)
    up_low = up_grad.astype(jnp.bfloat16)
    grad_gate = inner_rows(ffn_in, gate_low)
    grad_up = inner_rows(ffn_in, up_low)
    ffn_in_grad = lax.psum(outer_cols(gate_low, ffn_gate) + outer_cols(up_low, ffn_up), "kv")
    norm_grad, grad_gain_ffn = jax.vjp(norm_rows, after_cross, gain_three)[1](ffn_in_grad)
    cross_out_grad = grad_out + norm_grad
    ffn_parts = (grad_gain_ffn, grad_gate, grad_up, grad_down)
    ffn_parts = lax.psum((grad_gain_ffn, grad_gate, grad_up, grad_down), "batch")
    branch_grad = cross_out_grad.astype(jnp.bfloat16)
    grad_cross_out = inner_rows(mixed_cross, branch_grad)
    mixed_grad = outer_cols(branch_grad, cross_output).astype(jnp.bfloat16)
    cq_grad, ck_grad, cv_grad, grad_cross_tab = attend_backward(
        cross_q, cross_k, cross_v, mixed_grad, total_cross, cross_table, seq_len, True, False
    )
    grad_cq = inner_rows(cross_in, cq_grad)
    grad_ck = inner_rows(flat_mem, ck_grad)
    grad_cv = inner_rows(flat_mem, cv_grad)
    cross_in_grad = lax.psum(outer_cols(cq_grad, cross_query), "kv")
    memory_term = outer_cols(ck_grad, cross_key) + outer_cols(cv_grad, cross_value)
    memory_grad = lax.psum_scatter(
        memory_term.reshape(memory.shape), "kv", scatter_dimension=2, tiled=True
    )
    norm_grad, grad_gain_cross = jax.vjp(norm_rows, after_self, gain_two)[1](cross_in_grad)
    self_out_grad = cross_out_grad + norm_grad
    cross_parts = (grad_gain_cross, grad_cq, grad_ck, grad_cv, grad_cross_out, grad_cross_tab)
    cross_parts = lax.psum(
        (grad_gain_cross, grad_cq, grad_ck, grad_cv, grad_cross_out, grad_cross_tab), "batch"
    )
    branch_grad = self_out_grad.astype(jnp.bfloat16)
    grad_self_out = inner_rows(mixed_self, branch_grad)
    mixed_grad = outer_cols(branch_grad, self_output).astype(jnp.bfloat16)
    sq_grad, sk_grad, sv_grad, grad_self_tab = attend_backward(
        queries, self_keys, self_values, mixed_grad, total_self, self_table, seq_len, False, True
    )
    grad_sq = inner_rows(attn_in, sq_grad)
    grad_sk = inner_rows(attn_in, sk_grad)
    grad_sv = inner_rows(attn_in, sv_grad)
    attn_term = (
        outer_cols(sq_grad, self_query)
        + outer_cols(sk_grad, self_key)
        + outer_cols(sv_grad, self_value)
    )
    attn_in_grad = lax.psum(attn_term, "kv")
    norm_grad, grad_gain_self = jax.vjp(norm_rows, flat_in, gain_one)[1](attn_in_grad)
    input_grad = (self_out_grad + norm_grad).reshape(inputs.shape)
    self_parts = (grad_gain_self, grad_sq, grad_sk, grad_sv, grad_self_out, grad_self_tab)
    self_parts = lax.psum(
        (grad_gain_self, grad_sq, grad_sk, grad_sv, grad_self_out, grad_self_tab), "batch"
    )
    summed = tuple(self_parts) + tuple(cross_parts) + tuple(ffn_parts)
    return (
        layer_out,
        input_grad,
        memory_grad,
        summed[0],
        summed[1],
        summed[2],
        summed[3],
        summed[4],
        summed[5],
        summed[6],
        summed[7],
        summed[8],
        summed[9],
        summed[10],
        summed[11],
        summed[12],
        summed[13],
        summed[14],
        summed[15],
    )


def solution(mesh):
    return jax.shard_map(
        on_device,
        mesh=mesh,
        in_specs=(
            P("batch", None, None),
            P("batch", None, None),
            P("batch", None, None),
            P(),
            P(None, "kv"),
            P(None, "kv"),
            P(None, "kv"),
            P("kv", None),
            P(None, "kv"),
            P(),
            P(None, "kv"),
            P(None, "kv"),
            P(None, "kv"),
            P("kv", None),
            P(None, "kv"),
            P(),
            P(None, "kv"),
            P(None, "kv"),
            P("kv", None),
        ),
        out_specs=(
            P("batch", None, None),
            P("batch", None, None),
            P("batch", None, "kv"),
            P(),
            P(None, "kv"),
            P(None, "kv"),
            P(None, "kv"),
            P("kv", None),
            P(None, "kv"),
            P(),
            P(None, "kv"),
            P(None, "kv"),
            P(None, "kv"),
            P("kv", None),
            P(None, "kv"),
            P(),
            P(None, "kv"),
            P(None, "kv"),
            P("kv", None),
        ),
        check_vma=False,
    )
```

profile of v0, /device:TPU:0, one launch (start us, length us, event | category | flops | bytes accessed | tf_op | source)
XLA Modules:
  0.0 2202.8 jit_solution(5435869802848718309)
XLA Ops:
  23.0 77.3 %while.66 = (s32[]{:T(128)}, bf16[2,512,256]{2,1,0:T(8,128)(2,1)}, f32[2,2,2,512]{3,2,1,0:T(2,128)S(1)}, s32[2]{0:T(128)S(1)}, bf16[1024,256]{0,1:T(8,128)(2,1)S...) while((s32[]{:T(128)}, bf16[2,512,256]{2,1,0:T(8,128)(2,1)}, ...), condition=%wide.region_4.5_spmd, body=%wide.region_1.4_spmd.sunk | while | flops 755104256 | bytes 67705920 | solution.py:125
  108.0 154.5 %all-reduce.10.cloned.1.call-done = f32[1024,1024]{1,0:T(8,128)} async-done(((f32[1024,1024]{1,0:T(8,128)}), f32[1024,1024]{1,0:T(8,128)}) %all-reduce.10.cloned.1.call-update) | async-done | bytes 4194320 | tf_op jit(solution)/shard_map/psum | solution.py:243
  271.6 68.5 %while.67 = (s32[]{:T(128)}, bf16[2,512,256]{2,1,0:T(8,128)(2,1)}, f32[2,2,2,512]{3,2,1,0:T(2,128)S(1)}, s32[2]{0:T(128)S(1)}, bf16[1024,256]{0,1:T(8,128)(2,1)S...) while((s32[]{:T(128)}, bf16[2,512,256]{2,1,0:T(8,128)(2,1)}, ...), condition=%wide.region_10.11_spmd, body=%wide.region_7.10_spmd.sunk | while | flops 728365568 | bytes 65606692 | solution.py:125
  344.9 153.5 %all-reduce.12.cloned.1.call-done = f32[1024,1024]{1,0:T(8,128)} async-done(((f32[1024,1024]{1,0:T(8,128)}), f32[1024,1024]{1,0:T(8,128)}) %all-reduce.12.cloned.1.call-update) | async-done | bytes 4194320 | tf_op jit(solution)/shard_map/psum | solution.py:257
  519.7 154.1 %all-reduce.14.cloned.1.call-done = f32[1024,1024]{1,0:T(8,128)} async-done(((f32[1024,1024]{1,0:T(8,128)}), f32[1024,1024]{1,0:T(8,128)}) %all-reduce.14.cloned.1.call-update) | async-done | bytes 4194320 | tf_op jit(solution)/shard_map/psum | solution.py:277
  685.3 367.2 %while.68 = (s32[]{:T(128)}, f32[1024,128]{0,1:T(8,128)S(1)}, f32[1024,128]{0,1:T(8,128)}, f32[32,4]{0,1:T(4,128)S(1)}, bf16[2,512,256]{2,1,0:T(8,128)(2,1)}, /*...) while((s32[]{:T(128)}, f32[1024,128]{0,1:T(8,128)S(1)}, ...), condition=%wide.region_18.19_spmd.clone, body=%wide.region_16.18_spmd.clone.sunk | while | flops 1670511360 | bytes 323533248 | solution.py:192
  707.1 12.3 iota_compare_fusion.21
  719.5 90.0 %copy.134 = pred[512,1024,32]{1,2,0:T(32,128)(4,1)} copy(pred[512,1024,32]{0,2,1:T(32,128)(4,1)} %iota_compare_fusion.21) | data formatting | bytes 33554432 | tf_op jit(solution)/shard_map/while/body/eval_jaxpr/eq | solution.py:54
  856.6 12.5 fusion.389
  882.0 12.3 iota_compare_fusion.21
  894.4 90.0 %copy.134 = pred[512,1024,32]{1,2,0:T(32,128)(4,1)} copy(pred[512,1024,32]{0,2,1:T(32,128)(4,1)} %iota_compare_fusion.21) | data formatting | bytes 33554432 | tf_op jit(solution)/shard_map/while/body/eval_jaxpr/eq | solution.py:54
  1031.5 12.5 fusion.389
  1076.4 134.5 %all-reduce.16.cloned.1.call-done = f32[1024,1024]{1,0:T(8,128)} async-done(((f32[1024,1024]{1,0:T(8,128)}), f32[1024,1024]{1,0:T(8,128)}) %all-reduce.16.cloned.1.call-update) | async-done | bytes 4194320 | tf_op jit(solution)/shard_map/psum | solution.py:291
  1224.4 375.4 %while.69 = (s32[]{:T(128)}, f32[1024,128]{0,1:T(8,128)}, f32[1024,128]{0,1:T(8,128)}, f32[32,4]{0,1:T(4,128)S(1)}, bf16[2,512,256]{2,1,0:T(8,128)(2,1)}, /*inde...) while((s32[]{:T(128)}, f32[1024,128]{0,1:T(8,128)}, ...), condition=%wide.region_23.24_spmd.clone, body=%wide.region_21.23_spmd.clone.sunk | while | flops 1697250048 | bytes 330875328 | solution.py:192
  1236.4 13.4 iota_compare_fusion.22
  1249.8 90.0 %copy.140 = pred[512,1024,32]{1,2,0:T(32,128)(4,1)} copy(pred[512,1024,32]{0,2,1:T(32,128)(4,1)} %iota_compare_fusion.22) | data formatting | bytes 33554432 | tf_op jit(solution)/shard_map/while/body/eval_jaxpr/eq | solution.py:54
  1387.7 12.5 fusion.409
  1420.0 13.4 iota_compare_fusion.22
  1433.4 90.0 %copy.140 = pred[512,1024,32]{1,2,0:T(32,128)(4,1)} copy(pred[512,1024,32]{0,2,1:T(32,128)(4,1)} %iota_compare_fusion.22) | data formatting | bytes 33554432 | tf_op jit(solution)/shard_map/while/body/eval_jaxpr/eq | solution.py:54
  1571.4 12.5 fusion.409
  1623.3 184.9 %all-reduce.18.cloned.1.call-done = (f32[1024,256]{1,0:T(8,128)}, f32[1024,128]{1,0:T(8,128)}, f32[1024,128]{1,0:T(8,128)}, f32[256,1024]{1,0:T(8,128)}, f32[102...) async-done(((f32[1024,256]{1,0:T(8,128)}, ...) | async-done | bytes 14942224 | tf_op jit(solution)/shard_map/psum | solution.py:320
  1812.2 290.9 %all-reduce.20.cloned.1.call-done = (f32[1024,1024]{1,0:T(8,128)}, f32[1024,1024]{1,0:T(8,128)}) async-done(((f32[1024,1024]{1,0:T(8,128)}, f32[1024,1024]{1,0:T(8,128)}), (f32[1024,1024]{1,0:T(8,128)}, f32[1024,1024]{1,0:T(8,128)})) %all-reduce.20.cloned.1.call-update) | async-done | bytes 8388624 | tf_op jit(solution)/shard_map/psum | solution.py:264
  2107.5 25.8 %all-reduce = (f32[1024]{0:T(1024)}, f32[32,4]{0,1:T(4,128)}, f32[1024]{0:T(1024)}, f32[32,4]{0,1:T(4,128)}, f32[1024]{0:T(1024)}) all-reduce(f32[1024]{0:T(1024)S(1)} %get-tuple-element.743, f32[32,4]{0,1:T(4,128)S(1)} %get-tuple-element.541, f32[1024]{0:T(1024)S(1)} %copy-done.93, ...), channel_id=1, replica_groups=mesh['batch'=8,'kv'=4] {'batch'}, use_global_device_ids=true, to_apply=%region_28.29 | all-reduce | flops 3328 | bytes 26624 | tf_op jit(solution)/shard_map/psum | solution.py:320
  2143.2 38.7 %reduce-scatter.2.cloned.1.call-done = f32[1,1024,256]{2,1,0:T(8,128)} async-done(((f32[1,1024,1024]{2,1,0:T(8,128)}), f32[1,1024,256]{2,1,0:T(8,128)}) %reduce-scatter.2.cloned.1.call-update) | async-done | bytes 1048592 | tf_op jit(solution)/shard_map/reduce_scatter | solution.py:293
  (497 shorter events, 548.6 us)
Async XLA Ops:
  7.2 98.0 %copy-start = (bf16[1,1024,1024]{2,1,0:T(8,128)(2,1)S(1)}, bf16[1,1024,1024]{2,1,0:T(8,128)(2,1)}, u32[]{:S(2)}) copy-start(bf16[1,1024,1024]{2,1,0:T(8,128)(2,1)} %param.28) | copy-start | bytes 6291460
  7.2 255.2 %all-reduce.10.cloned.1.call-start = ((), (), s32[]{:S(2)}) async-start(), calls=%async_computation.1 | async-start | bytes 8388608 | tf_op jit(solution)/shard_map/psum | solution.py:243
  104.6 393.8 %all-reduce.12.cloned.1.call-start = ((), (), s32[]{:S(2)}) async-start(), calls=%async_computation.2 | async-start | bytes 8388608 | tf_op jit(solution)/shard_map/psum | solution.py:257
  105.5 160.4 %copy-start.77 = (f32[1024]{0:T(1024)}, f32[1024]{0:T(1024)S(1)}, u32[]{:S(2)}) copy-start(f32[1024]{0:T(1024)S(1)} %convert_element_type.1133) | copy-start | bytes 12292
  108.0 160.0 %copy-start.52 = (bf16[1024,256]{1,0:T(8,128)(2,1)S(1)}, bf16[1024,256]{1,0:T(8,128)(2,1)}, u32[]{:S(2)}) copy-start(bf16[1024,256]{1,0:T(8,128)(2,1)} %param.37) | copy-start | bytes 1572868
  344.3 329.6 %all-reduce.14.cloned.1.call-start = ((), (), s32[]{:S(2)}) async-start(), calls=%async_computation.3 | async-start | bytes 8388608 | tf_op jit(solution)/shard_map/psum | solution.py:277
  519.7 691.2 %all-reduce.16.cloned.1.call-start = ((), (), s32[]{:S(2)}) async-start(), calls=%async_computation.4 | async-start | bytes 8388608 | tf_op jit(solution)/shard_map/psum | solution.py:291
  702.3 17.1 copy-start.16
  836.9 8.4 slice-start.3
  856.6 15.6 copy-start.4
  877.2 17.1 copy-start.16
  1011.8 8.4 slice-start.3
  1031.5 15.6 copy-start.4
  1052.5 16.2 copy-start.32
  1056.7 751.5 %all-reduce.18.cloned.1.call-start = ((), (), s32[]{:S(2)}) async-start(), calls=%async_computation.6 | async-start | bytes 29884416 | tf_op jit(solution)/shard_map/psum | solution.py:320
  1076.4 139.7 %copy-start.88 = (f32[1024]{0:T(1024)S(1)}, f32[1024]{0:T(1024)}, u32[]{:S(2)}) copy-start(f32[1024]{0:T(1024)} %copy-done.87) | copy-start | bytes 12292
  1367.5 8.3 slice-start.1
  1387.7 15.6 copy-start.2
  1551.2 8.3 slice-start.1
  1571.4 15.6 copy-start.2
  1606.9 496.2 %all-reduce.20.cloned.1.call-start = ((), (), s32[]{:S(2)}) async-start(), calls=%async_computation.7 | async-start | bytes 16777216 | tf_op jit(solution)/shard_map/psum | solution.py:264
  1618.3 563.6 %reduce-scatter.2.cloned.1.call-start = ((), (), s32[]{:S(2)}) async-start(), calls=%async_computation.5 | async-start | bytes 5242880 | tf_op jit(solution)/shard_map/reduce_scatter | solution.py:293
  2103.2 30.1 %copy-start.86 = (f32[1024]{0:T(1024)S(1)}, f32[1024]{0:T(1024)}, u32[]{:S(2)}) copy-start(f32[1024]{0:T(1024)} %copy-done.85) | copy-start | bytes 12292
  2140.6 41.3 %copy-start.70 = (f32[1024,256]{1,0:T(8,128)S(1)}, f32[1024,256]{1,0:T(8,128)}, u32[]{:S(2)}) copy-start(f32[1024,256]{1,0:T(8,128)} %get-tuple-element.1320) | copy-start | bytes 3145732
  (114 other events, 340.1 us)
Sparse Core Ops, SparseCore 0:
  104.7 157.6 all-reduce.9
  344.4 153.9 all-reduce.11
  519.8 153.9 all-reduce.13
  1056.8 153.9 all-reduce.15
  1607.1 201.0 all-reduce.17
  1811.4 291.7 all-reduce.19
  2106.1 75.7 reduce-scatter.1
where the time goes:
time: 2210 us; the launch traced here: 2200 us
  waiting for transfers between devices  1110 us (50%)
  local copies, waits for them, and re-layouts  535 us (24%)
  matrix products  319 us (14%)
  other arithmetic  155 us (7%)
  loops' own time  40.9 us (2%)
  blocking collectives  25.8 us (1%)
    eq x4, local copies, waits for them, and re-layouts, block_buckets(): level_ids[:, :, None] == jnp.arange(buckets, dtype=jnp.int32)[None, None, :]  360 us
    psum x1, waiting for transfers between devices, on_device(): lax.psum(jnp.dot(hidden, ffn_down, preferred_element_type=jnp.float32), '...  291 us
    psum x1, waiting for transfers between devices, on_device(): lax.psum((grad_gain_self, grad_sq, grad_sk, grad_sv, grad_self_out, grad_...  185 us
    psum x1, waiting for transfers between devices, on_device(): lax.psum(jnp.dot(mixed_self, self_output, preferred_element_type=jnp.floa...  154 us
    psum x1, waiting for transfers between devices, on_device(): lax.psum(outer_cols(gate_low, ffn_gate) + outer_cols(up_low, ffn_up), 'kv')  154 us
    psum x1, waiting for transfers between devices, on_device(): lax.psum(jnp.dot(mixed_cross, cross_output, preferred_element_type=jnp.fl...  153 us
    psum x1, waiting for transfers between devices, on_device(): cross_in_grad = lax.psum(outer_cols(cq_grad, cross_query), 'kv')  134 us
    dot_general x8, matrix products, one_block(): jnp.einsum('qkb,bh->hqk', onehot, bias_table, preferred_element_type=jnp....  82.8 us
  transfers between devices with their start and end apart: 7, of which 7 were waited for; matrix products, arithmetic and copies ran while one was open for 2% of the time, Pallas kernels for 0%

commit v1 on v0

v1 whole, which is shorter than its diff:
```python
import functools
import jax, jax.numpy as jnp
import numpy as np
from jax import lax
from jax.experimental import pallas as pl
from jax.experimental.pallas import tpu as pltpu
from jax.sharding import PartitionSpec as P

DH = 64
eps = 1e-06
QB = 256
NEG = -1e30


def mm(a, b, dims):
    return lax.dot_general(a, b, (dims, ((), ())), preferred_element_type=jnp.float32)


NN = ((1,), (0,))
NT = ((1,), (1,))
TN = ((0,), (0,))


def make_band(x_ref, far_ref, group, head, band_ref):
    tiles = []
    for d in range(3):
        row = jnp.broadcast_to(x_ref[0, 3 * head + d, :].reshape(1, 256), (128, 256))
        tiles.append(pltpu.roll(row, 0, axis=1, stride=1, stride_axis=0)[:, :128])
    left = jnp.full((128, 128), far_ref[group, 2 * head], jnp.float32)
    right = jnp.full((128, 128), far_ref[group, 2 * head + 1], jnp.float32)
    rows = [
        (left, left), (left, left), (left, left),
        (tiles[0], left), (tiles[1], tiles[0]), (tiles[2], tiles[1]), (right, tiles[2]),
        (right, right), (right, right), (right, right),
    ]
    for n, (a, b) in enumerate(rows):
        band_ref[head, n * 128:(n + 1) * 128, 0:128] = a
        band_ref[head, n * 128:(n + 1) * 128, 128:256] = b


def band_at(chunk, block):
    return pl.multiple_of((jnp.clip(chunk - block, -2, 2) + 2) * QB, QB)


def over_chunks(count, body, init):
    if isinstance(count, int):
        for c in range(count):
            init = body(c, init)
        return init
    return lax.fori_loop(0, count, body, init)


def ds(c):
    return pl.ds(pl.multiple_of(c * QB, QB), QB)


def part_sum(tile, op):
    return op(tile.reshape(QB // 8, 8, QB), axis=0)


def fwd_kernel(causal, row_ref, far_ref, x_ref, q_ref, k_ref, v_ref, o_ref, l_ref, band, keys, s_ref):
    g, r = pl.program_id(0), pl.program_id(1)
    block = r + row_ref[0]
    total_chunks = k_ref.shape[1] // QB

    @pl.when(r == 0)
    def _():
        for h in range(2):
            make_band(x_ref, far_ref, g, h, band)
        keys[...] = k_ref[...].T

    count = block + 1 if causal else total_chunks
    for h in range(2):
        q = q_ref[h * DH:(h + 1) * DH, :]

        def scores(c, top):
            s = mm(keys[ds(c), :], q, NN) + band[h, pl.ds(band_at(c, block), QB), :]
            s_ref[ds(c), :] = s
            return jnp.maximum(top, part_sum(s, jnp.max))

        top = over_chunks(count, scores, jnp.full((8, QB), NEG, jnp.float32))
        top = jnp.max(top, axis=0, keepdims=True)

        def weigh(c, tot):
            e = jnp.exp(s_ref[ds(c), :] - top)
            s_ref[ds(c), :] = e
            return tot + part_sum(e, jnp.sum)

        tot = over_chunks(count, weigh, jnp.zeros((8, QB), jnp.float32))
        tot = jnp.sum(tot, axis=0, keepdims=True)
        inv = 1.0 / tot

        def mix(c, acc):
            p = (s_ref[ds(c), :] * inv).astype(jnp.bfloat16)
            return acc + mm(v_ref[:, ds(c)], p, NN)

        acc = over_chunks(count, mix, jnp.zeros((DH, QB), jnp.float32))
        o_ref[h * DH:(h + 1) * DH, :] = acc.astype(jnp.bfloat16)
        l_ref[0, h:h + 1, :] = top + jnp.log(tot)


def bwd_kernel(causal, row_ref, far_ref, x_ref, q_ref, k_ref, v_ref, d_ref, l_ref,
               dq_ref, dk_ref, dv_ref, t_ref, band, keys, values, p_ref, g_ref, near):
    g, r = pl.program_id(0), pl.program_id(1)
    block = r + row_ref[0]
    total_chunks = k_ref.shape[1] // QB

    @pl.when(r == 0)
    def _():
        for h in range(2):
            make_band(x_ref, far_ref, g, h, band)
        keys[...] = k_ref[...].T
        values[...] = v_ref[...].T
        dk_ref[...] = jnp.zeros_like(dk_ref)
        dv_ref[...] = jnp.zeros_like(dv_ref)
        near[...] = jnp.zeros_like(near)

    count = block + 1 if causal else total_chunks
    for h in range(2):
        q = q_ref[h * DH:(h + 1) * DH, :]
        d = d_ref[h * DH:(h + 1) * DH, :]
        log_total = l_ref[0, h:h + 1, :]

        def weigh(c, dot):
            s = mm(keys[ds(c), :], q, NN) + band[h, pl.ds(band_at(c, block), QB), :]
            p = jnp.exp(s - log_total)
            dp = mm(values[ds(c), :], d, NN)
            p_ref[ds(c), :] = p
            g_ref[ds(c), :] = dp
            return dot + part_sum(p * dp, jnp.sum)

        dot = over_chunks(count, weigh, jnp.zeros((8, QB), jnp.float32))
        dot = jnp.sum(dot, axis=0, keepdims=True)

        def back(c, acc):
            p = p_ref[ds(c), :]
            low = (p * (g_ref[ds(c), :] - dot)).astype(jnp.bfloat16)
            dk_ref[:, ds(c)] += mm(q, low, NT)
            dv_ref[:, ds(c)] += mm(d, p.astype(jnp.bfloat16), NT)
            at = pl.ds(band_at(c, block), QB)
            near[h, at, :] += low.astype(jnp.float32)
            return acc + mm(k_ref[:, ds(c)], low, NN)

        acc = over_chunks(count, back, jnp.zeros((DH, QB), jnp.float32))
        dq_ref[h * DH:(h + 1) * DH, :] = acc.astype(jnp.bfloat16)

    @pl.when(r == pl.num_programs(1) - 1)
    def _():
        for h in range(2):
            def piece(n, side):
                return near[h, n * 128:(n + 1) * 128, side * 128:(side + 1) * 128]

            left = piece(3, 1) + sum(piece(n, 0) + piece(n, 1) for n in range(3))
            right = piece(6, 0) + sum(piece(n, 0) + piece(n, 1) for n in range(7, 10))
            tiles = [piece(3, 0) + piece(4, 1), piece(4, 0) + piece(5, 1), piece(5, 0) + piece(6, 1)]
            for n, tile in enumerate(tiles):
                wide = jnp.concatenate([tile, jnp.zeros_like(tile)], axis=1)
                rows = wide[0:8]
                for a in range(8, 128, 8):
                    rows = rows + pltpu.roll(wide[a:a + 8], 256 - a, axis=1)
                line = rows[0:1]
                for b in range(1, 8):
                    line = line + pltpu.roll(rows[b:b + 1], 256 - b, axis=1)
                t_ref[0, 5 * h + n:5 * h + n + 1, :] = line
            for n, far in enumerate((left, right)):
                t_ref[0, 5 * h + 3 + n:5 * h + 4 + n, 0:128] = jnp.sum(far, axis=0, keepdims=True)
                t_ref[0, 5 * h + 3 + n:5 * h + 4 + n, 128:256] = jnp.zeros((1, 128), jnp.float32)


def specs(rows, keys):
    smem = pl.BlockSpec(memory_space=pltpu.SMEM)
    return dict(
        smem=smem,
        x=pl.BlockSpec((1, 6, 256), lambda g, r: (g, 0, 0)),
        q=pl.BlockSpec((2 * DH, QB), lambda g, r: (g, r)),
        k=pl.BlockSpec((DH, keys), lambda g, r: (g, 0)),
        l=pl.BlockSpec((1, 2, QB), lambda g, r: (g, 0, r)),
        t=pl.BlockSpec((1, 10, 256), lambda g, r: (g, 0, 0)),
    )


def attend(row, far, x, q, k, v, causal):
    groups, keys, rows = k.shape[0] // DH, k.shape[1], q.shape[1]
    s = specs(rows, keys)
    elements = 2 * groups * rows * keys
    return pl.pallas_call(
        functools.partial(fwd_kernel, causal),
        out_shape=(jax.ShapeDtypeStruct(q.shape, jnp.bfloat16),
                   jax.ShapeDtypeStruct((groups, 2, rows), jnp.float32)),
        grid=(groups, rows // QB),
        in_specs=[s["smem"], s["smem"], s["x"], s["q"], s["k"], s["k"]],
        out_specs=(s["q"], s["l"]),
        scratch_shapes=[pltpu.VMEM((2, 10 * 128, 256), jnp.float32), pltpu.VMEM((keys, DH), jnp.bfloat16),
                        pltpu.VMEM((keys, QB), jnp.float32)],
        compiler_params=pltpu.CompilerParams(dimension_semantics=("arbitrary", "arbitrary"), vmem_limit_bytes=24 << 20),
        cost_estimate=pl.CostEstimate(flops=4 * DH * elements, transcendentals=elements, bytes_accessed=4 * q.size + 4 * k.size),
        name="attend",
    )(row, far, x, q, k, v)


def attend_back(row, far, x, q, k, v, d, logs, causal):
    groups, keys, rows = k.shape[0] // DH, k.shape[1], q.shape[1]
    s = specs(rows, keys)
    elements = 2 * groups * rows * keys
    return pl.pallas_call(
        functools.partial(bwd_kernel, causal),
        out_shape=(jax.ShapeDtypeStruct(q.shape, jnp.bfloat16),
                   jax.ShapeDtypeStruct(k.shape, jnp.float32),
                   jax.ShapeDtypeStruct(k.shape, jnp.float32),
                   jax.ShapeDtypeStruct((groups, 10, 256), jnp.float32)),
        grid=(groups, rows // QB),
        in_specs=[s["smem"], s["smem"], s["x"], s["q"], s["k"], s["k"], s["q"], s["l"]],
        out_specs=(s["q"], s["k"], s["k"], s["t"]),
        scratch_shapes=[pltpu.VMEM((2, 10 * 128, 256), jnp.float32), pltpu.VMEM((keys, DH), jnp.bfloat16),
                        pltpu.VMEM((keys, DH), jnp.bfloat16),
                        pltpu.VMEM((keys, QB), jnp.float32), pltpu.VMEM((keys, QB), jnp.float32),
                        pltpu.VMEM((2, 10 * 128, 256), jnp.float32)],
        compiler_params=pltpu.CompilerParams(dimension_semantics=("arbitrary", "arbitrary"), vmem_limit_bytes=32 << 20),
        cost_estimate=pl.CostEstimate(flops=10 * DH * elements, transcendentals=elements, bytes_accessed=6 * q.size + 12 * k.size),
        name="attend_back",
    )(row, far, x, q, k, v, d, logs)


MAXDIST = 128


def side_buckets(n, buckets):
    exact = buckets // 2
    scaled = np.log(np.maximum(n, 1) / exact) / np.log(MAXDIST / exact)
    far = np.minimum(exact + np.floor(scaled * (buckets - exact)).astype(np.int64), buckets - 1)
    return np.where(n < exact, n, far)


def relative_buckets(r, two_sided, buckets):
    if two_sided:
        per = buckets // 2
        return side_buckets(np.abs(r), per) + np.where(r > 0, per, 0)
    return side_buckets(np.maximum(-r, 0), buckets)


def lane_offsets():
    m = np.arange(256)
    return np.stack([128 * d - np.where(m < 128, m, m - 256) for d in (-1, 0, 1)])


def bias_vectors(table, two_sided):
    buckets, heads = table.shape
    rel = lane_offsets()
    ids = relative_buckets(rel, two_sided, buckets)
    onehot = (ids.reshape(-1)[:, None] == np.arange(buckets)[None, :])
    x = jnp.dot(jnp.asarray(onehot, jnp.bfloat16), table, preferred_element_type=jnp.float32)
    x = x.reshape(3, 256, heads)
    last = table.shape[0] - 1
    if two_sided:
        left, right = table[last // 2].astype(jnp.float32), table[last].astype(jnp.float32)
    else:
        x = jnp.where(jnp.asarray(rel > 0)[:, :, None], NEG, x)
        left, right = table[last].astype(jnp.float32), jnp.full((heads,), NEG, jnp.float32)
    x = jnp.transpose(x, (2, 0, 1)).reshape(heads // 2, 6, 256)
    far = jnp.stack([left, right], axis=1).reshape(heads // 2, 4)
    return x, far


def table_gradient(t, two_sided, buckets):
    groups = t.shape[0]
    t = t.reshape(2 * groups, 5, 256)
    rel = lane_offsets()
    ids = relative_buckets(rel, two_sided, buckets)
    onehot = np.zeros((5, 256, buckets), np.float32)
    onehot[:3] = (ids[:, :, None] == np.arange(buckets)) & (np.arange(256) != 128)[None, :, None]
    last = buckets - 1
    if two_sided:
        onehot[3, :, last // 2] = 1
        onehot[4, :, last] = 1
    else:
        onehot[:3] *= (rel <= 0)[:, :, None]
        onehot[3, :, last] = 1
    return lax.dot_general(jnp.asarray(onehot.reshape(5 * 256, buckets), jnp.bfloat16).astype(jnp.float32), t.reshape(2 * groups, 5 * 256),
                           (((0,), (1,)), ((), ())), precision=lax.Precision.HIGHEST)


def norm_rows(hidden, gain_vec):
    inv_scale = lax.rsqrt(jnp.mean(hidden * hidden, axis=-1, keepdims=True) + eps)
    return hidden * inv_scale * gain_vec


def inner_rows(left_mat, right_mat):
    return lax.dot_general(
        left_mat, right_mat, (((0,), (0,)), ((), ())), preferred_element_type=jnp.float32
    )


def outer_cols(left_mat, right_mat):
    return lax.dot_general(
        left_mat, right_mat, (((1,), (1,)), ((), ())), preferred_element_type=jnp.float32
    )


def gate_times_up(gate_value, up_value):
    return jax.nn.gelu(gate_value, approximate=True) * up_value


def on_device(
    inputs,
    memory,
    out_grad,
    gain_self,
    self_query,
    self_key,
    self_value,
    self_output,
    self_table,
    gain_cross,
    cross_query,
    cross_key,
    cross_value,
    cross_output,
    cross_table,
    gain_ffn,
    ffn_gate,
    ffn_up,
    ffn_down,
):
    seq_len = inputs.shape[1]
    model_width = inputs.shape[2]
    rows_here = inputs.shape[0] * seq_len
    flat_in = inputs.reshape(rows_here, model_width).astype(jnp.float32)
    flat_mem = memory.reshape(memory.shape[0] * memory.shape[1], model_width)
    gain_one = gain_self.astype(jnp.float32)
    gain_two = gain_cross.astype(jnp.float32)
    gain_three = gain_ffn.astype(jnp.float32)
    attn_in = norm_rows(flat_in, gain_one).astype(jnp.bfloat16)
    row = jnp.zeros((1,), jnp.int32)
    self_x, self_far = bias_vectors(self_table, False)
    cross_x, cross_far = bias_vectors(cross_table, True)
    queries = mm(self_query, attn_in, ((0,), (1,))).astype(jnp.bfloat16)
    self_keys = mm(self_key, attn_in, ((0,), (1,))).astype(jnp.bfloat16)
    self_values = mm(self_value, attn_in, ((0,), (1,))).astype(jnp.bfloat16)
    mixed_self, total_self = attend(
        row, self_far, self_x, queries, self_keys, self_values, True
    )
    after_self = flat_in + lax.psum(
        mm(mixed_self, self_output, TN), "kv"
    )
    cross_in = norm_rows(after_self, gain_two).astype(jnp.bfloat16)
    cross_q = mm(cross_query, cross_in, ((0,), (1,))).astype(jnp.bfloat16)
    cross_k = mm(cross_key, flat_mem, ((0,), (1,))).astype(jnp.bfloat16)
    cross_v = mm(cross_value, flat_mem, ((0,), (1,))).astype(jnp.bfloat16)
    mixed_cross, total_cross = attend(
        row, cross_far, cross_x, cross_q, cross_k, cross_v, False
    )
    after_cross = after_self + lax.psum(
        mm(mixed_cross, cross_output, TN), "kv"
    )
    ffn_in = norm_rows(after_cross, gain_three).astype(jnp.bfloat16)
    gate_pre = jnp.dot(ffn_in, ffn_gate, preferred_element_type=jnp.float32)
    up_pre = jnp.dot(ffn_in, ffn_up, preferred_element_type=jnp.float32)
    hidden = gate_times_up(gate_pre, up_pre).astype(jnp.bfloat16)
    result = after_cross + lax.psum(
        jnp.dot(hidden, ffn_down, preferred_element_type=jnp.float32), "kv"
    )
    layer_out = result.astype(jnp.bfloat16).reshape(inputs.shape)
    grad_out = out_grad.reshape(rows_here, model_width).astype(jnp.float32)
    branch_grad = grad_out.astype(jnp.bfloat16)
    grad_down = inner_rows(hidden, branch_grad)
    hidden_grad = outer_cols(branch_grad, ffn_down)
    gate_grad, up_grad = jax.vjp(gate_times_up, gate_pre, up_pre)[1](hidden_grad)
    gate_low = gate_grad.astype(jnp.bfloat16)
    up_low = up_grad.astype(jnp.bfloat16)
    grad_gate = inner_rows(ffn_in, gate_low)
    grad_up = inner_rows(ffn_in, up_low)
    ffn_in_grad = lax.psum(outer_cols(gate_low, ffn_gate) + outer_cols(up_low, ffn_up), "kv")
    norm_grad, grad_gain_ffn = jax.vjp(norm_rows, after_cross, gain_three)[1](ffn_in_grad)
    cross_out_grad = grad_out + norm_grad
    ffn_parts = lax.psum((grad_gain_ffn, grad_gate, grad_up, grad_down), "batch")
    branch_grad = cross_out_grad.astype(jnp.bfloat16)
    grad_cross_out = mm(mixed_cross, branch_grad, NN)
    mixed_grad = mm(cross_output, branch_grad, NT).astype(jnp.bfloat16)
    cq_grad, ck_grad, cv_grad, cross_lines = attend_back(
        row, cross_far, cross_x, cross_q, cross_k, cross_v, mixed_grad, total_cross, False
    )
    ck_grad, cv_grad = ck_grad.astype(jnp.bfloat16), cv_grad.astype(jnp.bfloat16)
    grad_cross_tab = table_gradient(cross_lines, True, cross_table.shape[0])
    grad_cq = mm(cross_in, cq_grad, ((0,), (1,)))
    grad_ck = mm(flat_mem, ck_grad, ((0,), (1,)))
    grad_cv = mm(flat_mem, cv_grad, ((0,), (1,)))
    cross_in_grad = lax.psum(mm(cq_grad, cross_query, ((0,), (1,))), "kv")
    memory_term = mm(ck_grad, cross_key, ((0,), (1,))) + mm(cv_grad, cross_value, ((0,), (1,)))
    memory_grad = lax.psum_scatter(
        memory_term.reshape(memory.shape), "kv", scatter_dimension=2, tiled=True
    )
    norm_grad, grad_gain_cross = jax.vjp(norm_rows, after_self, gain_two)[1](cross_in_grad)
    self_out_grad = cross_out_grad + norm_grad
    cross_parts = lax.psum(
        (grad_gain_cross, grad_cq, grad_ck, grad_cv, grad_cross_out, grad_cross_tab), "batch"
    )
    branch_grad = self_out_grad.astype(jnp.bfloat16)
    grad_self_out = mm(mixed_self, branch_grad, NN)
    mixed_grad = mm(self_output, branch_grad, NT).astype(jnp.bfloat16)
    sq_grad, sk_grad, sv_grad, self_lines = attend_back(
        row, self_far, self_x, queries, self_keys, self_values, mixed_grad, total_self, True
    )
    sk_grad, sv_grad = sk_grad.astype(jnp.bfloat16), sv_grad.astype(jnp.bfloat16)
    grad_self_tab = table_gradient(self_lines, False, self_table.shape[0])
    grad_sq = mm(attn_in, sq_grad, ((0,), (1,)))
    grad_sk = mm(attn_in, sk_grad, ((0,), (1,)))
    grad_sv = mm(attn_in, sv_grad, ((0,), (1,)))
    attn_term = (
        mm(sq_grad, self_query, ((0,), (1,)))
        + mm(sk_grad, self_key, ((0,), (1,)))
        + mm(sv_grad, self_value, ((0,), (1,)))
    )
    attn_in_grad = lax.psum(attn_term, "kv")
    norm_grad, grad_gain_self = jax.vjp(norm_rows, flat_in, gain_one)[1](attn_in_grad)
    input_grad = (self_out_grad + norm_grad).reshape(inputs.shape)
    self_parts = lax.psum(
        (grad_gain_self, grad_sq, grad_sk, grad_sv, grad_self_out, grad_self_tab), "batch"
    )
    summed = tuple(self_parts) + tuple(cross_parts) + tuple(ffn_parts)
    return (
        layer_out,
        input_grad,
        memory_grad,
        summed[0],
        summed[1],
        summed[2],
        summed[3],
        summed[4],
        summed[5],
        summed[6],
        summed[7],
        summed[8],
        summed[9],
        summed[10],
        summed[11],
        summed[12],
        summed[13],
        summed[14],
        summed[15],
    )


def solution(mesh):
    return jax.shard_map(
        on_device,
        mesh=mesh,
        in_specs=(
            P("batch", None, None),
            P("batch", None, None),
            P("batch", None, None),
            P(),
            P(None, "kv"),
            P(None, "kv"),
            P(None, "kv"),
            P("kv", None),
            P(None, "kv"),
            P(),
            P(None, "kv"),
            P(None, "kv"),
            P(None, "kv"),
            P("kv", None),
            P(None, "kv"),
            P(),
            P(None, "kv"),
            P(None, "kv"),
            P("kv", None),
        ),
        out_specs=(
            P("batch", None, None),
            P("batch", None, None),
            P("batch", None, "kv"),
            P(),
            P(None, "kv"),
            P(None, "kv"),
            P(None, "kv"),
            P("kv", None),
            P(None, "kv"),
            P(),
            P(None, "kv"),
            P(None, "kv"),
            P(None, "kv"),
            P("kv", None),
            P(None, "kv"),
            P(),
            P(None, "kv"),
            P(None, "kv"),
            P("kv", None),
        ),
        check_vma=False,
    )
```

time: 2210 us -> 1380 us (0.62)
  local copies, waits for them, and re-layouts: 535 us -> 36.5 us
  matrix products: 319 us -> 71.6 us
  other arithmetic: 155 us -> 38.9 us
  Pallas kernels: 0 us -> 70.6 us
  loops' own time: 40.9 us -> 0 us
    eq x4 -> x0, local copies, waits for them, and re-layouts: 360 us -> none  [block_buckets(): level_ids[:, :, None] == jnp.arange(buckets, dtype=jnp.int32)[None, None, :]]
    dot_general x48 -> x28, matrix products: 256 us -> 39.2 us  [the longest x24 37.5 us: mm(): lax.dot_general(a, b, (dims, ((), ())), preferred_element_type=jnp.float32)]
    pallas_call x0 -> x4, Pallas kernels: none -> 70.6 us  [the longest x2 41.1 us: attend_back(): pl.pallas_call(functools.partial(bwd_kernel, causal), out_shape=(jax.Shap...]
    dot_general x8 -> x0, local copies, waits for them, and re-layouts: 65.7 us -> none  [one_block(): jnp.einsum('qkb,bh->hqk', onehot, bias_table, preferred_element_type=jnp....]
    eq x4 -> x0, other arithmetic: 51.5 us -> none  [block_buckets(): level_ids[:, :, None] == jnp.arange(buckets, dtype=jnp.int32)[None, None, :]]
    add x20 -> x0, other arithmetic: 43.8 us -> none  [the longest x8 42.6 us: block_buckets(): level_ids = level_ids + (distance >= first_distance).astype(jnp.int32)]
    another operation x4 -> x0, loops' own time: 40.9 us -> none  [the longest x2 36.7 us: attend_backward(): lax.scan(one_block, start_sums, jnp.arange(blocks, dtype=jnp.int32))]
    reshape x4 -> x5, local copies, waits for them, and re-layouts: 31.4 us -> 0.31 us  [the longest x3 0.26 us: bias_vectors(): far = jnp.stack([left, right], axis=1).reshape(heads // 2, 4)]
  transfers between devices with their start and end apart: 7 -> 7, of which waited for: 7 -> 7; matrix products, arithmetic and copies ran while one was open for 2% -> 4% of each run, Pallas kernels for 0% -> 0%
where the time goes in v1:
time: 1380 us; the launch traced here: 1370 us
  waiting for transfers between devices  1110 us (80%)
  matrix products  71.6 us (5%)
  Pallas kernels  70.6 us (5%)
  other arithmetic  38.9 us (3%)
  local copies, waits for them, and re-layouts  36.5 us (3%)
  blocking collectives  25.8 us (2%)
  between operations  15.1 us (1%)
    psum x1, waiting for transfers between devices, on_device(): lax.psum(jnp.dot(hidden, ffn_down, preferred_element_type=jnp.float32), '...  291 us
    psum x1, waiting for transfers between devices, on_device(): lax.psum((grad_gain_self, grad_sq, grad_sk, grad_sv, grad_self_out, grad_...  184 us
    psum x1, waiting for transfers between devices, on_device(): lax.psum(outer_cols(gate_low, ffn_gate) + outer_cols(up_low, ffn_up), 'kv')  154 us
    psum x1, waiting for transfers between devices, on_device(): after_cross = after_self + lax.psum(mm(mixed_cross, cross_output, TN), 'kv')  153 us
    psum x1, waiting for transfers between devices, on_device(): after_self = flat_in + lax.psum(mm(mixed_self, self_output, TN), 'kv')  153 us
    psum x1, waiting for transfers between devices, on_device(): cross_in_grad = lax.psum(mm(cq_grad, cross_query, ((0,), (1,))), 'kv')  134 us
    pallas_call x2, Pallas kernels, attend_back(): pl.pallas_call(functools.partial(bwd_kernel, causal), out_shape=(jax.Shap...  41.1 us
    reduce_scatter x1, waiting for transfers between devices, on_device(): lax.psum_scatter(memory_term.reshape(memory.shape), 'kv', scatter_dimensi...  38.8 us
  transfers between devices with their start and end apart: 7, of which 7 were waited for; matrix products, arithmetic and copies ran while one was open for 4% of the time, Pallas kernels for 0%

profile of v1, /device:TPU:0, one launch (start us, length us, event | category | flops | bytes accessed | tf_op | source)
XLA Modules:
  0.0 1367.8 jit_solution(5400470772884203348)
XLA Ops:
  15.7 17.2 %attend.2 = (bf16[256,1024]{1,0:T(8,128)(2,1)S(1)}, f32[2,2,1024]{2,1,0:T(2,128)S(1)}) custom-call(s32[1]{0:T(128)} %constant.12.clone.1.row_ref, f32[2,4]{1,0:T(2,128)S(1)} %reshape.173.far_ref, f32[2,6,256]{2,1,0:T(8,128)S(1)} %reshape.175.x_ref, bf16[256,1024]{1,0:T(8,128)(2,1)S(1)} %copy-done.18, bf16[128,1024]{1,0:T(8,128)(2,1)S(1)} %fusion.46.k_ref, ...), custom_call_target="tpu_custom_call" | custom-call | flops 1073741824 | bytes 1572864 | tf_op jit(solution)/shard_map/attend/pallas_call | solution.py:186
  41.1 152.5 %all-reduce.11.cloned.1.call-done = f32[1024,1024]{1,0:T(8,128)} async-done(((f32[1024,1024]{1,0:T(8,128)}), f32[1024,1024]{1,0:T(8,128)}) %all-reduce.11.cloned.1.call-update) | async-done | bytes 4194320 | tf_op jit(solution)/shard_map/psum | solution.py:342
  193.6 3.5 multiply_reduce_fusion.5
  198.5 12.3 attend.3
  214.3 153.5 %all-reduce.13.cloned.1.call-done = f32[1024,1024]{1,0:T(8,128)} async-done(((f32[1024,1024]{1,0:T(8,128)}), f32[1024,1024]{1,0:T(8,128)}) %all-reduce.13.cloned.1.call-update) | async-done | bytes 4194320 | tf_op jit(solution)/shard_map/psum | solution.py:352
  367.7 4.0 multiply_reduce_fusion.4
  378.3 4.8 multiply_convert_fusion.2
  385.1 4.0 convolution_add_fusion
  389.4 153.8 %all-reduce.15.cloned.1.call-done = f32[1024,1024]{1,0:T(8,128)} async-done(((f32[1024,1024]{1,0:T(8,128)}), f32[1024,1024]{1,0:T(8,128)}) %all-reduce.15.cloned.1.call-update) | async-done | bytes 4194320 | tf_op jit(solution)/shard_map/psum | solution.py:372
  543.2 4.6 multiply_reduce_fusion
  553.8 19.1 %attend_back.2 = (bf16[256,1024]{1,0:T(8,128)(2,1)S(1)}, f32[128,1024]{1,0:T(8,128)S(1)}, f32[128,1024]{1,0:T(8,128)S(1)}, f32[2,10,256]{2,1,0:T(8,128)S(1)}) custom-call(s32[1]{0:T(128)} %constant.12.clone.1.row_ref, f32[2,4]{1,0:T(2,128)S(1)} %reshape.188.far_ref, f32[2,6,256]{2,1,0:T(8,128)S(1)} %reshape.179.x_ref, bf16[256,1024]{1,0:T(8,128)(2,1)S(1)} %copy-done.11, ...), custom_call_target="tpu_custom_call" | custom-call | flops 2684354560 | bytes 3145728 | tf_op jit(solution)/shard_map/attend_back/pallas_call | solution.py:205
  578.5 5.4 fusion.83
  584.0 3.2 fusion.84
  587.2 3.2 fusion.18
  597.8 134.4 %all-reduce.17.cloned.1.call-done = f32[1024,1024]{1,0:T(8,128)} async-done(((f32[1024,1024]{1,0:T(8,128)}), f32[1024,1024]{1,0:T(8,128)}) %all-reduce.17.cloned.1.call-update) | async-done | bytes 4194320 | tf_op jit(solution)/shard_map/psum | solution.py:387
  732.2 4.6 multiply_reduce_fusion.1
  743.6 22.0 %attend_back.3 = (bf16[256,1024]{1,0:T(8,128)(2,1)S(1)}, f32[128,1024]{1,0:T(8,128)S(1)}, f32[128,1024]{1,0:T(8,128)S(1)}, f32[2,10,256]{2,1,0:T(8,128)S(1)}) custom-call(s32[1]{0:T(128)} %constant.12.clone.1.row_ref, f32[2,4]{1,0:T(2,128)S(1)} %reshape.173.far_ref, f32[2,6,256]{2,1,0:T(8,128)S(1)} %reshape.175.x_ref, bf16[256,1024]{1,0:T(8,128)(2,1)S(1)} %copy-done.19, ...), custom_call_target="tpu_custom_call" | custom-call | flops 2684354560 | bytes 3145728 | tf_op jit(solution)/shard_map/attend_back/pallas_call | solution.py:205
  770.6 6.4 fusion.76
  787.9 183.9 %all-reduce.19.cloned.1.call-done = (f32[1024,256]{1,0:T(8,128)}, f32[1024,128]{1,0:T(8,128)}, f32[1024,128]{1,0:T(8,128)}, f32[256,1024]{1,0:T(8,128)}, f32[102...) async-done(((f32[1024,256]{1,0:T(8,128)}, ...) | async-done | bytes 14942224 | tf_op jit(solution)/shard_map/psum | solution.py:416
  975.8 290.9 %all-reduce.21.cloned.1.call-done = (f32[1024,1024]{1,0:T(8,128)}, f32[1024,1024]{1,0:T(8,128)}) async-done(((f32[1024,1024]{1,0:T(8,128)}, f32[1024,1024]{1,0:T(8,128)}), (f32[1024,1024]{1,0:T(8,128)}, f32[1024,1024]{1,0:T(8,128)})) %all-reduce.21.cloned.1.call-update) | async-done | bytes 8388624 | tf_op jit(solution)/shard_map/psum | solution.py:359
  1266.7 4.3 fusion.3
  1271.0 25.8 %all-reduce.1 = (f32[1024]{0:T(1024)}, f32[32,4]{0,1:T(4,128)}, f32[1024]{0:T(1024)}, f32[32,4]{0,1:T(4,128)}, f32[1024]{0:T(1024)}) all-reduce(f32[1024]{0:T(1024)S(1)} %get-tuple-element.85, f32[32,4]{0,1:T(4,128)S(1)} %fusion.81, f32[1024]{0:T(1024)S(1)} %get-tuple-element.83, ...), channel_id=1, replica_groups=mesh['batch'=8,'kv'=4] {'batch'}, use_global_device_ids=true, to_apply=%region_14.15 | all-reduce | flops 3328 | bytes 26624 | tf_op jit(solution)/shard_map/psum | solution.py:416
  1296.8 5.7 fusion.17
  1306.7 38.8 %reduce-scatter.2.cloned.1.call-done = f32[1,1024,256]{2,1,0:T(8,128)} async-done(((f32[1,1024,1024]{2,1,0:T(8,128)}), f32[1,1024,256]{2,1,0:T(8,128)}) %reduce-scatter.2.cloned.1.call-update) | async-done | bytes 1048592 | tf_op jit(solution)/shard_map/reduce_scatter | solution.py:389
  (242 shorter events, 94.8 us)
Async XLA Ops:
  7.2 30.7 %copy-start = (bf16[1,1024,1024]{2,1,0:T(8,128)(2,1)S(1)}, bf16[1,1024,1024]{2,1,0:T(8,128)(2,1)}, u32[]{:S(2)}) copy-start(bf16[1,1024,1024]{2,1,0:T(8,128)(2,1)} %param.25) | copy-start | bytes 6291460
  7.2 186.4 %all-reduce.11.cloned.1.call-start = ((), (), s32[]{:S(2)}) async-start(), calls=%async_computation.1 | async-start | bytes 8388608 | tf_op jit(solution)/shard_map/psum | solution.py:342
  14.1 18.9 %copy-start.12 = (bf16[128,1024]{1,0:T(8,128)(2,1)}, bf16[128,1024]{1,0:T(8,128)(2,1)S(1)}, u32[]{:S(2)}) copy-start(bf16[128,1024]{1,0:T(8,128)(2,1)S(1)} %fusion.47.v_ref) | copy-start | bytes 786436
  15.7 17.2 %copy-start.43 = (bf16[256,1024]{1,0:T(8,128)(2,1)S(1)}, bf16[256,1024]{1,0:T(8,128)(2,1)}, u32[]{:S(2)}) copy-start(bf16[256,1024]{1,0:T(8,128)(2,1)} %param.31) | copy-start | bytes 1572868
  35.8 332.0 %all-reduce.13.cloned.1.call-start = ((), (), s32[]{:S(2)}) async-start(), calls=%async_computation.2 | async-start | bytes 8388608 | tf_op jit(solution)/shard_map/psum | solution.py:352
  41.0 156.1 %copy-start.41 = (bf16[1024,256]{1,0:T(8,128)(2,1)S(1)}, bf16[1024,256]{1,0:T(8,128)(2,1)}, u32[]{:S(2)}) copy-start(bf16[1024,256]{1,0:T(8,128)(2,1)} %param.34) | copy-start | bytes 1572868
  197.1 13.7 %copy-start.20 = (f32[1024,1024]{1,0:T(8,128)}, f32[1024,1024]{1,0:T(8,128)S(1)}, u32[]{:S(2)}) copy-start(f32[1024,1024]{1,0:T(8,128)S(1)} %get-tuple-element.110) | copy-start | bytes 12582916
  198.5 12.3 copy-start.10
  198.5 12.3 copy-start.39
  213.6 329.6 %all-reduce.15.cloned.1.call-start = ((), (), s32[]{:S(2)}) async-start(), calls=%async_computation.3 | async-start | bytes 8388608 | tf_op jit(solution)/shard_map/psum | solution.py:372
  389.1 343.1 %all-reduce.17.cloned.1.call-start = ((), (), s32[]{:S(2)}) async-start(), calls=%async_computation.4 | async-start | bytes 8388608 | tf_op jit(solution)/shard_map/psum | solution.py:387
  543.2 5.9 copy-start.35
  553.8 21.5 %copy-start.42 = (bf16[1024,256]{1,0:T(8,128)(2,1)S(1)}, bf16[1024,256]{1,0:T(8,128)(2,1)}, u32[]{:S(2)}) copy-start(bf16[1024,256]{1,0:T(8,128)(2,1)} %param.34) | copy-start | bytes 1572868
  578.0 393.7 %all-reduce.19.cloned.1.call-start = ((), (), s32[]{:S(2)}) async-start(), calls=%async_computation.6 | async-start | bytes 29884416 | tf_op jit(solution)/shard_map/psum | solution.py:416
  732.2 5.9 copy-start.31
  743.6 22.0 %copy-start.24 = (bf16[1024,1024]{1,0:T(8,128)(2,1)S(1)}, bf16[1024,1024]{1,0:T(8,128)(2,1)}, u32[]{:S(2)}) copy-start(bf16[1024,1024]{1,0:T(8,128)(2,1)} %copy-done.23) | copy-start | bytes 6291460
  770.5 6.5 copy-start.50
  770.5 496.2 %all-reduce.21.cloned.1.call-start = ((), (), s32[]{:S(2)}) async-start(), calls=%async_computation.7 | async-start | bytes 16777216 | tf_op jit(solution)/shard_map/psum | solution.py:359
  781.8 563.7 %reduce-scatter.2.cloned.1.call-start = ((), (), s32[]{:S(2)}) async-start(), calls=%async_computation.5 | async-start | bytes 5242880 | tf_op jit(solution)/shard_map/reduce_scatter | solution.py:389
  1296.8 5.7 copy-start.28
  1296.8 5.7 copy-start.33
  1296.8 7.3 copy-start.34
  1306.7 43.8 %copy-start.59 = (f32[256,1024]{1,0:T(8,128)S(1)}, f32[256,1024]{1,0:T(8,128)}, u32[]{:S(2)}) copy-start(f32[256,1024]{1,0:T(8,128)} %get-tuple-element.121) | copy-start | bytes 3145732
  1345.5 6.0 copy-start.58
  (61 other events, 136.8 us)
Sparse Core Ops, SparseCore 0:
  35.9 157.6 all-reduce.10
  213.7 153.9 all-reduce.12
  389.2 153.9 all-reduce.14
  578.1 153.9 all-reduce.16
  770.6 201.0 all-reduce.18
  975.0 291.7 all-reduce.20
  1269.7 75.7 reduce-scatter.1

commit v2 on v1

v2 whole, which is shorter than its diff:
```python
import functools
import jax, jax.numpy as jnp
import numpy as np
from jax import lax
from jax.experimental import pallas as pl
from jax.experimental.pallas import tpu as pltpu
from jax.sharding import PartitionSpec as P

DH = 64
eps = 1e-06
QB = 256
NEG = -1e30


def cost(scores, weight):
    return pl.CostEstimate(flops=0, transcendentals=0, bytes_accessed=scores * weight)


def mm(a, b, dims):
    return lax.dot_general(a, b, (dims, ((), ())), preferred_element_type=jnp.float32)


NN = ((1,), (0,))
NT = ((1,), (1,))
TN = ((0,), (0,))


def make_band(x_ref, head, band_ref):
    tiles = []
    for d in range(3):
        row = jnp.broadcast_to(x_ref[0, 3 * head + d, :].reshape(1, 256), (128, 256))
        tiles.append(pltpu.roll(row, 0, axis=1, stride=1, stride_axis=0)[:, :128])
    left = jnp.broadcast_to(x_ref[0, 6 + head, 0:128].reshape(1, 128), (128, 128))
    right = jnp.broadcast_to(x_ref[0, 6 + head, 128:256].reshape(1, 128), (128, 128))
    rows = [
        (left, left), (left, left), (left, left),
        (tiles[0], left), (tiles[1], tiles[0]), (tiles[2], tiles[1]), (right, tiles[2]),
        (right, right), (right, right), (right, right),
    ]
    for n, (a, b) in enumerate(rows):
        band_ref[head, n * 128:(n + 1) * 128, 0:128] = a
        band_ref[head, n * 128:(n + 1) * 128, 128:256] = b


def band_at(chunk, block):
    return pl.multiple_of((jnp.clip(chunk - block, -2, 2) + 2) * QB, QB)


def over_chunks(count, body, init):
    if isinstance(count, int):
        for c in range(count):
            init = body(c, init)
        return init
    return lax.fori_loop(0, count, body, init)


def ds(c):
    return pl.ds(pl.multiple_of(c * QB, QB), QB)


def part_sum(tile, op):
    return op(tile.reshape(QB // 8, 8, QB), axis=0)


def fwd_kernel(causal, row_ref, x_ref, q_ref, k_ref, v_ref, o_ref, l_ref, band, keys, s_ref):
    r = pl.program_id(1)
    block = r + row_ref[0]
    total_chunks = k_ref.shape[1] // QB

    @pl.when(r == 0)
    def _():
        for h in range(2):
            make_band(x_ref, h, band)
        keys[...] = k_ref[...].T

    count = block + 1 if causal else total_chunks
    for h in range(2):
        q = q_ref[h * DH:(h + 1) * DH, :]

        def scores(c, top):
            s = mm(keys[ds(c), :], q, NN) + band[h, pl.ds(band_at(c, block), QB), :]
            s_ref[ds(c), :] = s
            return jnp.maximum(top, part_sum(s, jnp.max))

        top = over_chunks(count, scores, jnp.full((8, QB), NEG, jnp.float32))
        top = jnp.max(top, axis=0, keepdims=True)

        def weigh(c, tot):
            e = jnp.exp(s_ref[ds(c), :] - top)
            s_ref[ds(c), :] = e
            return tot + part_sum(e, jnp.sum)

        tot = over_chunks(count, weigh, jnp.zeros((8, QB), jnp.float32))
        tot = jnp.sum(tot, axis=0, keepdims=True)
        inv = 1.0 / tot

        def mix(c, acc):
            p = (s_ref[ds(c), :] * inv).astype(jnp.bfloat16)
            return acc + mm(v_ref[:, ds(c)], p, NN)

        acc = over_chunks(count, mix, jnp.zeros((DH, QB), jnp.float32))
        o_ref[h * DH:(h + 1) * DH, :] = acc.astype(jnp.bfloat16)
        l_ref[0, h:h + 1, :] = top + jnp.log(tot)


def bwd_kernel(causal, row_ref, x_ref, q_ref, k_ref, v_ref, d_ref, l_ref,
               dq_ref, dk_ref, dv_ref, t_ref, band, keys, values, p_ref, g_ref, near):
    r = pl.program_id(1)
    block = r + row_ref[0]
    total_chunks = k_ref.shape[1] // QB

    @pl.when(r == 0)
    def _():
        for h in range(2):
            make_band(x_ref, h, band)
        keys[...] = k_ref[...].T
        values[...] = v_ref[...].T
        dk_ref[...] = jnp.zeros_like(dk_ref)
        dv_ref[...] = jnp.zeros_like(dv_ref)
        near[...] = jnp.zeros_like(near)

    count = block + 1 if causal else total_chunks
    for h in range(2):
        q = q_ref[h * DH:(h + 1) * DH, :]
        d = d_ref[h * DH:(h + 1) * DH, :]
        log_total = l_ref[0, h:h + 1, :]

        def weigh(c, dot):
            s = mm(keys[ds(c), :], q, NN) + band[h, pl.ds(band_at(c, block), QB), :]
            p = jnp.exp(s - log_total)
            dp = mm(values[ds(c), :], d, NN)
            p_ref[ds(c), :] = p
            g_ref[ds(c), :] = dp
            return dot + part_sum(p * dp, jnp.sum)

        dot = over_chunks(count, weigh, jnp.zeros((8, QB), jnp.float32))
        dot = jnp.sum(dot, axis=0, keepdims=True)

        def back(c, acc):
            p = p_ref[ds(c), :]
            low = (p * (g_ref[ds(c), :] - dot)).astype(jnp.bfloat16)
            dk_ref[:, ds(c)] += mm(q, low, NT)
            dv_ref[:, ds(c)] += mm(d, p.astype(jnp.bfloat16), NT)
            at = pl.ds(band_at(c, block), QB)
            near[h, at, :] += low.astype(jnp.float32)
            return acc + mm(k_ref[:, ds(c)], low, NN)

        acc = over_chunks(count, back, jnp.zeros((DH, QB), jnp.float32))
        dq_ref[h * DH:(h + 1) * DH, :] = acc.astype(jnp.bfloat16)

    @pl.when(r == pl.num_programs(1) - 1)
    def _():
        for h in range(2):
            def piece(n, side):
                return near[h, n * 128:(n + 1) * 128, side * 128:(side + 1) * 128]

            left = piece(3, 1) + sum(piece(n, 0) + piece(n, 1) for n in range(3))
            right = piece(6, 0) + sum(piece(n, 0) + piece(n, 1) for n in range(7, 10))
            tiles = [piece(3, 0) + piece(4, 1), piece(4, 0) + piece(5, 1), piece(5, 0) + piece(6, 1)]
            for n, tile in enumerate(tiles):
                wide = jnp.concatenate([tile, jnp.zeros_like(tile)], axis=1)
                rows = wide[0:8]
                for a in range(8, 128, 8):
                    rows = rows + pltpu.roll(wide[a:a + 8], 256 - a, axis=1)
                line = rows[0:1]
                for b in range(1, 8):
                    line = line + pltpu.roll(rows[b:b + 1], 256 - b, axis=1)
                t_ref[0, 5 * h + n:5 * h + n + 1, :] = line
            for n, far in enumerate((left, right)):
                t_ref[0, 5 * h + 3 + n:5 * h + 4 + n, 0:128] = jnp.sum(far, axis=0, keepdims=True)
                t_ref[0, 5 * h + 3 + n:5 * h + 4 + n, 128:256] = jnp.zeros((1, 128), jnp.float32)


def specs(rows, keys):
    smem = pl.BlockSpec(memory_space=pltpu.SMEM)
    return dict(
        smem=smem,
        x=pl.BlockSpec((1, 8, 256), lambda g, r: (g, 0, 0)),
        q=pl.BlockSpec((2 * DH, QB), lambda g, r: (g, r)),
        k=pl.BlockSpec((DH, keys), lambda g, r: (4 * (g // 2) + g % 2, 0)),
        v=pl.BlockSpec((DH, keys), lambda g, r: (4 * (g // 2) + g % 2 + 2, 0)),
        dk=pl.BlockSpec((DH, keys), lambda g, r: (g, 0)),
        l=pl.BlockSpec((1, 2, QB), lambda g, r: (g, 0, r)),
        t=pl.BlockSpec((1, 10, 256), lambda g, r: (g, 0, 0)),
    )


def attend(row, x, q, kv, causal):
    groups, keys, rows = kv.shape[0] // (2 * DH), kv.shape[1], q.shape[1]
    s = specs(rows, keys)
    return pl.pallas_call(
        functools.partial(fwd_kernel, causal),
        out_shape=(jax.ShapeDtypeStruct(q.shape, jnp.bfloat16),
                   jax.ShapeDtypeStruct((groups, 2, rows), jnp.float32)),
        grid=(groups, rows // QB),
        in_specs=[s["smem"], s["x"], s["q"], s["k"], s["v"]],
        out_specs=(s["q"], s["l"]),
        scratch_shapes=[pltpu.VMEM((2, 10 * 128, 256), jnp.float32), pltpu.VMEM((keys, DH), jnp.bfloat16),
                        pltpu.VMEM((keys, QB), jnp.float32)],
        compiler_params=pltpu.CompilerParams(dimension_semantics=("arbitrary", "arbitrary"), vmem_limit_bytes=24 << 20),
        cost_estimate=cost(2 * groups * rows * keys, 11),
        name="attend",
    )(row, x, q, kv, kv)


def attend_back(row, x, q, kv, d, logs, causal):
    groups, keys, rows = kv.shape[0] // (2 * DH), kv.shape[1], q.shape[1]
    s = specs(rows, keys)
    return pl.pallas_call(
        functools.partial(bwd_kernel, causal),
        out_shape=(jax.ShapeDtypeStruct(q.shape, jnp.bfloat16),
                   jax.ShapeDtypeStruct((groups * DH, keys), jnp.float32),
                   jax.ShapeDtypeStruct((groups * DH, keys), jnp.float32),
                   jax.ShapeDtypeStruct((groups, 10, 256), jnp.float32)),
        grid=(groups, rows // QB),
        in_specs=[s["smem"], s["x"], s["q"], s["k"], s["v"], s["q"], s["l"]],
        out_specs=(s["q"], s["dk"], s["dk"], s["t"]),
        scratch_shapes=[pltpu.VMEM((2, 10 * 128, 256), jnp.float32), pltpu.VMEM((keys, DH), jnp.bfloat16),
                        pltpu.VMEM((keys, DH), jnp.bfloat16),
                        pltpu.VMEM((keys, QB), jnp.float32), pltpu.VMEM((keys, QB), jnp.float32),
                        pltpu.VMEM((2, 10 * 128, 256), jnp.float32)],
        compiler_params=pltpu.CompilerParams(dimension_semantics=("arbitrary", "arbitrary"), vmem_limit_bytes=32 << 20),
        cost_estimate=cost(2 * groups * rows * keys, 18),
        name="attend_back",
    )(row, x, q, kv, kv, d, logs)


MAXDIST = 128


def side_buckets(n, buckets):
    exact = buckets // 2
    scaled = np.log(np.maximum(n, 1) / exact) / np.log(MAXDIST / exact)
    far = np.minimum(exact + np.floor(scaled * (buckets - exact)).astype(np.int64), buckets - 1)
    return np.where(n < exact, n, far)


def relative_buckets(r, two_sided, buckets):
    if two_sided:
        per = buckets // 2
        return side_buckets(np.abs(r), per) + np.where(r > 0, per, 0)
    return side_buckets(np.maximum(-r, 0), buckets)


def lane_offsets():
    m = np.arange(256)
    return np.stack([128 * d - np.where(m < 128, m, m - 256) for d in (-1, 0, 1)])


def bias_vectors(table, two_sided):
    buckets, heads = table.shape
    rel = lane_offsets()
    ids = relative_buckets(rel, two_sided, buckets)
    onehot = (ids.reshape(-1)[:, None] == np.arange(buckets)[None, :])
    x = jnp.dot(jnp.asarray(onehot, jnp.bfloat16), table, preferred_element_type=jnp.float32)
    x = x.reshape(3, 256, heads)
    last = table.shape[0] - 1
    if two_sided:
        left, right = table[last // 2].astype(jnp.float32), table[last].astype(jnp.float32)
    else:
        x = jnp.where(jnp.asarray(rel > 0)[:, :, None], NEG, x)
        left, right = table[last].astype(jnp.float32), jnp.full((heads,), NEG, jnp.float32)
    x = jnp.transpose(x, (2, 0, 1)).reshape(heads // 2, 6, 256)
    far = jnp.stack([left, right], axis=1).reshape(heads // 2, 2, 2, 1)
    return jnp.concatenate([x, jnp.broadcast_to(far, far.shape[:3] + (128,)).reshape(heads // 2, 2, 256)], axis=1)


def table_gradient(t, two_sided, buckets):
    groups = t.shape[0]
    t = t.reshape(2 * groups, 5, 256)
    rel = lane_offsets()
    ids = relative_buckets(rel, two_sided, buckets)
    onehot = np.zeros((5, 256, buckets), np.float32)
    onehot[:3] = (ids[:, :, None] == np.arange(buckets)) & (np.arange(256) != 128)[None, :, None]
    last = buckets - 1
    if two_sided:
        onehot[3, :, last // 2] = 1
        onehot[4, :, last] = 1
    else:
        onehot[:3] *= (rel <= 0)[:, :, None]
        onehot[3, :, last] = 1
    return lax.dot_general(jnp.asarray(onehot.reshape(5 * 256, buckets), jnp.bfloat16).astype(jnp.float32), t.reshape(2 * groups, 5 * 256),
                           (((0,), (1,)), ((), ())), precision=lax.Precision.HIGHEST)


def norm_rows(hidden, gain_vec):
    inv_scale = lax.rsqrt(jnp.mean(hidden * hidden, axis=-1, keepdims=True) + eps)
    return hidden * inv_scale * gain_vec


def gate_times_up(gate_value, up_value):
    return jax.nn.gelu(gate_value, approximate=True) * up_value


T0 = ((0,), (1,))


def block_of(x, index, size, axis=0):
    return lax.dynamic_slice_in_dim(x, index * size, size, axis)


class Gather:
    def __init__(self, x, n):
        self.n, self.x, self.d = n, x, 0
        self.right = self.left = x
        self.from_left, self.from_right = [], []

    def hop(self, tie, *others):
        n, self.d = self.n, self.d + 1
        d = self.d
        self.right = lax.ppermute(tie(self.right, *others), "kv", [(i, i + 1) for i in range(d - 1, n - 1)])
        self.left = lax.ppermute(tie(self.left, *others), "kv", [(i + 1, i) for i in range(n - d)])
        self.from_left.append(self.right)
        self.from_right.append(self.left)
        return [self.right, self.left]

    def blocks(self):
        n = self.n
        return [self.x] + [self.from_right[d - 1] + self.from_left[n - d - 1] for d in range(1, n)]


class Scatter:
    def __init__(self, parts, n):
        self.n, self.parts, self.d = n, parts, n
        self.got = [0.0, 0.0]

    def hop(self, tie, *others):
        n, self.d = self.n, self.d - 1
        d = self.d
        right, left = self.parts[d] + self.got[0], self.parts[n - d] + self.got[1]
        self.got = [
            lax.ppermute(tie(right, *others), "kv", [(i, i + 1) for i in range(n - d)]),
            lax.ppermute(tie(left, *others), "kv", [(i + 1, i) for i in range(d - 1, n - 1)]),
        ]
        return self.got

    def total(self):
        return self.parts[0] + self.got[0] + self.got[1]


def in_order(blocks, z, n):
    stacked = jnp.stack(blocks)
    return jnp.concatenate(
        [lax.dynamic_index_in_dim(stacked, (j - z + n) % n, 0, keepdims=False) for j in range(n)]
    )


def exchange(blocks, n):
    got = [blocks[0]]
    for d in range(1, n):
        got.append(lax.ppermute(blocks[n - d], "kv", [((i + d) % n, i) for i in range(n)]))
    return got


def whole_kernel(thin, deep, shares_ref, in_ref, so_ref, co_ref, *refs):
    so_out, co_out, cq_out, kv_out = refs[-4:]
    d = pl.program_id(0)
    half = shares_ref.shape[3]
    qcols = cq_out.shape[2]

    @pl.when(d == 0)
    def _():
        so_out[...] = so_ref[...]
        co_out[...] = co_ref[...]
        cq_out[0] = in_ref[:, :qcols]
        kv_out[0] = in_ref[:, qcols:]

    @pl.when(d > 0)
    def _():
        for i in range(shares_ref.shape[0]):
            here = shares_ref[i, 0, 0:deep, :].astype(jnp.bfloat16)
            cq_out[0, i * deep:(i + 1) * deep, :] = here[:, :qcols]
            kv_out[0, i * deep:(i + 1) * deep, :] = here[:, qcols:]
            for n, ref in enumerate((so_out, co_out)):
                for side in range(2):
                    at = deep + (2 * n + side) * thin
                    ref[i * thin:(i + 1) * thin, side * half:(side + 1) * half] = (
                        shares_ref[i, 0, at:at + thin, :].astype(jnp.bfloat16)
                    )


def whole_weights(shares, own_in, own_so, own_co, earlier):
    nb, others = shares.shape[:2]
    width, cols = own_in.shape
    tall = own_so.shape[0]
    step = 4
    turns = nb // step
    own = lambda d, i: (jnp.where(d == 0, i, turns - 1), 0)
    flat = pl.BlockSpec((tall // turns, width), lambda d, i: (d * turns + i, 0))
    deep = pl.BlockSpec((1, width // turns, cols // 2), lambda d, i: (d, i, 0))
    return pl.pallas_call(
        functools.partial(whole_kernel, tall // nb, width // nb),
        out_shape=(jax.ShapeDtypeStruct(((others + 1) * tall, width), jnp.bfloat16),) * 2
        + (jax.ShapeDtypeStruct((others + 1, width, cols // 2), jnp.bfloat16),) * 2,
        grid=(others + 1, turns),
        in_specs=[
            pl.BlockSpec((step, 1) + shares.shape[2:], lambda d, i: (jnp.where(d == 0, 0, i), jnp.maximum(d - 1, 0), 0, 0)),
            pl.BlockSpec((width // turns, cols), own),
            pl.BlockSpec((tall // turns, width), own),
            pl.BlockSpec((tall // turns, width), own),
        ] + [pl.BlockSpec((16, 128), lambda d, i: (0, 0))] * len(earlier),
        out_specs=(flat, flat, deep, deep),
        compiler_params=pltpu.CompilerParams(dimension_semantics=("arbitrary", "arbitrary"), vmem_limit_bytes=32 << 20),
        cost_estimate=cost(shares.size, 7),
        name="whole_weights",
    )(shares, own_in, own_so, own_co, *earlier)


def on_device(
    inputs,
    memory,
    out_grad,
    gain_self,
    self_query,
    self_key,
    self_value,
    self_output,
    self_table,
    gain_cross,
    cross_query,
    cross_key,
    cross_value,
    cross_output,
    cross_table,
    gain_ffn,
    ffn_gate,
    ffn_up,
    ffn_down,
):
    seq_len = inputs.shape[1]
    width = inputs.shape[2]
    n, nb = lax.axis_size("kv"), lax.axis_size("batch")
    z, b = lax.axis_index("kv"), lax.axis_index("batch")
    rows = seq_len // n
    low = jnp.bfloat16
    one = jnp.where(gain_self[0] < 100, 1.0, 2.0).astype(jnp.float32)

    def settle(x):
        return x * one

    def tie(x, *others):
        for other in others:
            x = x + other[(0,) * other.ndim].astype(jnp.float32) * (one - 1.0)
        return x

    def share(w):
        return block_of(w, b, w.shape[0] // nb).astype(jnp.float32)

    def halves(x):
        return jnp.concatenate([x[:, :width // 2], x[:, width // 2:]])

    qcols, kcols, ocols = cross_query.shape[1], cross_key.shape[1], cross_output.shape[0]
    far_pairs = [(i, i ^ 2) for i in range(n)]
    near_pairs = [(i, i ^ 1) for i in range(n)]
    cross_kv = jnp.concatenate([cross_key, cross_value], axis=1)
    unit = jnp.concatenate(
        [
            jnp.concatenate([share(cross_query), share(cross_kv)], axis=1),
            halves(share(self_output)),
            halves(share(cross_output)),
        ]
    )
    units = exchange([unit] * n, n)[1:]

    gain_one = gain_self.astype(jnp.float32)
    gain_two = gain_cross.astype(jnp.float32)
    gain_three = gain_ffn.astype(jnp.float32)
    self_x, own_cross_x = bias_vectors(self_table, False), bias_vectors(cross_table, True)

    flat_in = inputs.reshape(seq_len, width).astype(jnp.float32)
    flat_mem = memory.reshape(memory.shape[1], width)
    attn_in = norm_rows(flat_in, gain_one).astype(low)
    zero = jnp.zeros((1,), jnp.int32)
    self_kv = jnp.concatenate([self_key, self_value], axis=1)
    sq = mm(self_query, attn_in, T0).astype(low)
    skv = mm(self_kv, attn_in, T0).astype(low)
    mixed, self_log = attend(zero, self_x, sq, skv, True)
    buckets, heads = self_table.shape
    deep, thin = width // nb, ocols // nb
    shares = lax.all_gather(tie(jnp.stack(units), mixed), "batch")
    mixed = tie(mixed.astype(jnp.float32), *units)
    rider = own_cross_x.reshape(-1, rows)
    got = exchange([jnp.concatenate([block_of(mixed, (z + d) % n, rows, 1), rider]) for d in range(n)], n)
    others = got[1:]
    mixed_self = settle(jnp.concatenate([x[:ocols] for x in got])).astype(low)
    cross_x = jnp.concatenate([x[ocols:] for x in got]).reshape(-1, 8, rows)
    own_in = jnp.concatenate([cross_query, cross_kv], axis=1)
    whole_so, whole_co, whole_cq, whole_kv = whole_weights(
        shares, own_in, self_output, cross_output, [mixed_self, cross_x.reshape(-1, rows)]
    )

    sent = jnp.stack([share(ffn_gate.T), share(ffn_up.T), share(ffn_down)])
    fetched = lax.ppermute(tie(sent, *others), "kv", far_pairs)
    sent = lax.all_gather(tie(fetched, whole_so), "batch", axis=1, tiled=True)

    in_rows = block_of(flat_in, z, rows)
    after_self = in_rows + mm(mixed_self, whole_so, TN)

    def into(w, x):
        y = lax.dot_general(w, x, (((1,), (1,)), ((), ())), preferred_element_type=jnp.float32)
        return y.astype(low).reshape(-1, x.shape[0])

    ckv = into(whole_kv, flat_mem)
    cross_in = norm_rows(after_self, gain_two).astype(low)
    cq = into(whole_cq, cross_in)
    place = z.reshape(1).astype(jnp.int32) * (rows // QB)
    mixed_cross, cross_log = attend(place, cross_x, cq, ckv, False)
    after_cross = after_self + mm(mixed_cross, whole_co, TN)

    own_self = jnp.concatenate([self_query, self_kv], axis=1)
    unit = tie(jnp.concatenate([share(self_query), share(self_kv)], axis=1), fetched)
    rest_self = lax.all_gather(tie(jnp.stack(exchange([unit] * n, n)[1:]), after_cross), "batch", axis=1, tiled=True)
    rest_self = settle(rest_self).astype(low)

    ffn_in = norm_rows(after_cross, gain_three).astype(low)
    other = settle(lax.ppermute(ffn_in.astype(jnp.float32), "kv", near_pairs)).astype(low)
    flat_grad = out_grad.reshape(seq_len, width)
    own_grad = block_of(flat_grad, z, rows)
    far_ffn = settle(sent).astype(low)
    weights = ((ffn_gate, ffn_up, ffn_down, False), (far_ffn[0], far_ffn[1], far_ffn[2], True))
    parts, grads, inputs_of = [], [], ((ffn_in, own_grad), (other, block_of(flat_grad, z ^ 1, rows)))
    for x, dy in inputs_of:
        in_part = out_part = 0.0
        for w_gate, w_up, w_down, turned in weights:
            there, back = (NT, NN) if turned else (NN, NT)
            gate_pre, up_pre = mm(x, w_gate, there), mm(x, w_up, there)
            hidden = gate_times_up(gate_pre, up_pre).astype(low)
            out_part = out_part + mm(hidden, w_down, NN)
            gate_grad, up_grad = jax.vjp(gate_times_up, gate_pre, up_pre)[1](mm(dy, w_down, NT))
            gate_grad, up_grad = gate_grad.astype(low), up_grad.astype(low)
            in_part = in_part + mm(gate_grad, w_gate, back) + mm(up_grad, w_up, back)
            grads.append((gate_grad, up_grad, hidden))
        parts.append((in_part, out_part))
    ffn_in_grad = parts[0][0] + lax.ppermute(parts[1][0], "kv", near_pairs)
    both_in, both_grad = (jnp.concatenate(x) for x in zip(*inputs_of))
    ffn_sums = jnp.stack(
        [
            mm(jnp.concatenate([grads[side][kind], grads[2 + side][kind]]), both_grad if kind == 2 else both_in, TN)
            for side in range(2) for kind in range(3)
        ]
    )
    ffn_sums = lax.psum_scatter(ffn_sums, "batch", scatter_dimension=1, tiled=True)
    ffn_out = parts[0][1] + lax.ppermute(tie(parts[1][1], ffn_in_grad), "kv", near_pairs)

    norm_grad, grad_gain_ffn = jax.vjp(norm_rows, after_cross, gain_three)[1](ffn_in_grad)
    cross_out_grad = own_grad.astype(jnp.float32) + norm_grad
    branch_cross = cross_out_grad.astype(low)
    mixed_grad = mm(whole_co, branch_cross, NT).astype(low)
    cq_grad, ck_grad, cv_grad, cross_lines = attend_back(
        place, cross_x, cq, ckv, mixed_grad, cross_log, False
    )
    result = (tie(after_cross, cq_grad) + ffn_out).astype(low).astype(jnp.float32)
    line = Gather(result, n)
    first = line.hop(tie)
    cross_in_grad = lax.dot_general(
        cq_grad.reshape(n, qcols, rows), whole_cq, (((0, 1), (0, 2)), ((), ())), preferred_element_type=jnp.float32
    )
    norm_grad, grad_gain_cross = jax.vjp(norm_rows, after_self, gain_two)[1](cross_in_grad)
    self_out_grad = cross_out_grad + norm_grad
    branch_self = self_out_grad.astype(low)
    mixed_grad = tie(mm(whole_so, branch_self, NT).astype(low).astype(jnp.float32), result)
    got = exchange([mixed_grad[d * ocols:(d + 1) * ocols] for d in range(n)], n)
    arrived = got[1:]
    stacked = jnp.stack(got)
    mixed_grad = tie(
        jnp.concatenate(
            [lax.dynamic_index_in_dim(stacked, (j - z + n) % n, 0, keepdims=False) for j in range(n)], axis=1
        ),
        *first,
    )
    mixed_grad = settle(mixed_grad).astype(low)
    ckv_grad = jnp.concatenate(
        [ck_grad.reshape(n, kcols, -1), cv_grad.reshape(n, kcols, -1)], axis=1
    ).astype(low)
    memory_part = [
        lax.dot_general(ckv_grad, block_of(whole_kv, (z + d) % n, width // n, 1),
                        (((0, 1), (0, 2)), ((), ())), preferred_element_type=jnp.float32)
        for d in range(n)
    ]

    sq_grad, sk_grad, sv_grad, self_lines = attend_back(zero, self_x, sq, skv, mixed_grad, self_log, True)
    skv_grad = jnp.concatenate([sk_grad, sv_grad]).astype(low)
    memory_line = Scatter(memory_part, n)
    second, memory_one = line.hop(tie), memory_line.hop(tie)
    turned = jnp.concatenate([sq_grad, skv_grad]).astype(jnp.float32)
    got = exchange([tie(block_of(turned, (z + d) % n, rows, 1), *second, *memory_one) for d in range(n)], n)
    rest = settle(jnp.stack(got[1:])).astype(low)
    attn_in_grad = mm(got[0].astype(low), own_self, T0) + lax.dot_general(
        rest, rest_self, (((0, 1), (0, 2)), ((), ())), preferred_element_type=jnp.float32
    )
    early = got[1:]
    third, memory_two = line.hop(tie), memory_line.hop(tie)
    attn_term = mm(sq_grad, self_query, T0) + mm(skv_grad, self_kv, T0)
    norm_grad, _ = jax.vjp(norm_rows, in_rows, gain_one)[1](attn_in_grad)
    last = tie(self_out_grad + norm_grad, *third, *memory_two)
    _, grad_gain_self = jax.vjp(norm_rows, flat_in, gain_one)[1](attn_term)

    ends_line = Gather(last, n)
    one_hop = ends_line.hop(tie)
    memory_three = memory_line.hop(tie)
    two_hops = ends_line.hop(tie)
    ends_line.hop(tie)
    layer_out = settle(in_order(line.blocks(), z, n)).astype(low)
    input_grad = in_order(ends_line.blocks(), z, n)
    memory_grad = memory_line.total()

    self_tab = table_gradient(self_lines, False, buckets)
    cross_tab = table_gradient(cross_lines, True, buckets)
    spots = [(z + d) % n for d in range(n)]
    tabs = jnp.zeros((2, n, buckets * heads), jnp.float32)
    tabs = lax.dynamic_update_slice(tabs, self_tab.reshape(1, 1, -1), (0, z, 0))
    for d in range(n):
        tabs = lax.dynamic_update_slice(
            tabs, cross_tab[:, d * heads:(d + 1) * heads].reshape(1, 1, -1), (1, spots[d], 0)
        )
    small = jnp.stack([grad_gain_self, grad_gain_cross, grad_gain_ffn, jnp.pad(tabs.reshape(-1), (0, width - tabs.size))], axis=1)
    small = jnp.pad(small, ((0, 0), (0, 124)))
    sums = jnp.concatenate(
        [
            mm(branch_cross, mixed_cross, T0),
            mm(cross_in, cq_grad, T0),
            mm(flat_mem, ckv_grad.reshape(-1, flat_mem.shape[0]), T0),
            mm(branch_self, mixed_self, T0),
            mm(attn_in, sq_grad, T0),
            mm(attn_in, skv_grad, T0),
            small,
        ],
        axis=1,
    )
    sums = lax.psum_scatter(sums, "batch", tiled=True)
    self_sums, small = sums[:, 4 * width:-128], sums[:, -128:]
    attn_line = Scatter(
        [
            jnp.concatenate(
                [sums[:, at * width + d * size:at * width + (d + 1) * size]
                 for at, size in enumerate((ocols, qcols, 2 * kcols, ocols))] + [small],
                axis=1,
            )
            for d in range(n)
        ],
        n,
    )
    attn_line.hop(tie, *one_hop)
    attn_line.hop(tie)
    attn_line.hop(tie)
    attn_sums = attn_line.total()
    ffn_sums = ffn_sums[:3] + lax.ppermute(tie(ffn_sums[3:], sq_grad), "kv", far_pairs)
    ffn_sums = lax.all_gather(tie(ffn_sums, last), "batch", axis=1, tiled=True)
    attn_sums = lax.all_gather(tie(jnp.concatenate([attn_sums, self_sums], axis=1), *memory_three), "batch", tiled=True)

    def columns(x, sizes):
        at = 0
        for size in sizes:
            yield x[:, at:at + size]
            at += size

    grad_co, grad_cq, grad_ck, grad_cv, grad_so, small, grad_sq, grad_sk, grad_sv = columns(
        attn_sums,
        (ocols, qcols, kcols, kcols, ocols, 128, self_query.shape[1], self_key.shape[1], self_value.shape[1]),
    )
    small = small[:, :4].T
    tabs = small[3, :tabs.size].reshape(tabs.shape)
    tabs = lax.dynamic_index_in_dim(tabs, z, 1, keepdims=False).reshape(2, buckets, heads)
    return (
        layer_out.reshape(inputs.shape),
        input_grad.reshape(inputs.shape),
        memory_grad.reshape(1, memory.shape[1], width // n),
        small[0],
        grad_sq,
        grad_sk,
        grad_sv,
        grad_so.T,
        tabs[0],
        small[1],
        grad_cq,
        grad_ck,
        grad_cv,
        grad_co.T,
        tabs[1],
        small[2],
        ffn_sums[0].T,
        ffn_sums[1].T,
        ffn_sums[2],
    )


def solution(mesh):
    return jax.shard_map(
        on_device,
        mesh=mesh,
        in_specs=(
            P("batch", None, None),
            P("batch", None, None),
            P("batch", None, None),
            P(),
            P(None, "kv"),
            P(None, "kv"),
            P(None, "kv"),
            P("kv", None),
            P(None, "kv"),
            P(),
            P(None, "kv"),
            P(None, "kv"),
            P(None, "kv"),
            P("kv", None),
            P(None, "kv"),
            P(),
            P(None, "kv"),
            P(None, "kv"),
            P("kv", None),
        ),
        out_specs=(
            P("batch", None, None),
            P("batch", None, None),
            P("batch", None, "kv"),
            P(),
            P(None, "kv"),
            P(None, "kv"),
            P(None, "kv"),
            P("kv", None),
            P(None, "kv"),
            P(),
            P(None, "kv"),
            P(None, "kv"),
            P(None, "kv"),
            P("kv", None),
            P(None, "kv"),
            P(),
            P(None, "kv"),
            P(None, "kv"),
            P("kv", None),
        ),
        check_vma=False,
    )
```

time: 1380 us -> 836 us (0.61)
  waiting for transfers between devices: 1110 us -> 273 us
  starting transfers between devices: 1.43 us -> 148 us
  local copies, waits for them, and re-layouts: 36.5 us -> 111 us
  other arithmetic: 38.9 us -> 72.4 us
  matrix products: 71.6 us -> 104 us
  blocking collectives: 25.8 us -> 0 us
  between operations: 15.1 us -> 36.4 us
    psum x6 -> x0, waiting for transfers between devices: 1070 us -> none  [the longest x1 291 us: on_device(): lax.psum(jnp.dot(hidden, ffn_down, preferred_element_type=jnp.float32), '...]
    ppermute x0 -> x44, waiting for transfers between devices: none -> 251 us  [the longest x15 94.1 us: exchange(): lax.ppermute(blocks[n - d], 'kv', [((i + d) % n, i) for i in range(n)])]
    ppermute x0 -> x44, starting transfers between devices: none -> 148 us  [the longest x6 41.4 us: hop(): lax.ppermute(tie(right, *others), 'kv', [(i, i + 1) for i in range(n - d)])]
    dot_general x24 -> x45, matrix products: 37.5 us -> 77.7 us  [mm(): lax.dot_general(a, b, (dims, ((), ())), preferred_element_type=jnp.float32)]
    reduce_scatter x1 -> x2, waiting for transfers between devices: 38.8 us -> 0.04 us  [the longest x1 0.02 us: on_device(): lax.psum_scatter(ffn_sums, 'batch', scatter_dimension=1, tiled=True)]
    slice x0 -> x46, local copies, waits for them, and re-layouts: none -> 36.8 us  [the longest x29 28.5 us: tie(): x = x + other[(0,) * other.ndim].astype(jnp.float32) * (one - 1.0)]
    add x1 -> x20, other arithmetic: 2.58 us -> 28.8 us  [the longest x12 21.6 us: tie(): x = x + other[(0,) * other.ndim].astype(jnp.float32) * (one - 1.0)]
    psum x1 -> x0, blocking collectives: 25.8 us -> none  [on_device(): lax.psum((grad_gain_self, grad_sq, grad_sk, grad_sv, grad_self_out, grad_...]
  transfers between devices with their start and end apart: 7 -> 51, of which waited for: 7 -> 23; matrix products, arithmetic and copies ran while one was open for 4% -> 26% of each run, Pallas kernels for 0% -> 10%
where the time goes in v2:
time: 836 us; the launch traced here: 824 us
  waiting for transfers between devices  273 us (33%)
  starting transfers between devices  148 us (18%)
  local copies, waits for them, and re-layouts  111 us (13%)
  matrix products  104 us (12%)
  Pallas kernels  79.2 us (9%)
  other arithmetic  72.4 us (9%)
  between operations  36.4 us (4%)
    ppermute x15, waiting for transfers between devices, exchange(): lax.ppermute(blocks[n - d], 'kv', [((i + d) % n, i) for i in range(n)])  94.1 us
    dot_general x45, matrix products, mm(): lax.dot_general(a, b, (dims, ((), ())), preferred_element_type=jnp.float32)  77.7 us
    pallas_call x2, Pallas kernels, attend_back(): pl.pallas_call(functools.partial(bwd_kernel, causal), out_shape=(jax.Shap...  42.9 us
    unnamed x241, local copies, waits for them, and re-layouts  42 us
    ppermute x6, starting transfers between devices, hop(): lax.ppermute(tie(right, *others), 'kv', [(i, i + 1) for i in range(n - d)])  41.4 us
    ppermute x6, waiting for transfers between devices, hop(): lax.ppermute(tie(right, *others), 'kv', [(i, i + 1) for i in range(n - d)])  41.1 us
    ppermute x1, starting transfers between devices, on_device(): lax.ppermute(tie(ffn_sums[3:], sq_grad), 'kv', far_pairs)  37.4 us
    ppermute x6, waiting for transfers between devices, hop(): lax.ppermute(tie(self.left, *others), 'kv', [(i + 1, i) for i in range(n...  34.3 us
  transfers between devices with their start and end apart: 51, of which 23 were waited for; matrix products, arithmetic and copies ran while one was open for 26% of the time, Pallas kernels for 10%

profile of v2, /device:TPU:0, one launch (start us, length us, event | category | flops | bytes accessed | tf_op | source)
XLA Modules:
  0.0 823.9 jit_solution(13540251312607158113)
XLA Ops:
  30.4 16.6 %attend.2 = (bf16[256,1024]{1,0:T(8,128)(2,1)S(1)}, f32[2,2,1024]{2,1,0:T(2,128)S(1)}) custom-call(s32[1]{0:T(128)} %constant.180.clone.1.row_ref, f32[2,8,256]{2,1,0:T(8,128)S(1)} %pad_maximum_fusion.16.x_ref, bf16[256,1024]{1,0:T(8,128)(2,1)S(1)} %fusion.24.q_ref, bf16[256,1024]{1,0:T(8,128)(2,1)S(1)} %convolution_convert_fusion.3.k_ref.v_ref, ...), custom_call_target="tpu_custom_call" | custom-call | bytes 46137344 | tf_op jit(solution)/shard_map/attend/pallas_call | solution.py:191
  67.5 12.7 %collective-permute-start.3 = (f32[272,256]{1,0:T(8,128)}, f32[272,256]{1,0:T(8,128)}, u32[]{:S(2)}, u32[]{:S(2)}) collective-permute-start(f32[272,256]{1,0:T(8,128)} %get-tuple-element.198), channel_id=1, source_target_pairs={{1,0},{2,1},{3,2},{0,3},{5,4},{6,5},{7,6},{4,7},{9,8},{10,9},{11,1... | collective-permute-start | bytes 835592 | tf_op jit(solution)/shard_map/ppermute | solution.py:351
  89.5 15.9 %collective-permute-done.4 = f32[272,256]{1,0:T(8,128)} collective-permute-done((f32[272,256]{1,0:T(8,128)}, f32[272,256]{1,0:T(8,128)}, u32[]{:S(2)}, u32[]{:S(2)}) %collective-permute-start.4) | collective-permute-done | bytes 278560 | tf_op jit(solution)/shard_map/ppermute | solution.py:351
  118.7 22.1 %all-gather.6.cloned.1.call-done.shares_ref = f32[8,3,256,512]{3,2,1,0:T(8,128)} async-done(((f32[1,3,256,512]{3,2,1,0:T(8,128)}), f32[8,3,256,512]{3,2,1,0:T(8,128)}) %all-gather.6.cloned.1.call-update) | async-done | bytes 12582928 | tf_op jit(solution)/shard_map/all_gather | solution.py:480
  144.1 7.2 whole_weights.1
  173.6 12.5 %attend.3 = (bf16[1024,256]{1,0:T(8,128)(2,1)S(1)}, f32[8,2,256]{2,1,0:T(2,128)S(1)}) custom-call(s32[1]{0:T(128)} %bitcast.18.row_ref, f32[8,8,256]{2,1,0:T(8,128)S(1)} %get-tuple-element.192.x_ref, bf16[1024,256]{1,0:T(8,128)(2,1)S(1)} %bitcast.301, bf16[1024,1024]{1,0:T(8,128)(2,1)S(1)} %bitcast.297, bf16[1024,1024]{1,0:T(8,128)(2,1)S(1)} %bitcast.298), custom_call_target="tpu_custom_call" | custom-call | bytes 46137344 | tf_op jit(solution)/shard_map/attend/pallas_call | solution.py:191
  192.4 20.2 %collective-permute-done.7 = f32[256,1024]{1,0:T(8,128)S(1)} collective-permute-done((f32[256,1024]{1,0:T(8,128)S(1)}, f32[256,1024]{1,0:T(8,128)S(1)}, u32[]{:S(2)}, u32[]{:S(2)}) %collective-permute-start.7) | collective-permute-done | bytes 1048608 | tf_op jit(solution)/shard_map/ppermute | solution.py:516
  254.9 9.8 %collective-permute-done.25 = f32[128,512]{1,0:T(8,128)} collective-permute-done((f32[128,512]{1,0:T(8,128)}, f32[128,512]{1,0:T(8,128)}, u32[]{:S(2)}, u32[]{:S(2)}) %collective-permute-start.25) | collective-permute-done | bytes 262176 | tf_op jit(solution)/shard_map/ppermute | solution.py:351
  286.2 19.3 %collective-permute-done.8 = f32[256,1024]{1,0:T(8,128)S(1)} collective-permute-done((f32[256,1024]{1,0:T(8,128)S(1)}, f32[256,1024]{1,0:T(8,128)S(1)}, u32[]{:S(2)}, u32[]{:S(2)}) %collective-permute-start.8) | collective-permute-done | bytes 1048608 | tf_op jit(solution)/shard_map/ppermute | solution.py:534
  316.5 21.2 %attend_back.2 = (bf16[1024,256]{1,0:T(8,128)(2,1)S(1)}, f32[512,1024]{1,0:T(8,128)S(1)}, f32[512,1024]{1,0:T(8,128)S(1)}, f32[8,10,256]{2,1,0:T(8,128)S(1)}) custom-call(s32[1]{0:T(128)} %bitcast.18.row_ref, f32[8,8,256]{2,1,0:T(8,128)S(1)} %get-tuple-element.192.x_ref, bf16[1024,256]{1,0:T(8,128)(2,1)S(1)} %bitcast.302, bf16[1024,1024]{1,0:T(8,128)(2,1)S(1)} %bitcast.299, ...), custom_call_target="tpu_custom_call" | custom-call | bytes 75497472 | tf_op jit(solution)/shard_map/attend_back/pallas_call | solution.py:209
  396.6 20.3 %collective-permute-done.18 = f32[256,256]{0,1:T(8,128)S(1)} collective-permute-done((f32[256,256]{0,1:T(8,128)S(1)}, f32[256,256]{0,1:T(8,128)S(1)}, u32[]{:S(2)}, u32[]{:S(2)}) %collective-permute-start.18) | collective-permute-done | bytes 262176 | tf_op jit(solution)/shard_map/ppermute | solution.py:351
  416.9 11.4 %collective-permute-done.17 = f32[256,256]{0,1:T(8,128)S(1)} collective-permute-done((f32[256,256]{0,1:T(8,128)S(1)}, f32[256,256]{0,1:T(8,128)S(1)}, u32[]{:S(2)}, u32[]{:S(2)}) %collective-permute-start.17) | collective-permute-done | bytes 262176 | tf_op jit(solution)/shard_map/ppermute | solution.py:351
  432.9 21.7 %attend_back.3 = (bf16[256,1024]{1,0:T(8,128)(2,1)S(1)}, f32[128,1024]{1,0:T(8,128)S(1)}, f32[128,1024]{1,0:T(8,128)S(1)}, f32[2,10,256]{2,1,0:T(8,128)S(1)}) custom-call(s32[1]{0:T(128)} %constant.180.clone.1.row_ref, f32[2,8,256]{2,1,0:T(8,128)S(1)} %pad_maximum_fusion.16.x_ref, bf16[256,1024]{1,0:T(8,128)(2,1)S(1)} %copy-done.9, ...), custom_call_target="tpu_custom_call" | custom-call | bytes 75497472 | tf_op jit(solution)/shard_map/attend_back/pallas_call | solution.py:209
  481.0 17.9 %collective-permute-done.19 = f32[1024,256]{1,0:T(8,128)S(1)} collective-permute-done((f32[1024,256]{1,0:T(8,128)S(1)}, f32[1024,256]{1,0:T(8,128)S(1)}, u32[]{:S(2)}, u32[]{:S(2)}) %collective-permute-start.19) | collective-permute-done | bytes 1048608 | tf_op jit(solution)/shard_map/ppermute | solution.py:332
  540.5 37.4 %collective-permute-start.43 = (f32[3,88,1024]{2,1,0:T(8,128)}, f32[3,88,1024]{2,1,0:T(8,128)}, u32[]{:S(2)}, u32[]{:S(2)}) collective-permute-start(f32[3,88,1024]{2,1,0:T(8,128)} %slice_add_fusion), channel_id=1, source_target_pairs={{0,2},{1,3},{2,0},{3,1},{4,6},{5,7},{6,4},{7,5},{8,10},{9,11},{10,... | collective-permute-start | bytes 3244040 | tf_op jit(solution)/shard_map/ppermute | solution.py:647
  580.5 20.7 %collective-permute-done.22 = f32[512,256]{1,0:T(8,128)} collective-permute-done((f32[512,256]{1,0:T(8,128)}, f32[512,256]{1,0:T(8,128)}, u32[]{:S(2)}, u32[]{:S(2)}) %collective-permute-start.22) | collective-permute-done | bytes 524320 | tf_op jit(solution)/shard_map/ppermute | solution.py:351
  626.7 18.2 %collective-permute-done.30 = f32[256,1024]{1,0:T(8,128)S(1)} collective-permute-done((f32[256,1024]{1,0:T(8,128)}, f32[256,1024]{1,0:T(8,128)S(1)}, u32[]{:S(2)}, u32[]{:S(2)}) %collective-permute-start.30) | collective-permute-done | bytes 1048608 | tf_op jit(solution)/shard_map/ppermute | solution.py:311
  657.2 8.7 %collective-permute-done.37 = f32[128,1152]{0,1:T(8,128)S(1)} collective-permute-done((f32[128,1152]{0,1:T(8,128)S(1)}, f32[128,1152]{0,1:T(8,128)S(1)}, u32[]{:S(2)}, u32[]{:S(2)}) %collective-permute-start.37) | collective-permute-done | bytes 589856 | tf_op jit(solution)/shard_map/ppermute | solution.py:332
  670.6 7.7 collective-permute-done.38
  690.9 17.5 %collective-permute-start.39 = (f32[128,1152]{0,1:T(8,128)}, f32[128,1152]{0,1:T(8,128)}, u32[]{:S(2)}, u32[]{:S(2)}) collective-permute-start(f32[128,1152]{0,1:T(8,128)} %get-tuple-element.190), channel_id=1, source_target_pairs={{0,1},{1,2},{2,3},{4,5},{5,6},{6,7},{8,9},{9,10},{10,11},{12,13},{... | collective-permute-start | bytes 1769480 | tf_op jit(solution)/shard_map/ppermute | solution.py:332
  712.7 13.1 %collective-permute-done.36 = f32[1024,256]{1,0:T(8,128)} collective-permute-done((f32[1024,256]{1,0:T(8,128)}, f32[1024,256]{1,0:T(8,128)}, u32[]{:S(2)}, u32[]{:S(2)}) %collective-permute-start.36) | collective-permute-done | bytes 1048608 | tf_op jit(solution)/shard_map/ppermute | solution.py:333
  747.2 21.4 %collective-permute-done.33 = f32[256,1024]{1,0:T(8,128)S(1)} collective-permute-done((f32[256,1024]{1,0:T(8,128)}, f32[256,1024]{1,0:T(8,128)S(1)}, u32[]{:S(2)}, u32[]{:S(2)}) %collective-permute-start.33) | collective-permute-done | bytes 1048608 | tf_op jit(solution)/shard_map/ppermute | solution.py:312
  776.5 10.9 %collective-permute-done.34 = f32[256,1024]{1,0:T(8,128)S(1)} collective-permute-done((f32[256,1024]{1,0:T(8,128)S(1)}, f32[256,1024]{1,0:T(8,128)S(1)}, u32[]{:S(2)}, u32[]{:S(2)}) %collective-permute-start.34) | collective-permute-done | bytes 1048608 | tf_op jit(solution)/shard_map/ppermute | solution.py:312
  790.9 7.4 slice_bitcast_fusion
  (551 shorter events, 395.8 us)
Async XLA Ops:
  7.2 133.6 %all-gather.6.cloned.1.call-start = ((), (), s32[]{:S(2)}) async-start(), calls=%async_computation.2 | async-start | bytes 14155776 | tf_op jit(solution)/shard_map/all_gather | solution.py:480
  18.6 36.9 %collective-permute-start.1 = (f32[256,512]{1,0:T(8,128)}, f32[256,512]{1,0:T(8,128)}, u32[]{:S(2)}, u32[]{:S(2)}) collective-permute-start(f32[256,512]{1,0:T(8,128)} %constant_dynamic-update-slice_fusion.2), channel_id=1, source_target_pairs={{2,0},{3,1},{0,2},{1,3},{6,4},{7,5},{4,6},{5,7},{10,8},{11,9},{8,1... | collective-permute-start | bytes 1572872 | tf_op jit(solution)/shard_map/ppermute | solution.py:351
  21.2 34.3 %collective-permute-start = (f32[256,512]{1,0:T(8,128)}, f32[256,512]{1,0:T(8,128)}, u32[]{:S(2)}, u32[]{:S(2)}) collective-permute-start(f32[256,512]{1,0:T(8,128)} %constant_dynamic-update-slice_fusion.2), channel_id=1, source_target_pairs={{1,0},{2,1},{3,2},{0,3},{5,4},{6,5},{7,6},{4,7},{9,8},{10,9},{11,1... | collective-permute-start | bytes 1572872 | tf_op jit(solution)/shard_map/ppermute | solution.py:351
  58.2 163.8 %all-gather.8.cloned.1.call-start = ((), (), s32[]{:S(2)}) async-start(), calls=%async_computation.3 | async-start | bytes 9732096 | tf_op jit(solution)/shard_map/all_gather | solution.py:494
  111.3 46.5 %collective-permute-start.6 = (f32[3,88,1024]{2,1,0:T(8,128)}, f32[3,88,1024]{2,1,0:T(8,128)}, u32[]{:S(2)}, u32[]{:S(2)}) collective-permute-start(f32[3,88,1024]{2,1,0:T(8,128)} %add_add_fusion.3), channel_id=1, source_target_pairs={{0,2},{1,3},{2,0},{3,1},{4,6},{5,7},{6,4},{7,5},{8,10},{9,11},{10,... | collective-permute-start | bytes 3244040 | tf_op jit(solution)/shard_map/ppermute | solution.py:493
  160.2 376.4 %reduce-scatter.5.cloned.1.call-start = ((), (), s32[]{:S(2)}) async-start(), calls=%async_computation.7 | async-start | bytes 19464192 | tf_op jit(solution)/shard_map/reduce_scatter | solution.py:542
  240.8 339.8 %all-gather.10.cloned.1.call-start = ((), (), s32[]{:S(2)}) async-start(), calls=%async_computation.4 | async-start | bytes 7077888 | tf_op jit(solution)/shard_map/all_gather | solution.py:512
  267.1 383.8 %reduce-scatter.3.cloned.1.call-start = ((), (), s32[]{:S(2)}) async-start(), calls=%async_computation.5 | async-start | bytes 21823488 | tf_op jit(solution)/shard_map/reduce_scatter | solution.py:630
  312.1 63.7 %collective-permute-start.9 = (f32[256,1024]{1,0:T(8,128)}, f32[256,1024]{1,0:T(8,128)}, u32[]{:S(2)}, u32[]{:S(2)}) collective-permute-start(f32[256,1024]{1,0:T(8,128)} %fusion.12), channel_id=1, source_target_pairs={{0,1},{1,0},{2,3},{3,2},{4,5},{5,4},{6,7},{7,6},{8,9},{9,8},{10,11... | collective-permute-start | bytes 3145736 | tf_op jit(solution)/shard_map/ppermute | solution.py:543
  380.4 48.6 %collective-permute-start.11 = (f32[256,1024]{1,0:T(8,128)}, f32[256,1024]{1,0:T(8,128)}, u32[]{:S(2)}, u32[]{:S(2)}) collective-permute-start(f32[256,1024]{1,0:T(8,128)} %fusion.22), channel_id=1, source_target_pairs={{0,1},{1,2},{2,3},{4,5},{5,6},{6,7},{8,9},{9,10},{10,11},{12,13},{... | collective-permute-start | bytes 3145736 | tf_op jit(solution)/shard_map/ppermute | solution.py:311
  384.8 46.2 %collective-permute-start.10 = (f32[256,1024]{1,0:T(8,128)}, f32[256,1024]{1,0:T(8,128)}, u32[]{:S(2)}, u32[]{:S(2)}) collective-permute-start(f32[256,1024]{1,0:T(8,128)} %fusion.22), channel_id=1, source_target_pairs={{1,0},{2,1},{3,2},{5,4},{6,5},{7,6},{9,8},{10,9},{11,10},{13,12},{... | collective-permute-start | bytes 3145736 | tf_op jit(solution)/shard_map/ppermute | solution.py:312
  391.5 36.8 %collective-permute-start.17 = (f32[256,256]{0,1:T(8,128)S(1)}, f32[256,256]{0,1:T(8,128)S(1)}, u32[]{:S(2)}, u32[]{:S(2)}) collective-permute-start(f32[256,256]{0,1:T(8,128)S(1)} %get-tuple-element.184), channel_id=1, source_target_pairs={{2,0},{3,1},{0,2},{1,3},{6,4},{7,5},{4,6},{5,7},{10,8},{11,9},{8,1... | collective-permute-start | bytes 786440 | tf_op jit(solution)/shard_map/ppermute | solution.py:351
  391.5 36.8 %collective-permute-start.16 = (f32[256,256]{0,1:T(8,128)S(1)}, f32[256,256]{0,1:T(8,128)S(1)}, u32[]{:S(2)}, u32[]{:S(2)}) collective-permute-start(f32[256,256]{0,1:T(8,128)S(1)} %get-tuple-element.185), channel_id=1, source_target_pairs={{1,0},{2,1},{3,2},{0,3},{5,4},{6,5},{7,6},{4,7},{9,8},{10,9},{11,1... | collective-permute-start | bytes 786440 | tf_op jit(solution)/shard_map/ppermute | solution.py:351
  466.0 324.9 %all-gather.14.cloned.1.call-start = ((), (), s32[]{:S(2)}) async-start(), calls=%async_computation.8 | async-start | bytes 9732096 | tf_op jit(solution)/shard_map/all_gather | solution.py:648
  478.0 34.5 %collective-permute-start.12 = (f32[256,1024]{1,0:T(8,128)}, f32[256,1024]{1,0:T(8,128)}, u32[]{:S(2)}, u32[]{:S(2)}) collective-permute-start(f32[256,1024]{1,0:T(8,128)} %collective-permute-done.11), channel_id=1, source_target_pairs={{1,2},{2,3},{5,6},{6,7},{9,10},{10,11},{13,14},{14,15},{17,18},{18... | collective-permute-start | bytes 3145736 | tf_op jit(solution)/shard_map/ppermute | solution.py:311
  479.7 34.7 %collective-permute-start.14 = (f32[256,1024]{1,0:T(8,128)}, f32[256,1024]{1,0:T(8,128)}, u32[]{:S(2)}, u32[]{:S(2)}) collective-permute-start(f32[256,1024]{1,0:T(8,128)} %collective-permute-done.10), channel_id=1, source_target_pairs={{1,0},{2,1},{5,4},{6,5},{9,8},{10,9},{13,12},{14,13},{17,16},{18,1... | collective-permute-start | bytes 3145736 | tf_op jit(solution)/shard_map/ppermute | solution.py:312
  518.9 61.6 %collective-permute-start.23 = (f32[512,256]{1,0:T(8,128)}, f32[512,256]{1,0:T(8,128)}, u32[]{:S(2)}, u32[]{:S(2)}) collective-permute-start(f32[512,256]{1,0:T(8,128)} %get-tuple-element.160), channel_id=1, source_target_pairs={{3,0},{0,1},{1,2},{2,3},{7,4},{4,5},{5,6},{6,7},{11,8},{8,9},{9,10... | collective-permute-start | bytes 1572872 | tf_op jit(solution)/shard_map/ppermute | solution.py:351
  521.0 80.3 %collective-permute-start.22 = (f32[512,256]{1,0:T(8,128)}, f32[512,256]{1,0:T(8,128)}, u32[]{:S(2)}, u32[]{:S(2)}) collective-permute-start(f32[512,256]{1,0:T(8,128)} %get-tuple-element.161), channel_id=1, source_target_pairs={{2,0},{3,1},{0,2},{1,3},{6,4},{7,5},{4,6},{5,7},{10,8},{11,9},{8,1... | collective-permute-start | bytes 1572872 | tf_op jit(solution)/shard_map/ppermute | solution.py:351
  533.6 73.5 %collective-permute-start.13 = (f32[256,1024]{1,0:T(8,128)}, f32[256,1024]{1,0:T(8,128)}, u32[]{:S(2)}, u32[]{:S(2)}) collective-permute-start(f32[256,1024]{1,0:T(8,128)} %collective-permute-done.12), channel_id=1, source_target_pairs={{2,3},{6,7},{10,11},{14,15},{18,19},{22,23},{26,27},{30,31}} | collective-permute-start | bytes 3145736 | tf_op jit(solution)/shard_map/ppermute | solution.py:311
  535.3 73.6 %collective-permute-start.15 = (f32[256,1024]{1,0:T(8,128)}, f32[256,1024]{1,0:T(8,128)}, u32[]{:S(2)}, u32[]{:S(2)}) collective-permute-start(f32[256,1024]{1,0:T(8,128)} %collective-permute-done.14), channel_id=1, source_target_pairs={{1,0},{5,4},{9,8},{13,12},{17,16},{21,20},{25,24},{29,28}} | collective-permute-start | bytes 3145736 | tf_op jit(solution)/shard_map/ppermute | solution.py:312
  540.5 80.4 %collective-permute-start.43 = (f32[3,88,1024]{2,1,0:T(8,128)}, f32[3,88,1024]{2,1,0:T(8,128)}, u32[]{:S(2)}, u32[]{:S(2)}) collective-permute-start(f32[3,88,1024]{2,1,0:T(8,128)} %slice_add_fusion), channel_id=1, source_target_pairs={{0,2},{1,3},{2,0},{3,1},{4,6},{5,7},{6,4},{7,5},{8,10},{9,11},{10,... | collective-permute-start | bytes 3244040 | tf_op jit(solution)/shard_map/ppermute | solution.py:647
  623.7 174.6 %all-gather.12.cloned.1.call-start = ((), (), s32[]{:S(2)}) async-start(), calls=%async_computation.6 | async-start | bytes 7667712 | tf_op jit(solution)/shard_map/all_gather | solution.py:649
  689.6 36.1 %collective-permute-start.36 = (f32[1024,256]{1,0:T(8,128)}, f32[1024,256]{1,0:T(8,128)}, u32[]{:S(2)}, u32[]{:S(2)}) collective-permute-start(f32[1024,256]{1,0:T(8,128)} %add.727), channel_id=1, source_target_pairs={{1,0},{2,1},{3,2},{5,4},{6,5},{7,6},{9,8},{10,9},{11,10},{13,12},{... | collective-permute-start | bytes 3145736 | tf_op jit(solution)/shard_map/ppermute | solution.py:333
  690.9 36.7 %collective-permute-start.39 = (f32[128,1152]{0,1:T(8,128)}, f32[128,1152]{0,1:T(8,128)}, u32[]{:S(2)}, u32[]{:S(2)}) collective-permute-start(f32[128,1152]{0,1:T(8,128)} %get-tuple-element.190), channel_id=1, source_target_pairs={{0,1},{1,2},{2,3},{4,5},{5,6},{6,7},{8,9},{9,10},{10,11},{12,13},{... | collective-permute-start | bytes 1769480 | tf_op jit(solution)/shard_map/ppermute | solution.py:332
  (140 other events, 1690.6 us)
Sparse Core Ops, SparseCore 0:
  58.3 82.4 all-gather.5
  160.3 55.4 all-gather.7
  240.9 118.5 reduce-scatter.4
  361.5 45.4 all-gather.9
  466.2 129.6 reduce-scatter.2
  623.8 52.7 all-gather.13
  734.5 54.8 all-gather.11

commit v3 on v2

--- a/solution.py
+++ b/solution.py
@@ -104,7 +104,7 @@
 
 
 def bwd_kernel(causal, row_ref, x_ref, q_ref, k_ref, v_ref, d_ref, l_ref,
-               dq_ref, dk_ref, dv_ref, t_ref, band, keys, values, p_ref, g_ref, near):
+               dq_ref, dkv_ref, t_ref, band, keys, values, p_ref, g_ref, near, dk_ref, dv_ref):
     r = pl.program_id(1)
     block = r + row_ref[0]
     total_chunks = k_ref.shape[1] // QB
@@ -150,6 +150,8 @@
 
     @pl.when(r == pl.num_programs(1) - 1)
     def _():
+        dkv_ref[0, 0, 0] = dk_ref[...].astype(jnp.bfloat16)
+        dkv_ref[0, 1, 0] = dv_ref[...].astype(jnp.bfloat16)
         for h in range(2):
             def piece(n, side):
                 return near[h, n * 128:(n + 1) * 128, side * 128:(side + 1) * 128]
@@ -179,7 +181,6 @@
         q=pl.BlockSpec((2 * DH, QB), lambda g, r: (g, r)),
         k=pl.BlockSpec((DH, keys), lambda g, r: (4 * (g // 2) + g % 2, 0)),
         v=pl.BlockSpec((DH, keys), lambda g, r: (4 * (g // 2) + g % 2 + 2, 0)),
-        dk=pl.BlockSpec((DH, keys), lambda g, r: (g, 0)),
         l=pl.BlockSpec((1, 2, QB), lambda g, r: (g, 0, r)),
         t=pl.BlockSpec((1, 10, 256), lambda g, r: (g, 0, 0)),
     )
@@ -206,23 +207,24 @@
 def attend_back(row, x, q, kv, d, logs, causal):
     groups, keys, rows = kv.shape[0] // (2 * DH), kv.shape[1], q.shape[1]
     s = specs(rows, keys)
-    return pl.pallas_call(
+    dq, dkv, lines = pl.pallas_call(
         functools.partial(bwd_kernel, causal),
-        out_shape=(jax.ShapeDtypeStruct(q.shape, jnp.bfloat16),
-                   jax.ShapeDtypeStruct((groups * DH, keys), jnp.float32),
-                   jax.ShapeDtypeStruct((groups * DH, keys), jnp.float32),
-                   jax.ShapeDtypeStruct((groups, 10, 256), jnp.float32)),
+        out_shape=[jax.ShapeDtypeStruct(q.shape, jnp.bfloat16),
+                   jax.ShapeDtypeStruct((groups // 2, 2, 2, DH, keys), jnp.bfloat16),
+                   jax.ShapeDtypeStruct((groups, 10, 256), jnp.float32)],
         grid=(groups, rows // QB),
         in_specs=[s["smem"], s["x"], s["q"], s["k"], s["v"], s["q"], s["l"]],
-        out_specs=(s["q"], s["dk"], s["dk"], s["t"]),
+        out_specs=[s["q"], pl.BlockSpec((1, 2, 1, DH, keys), lambda g, r: (g // 2, 0, g % 2, 0, 0)), s["t"]],
         scratch_shapes=[pltpu.VMEM((2, 10 * 128, 256), jnp.float32), pltpu.VMEM((keys, DH), jnp.bfloat16),
                         pltpu.VMEM((keys, DH), jnp.bfloat16),
                         pltpu.VMEM((keys, QB), jnp.float32), pltpu.VMEM((keys, QB), jnp.float32),
-                        pltpu.VMEM((2, 10 * 128, 256), jnp.float32)],
+                        pltpu.VMEM((2, 10 * 128, 256), jnp.float32),
+                        pltpu.VMEM((DH, keys), jnp.float32), pltpu.VMEM((DH, keys), jnp.float32)],
         compiler_params=pltpu.CompilerParams(dimension_semantics=("arbitrary", "arbitrary"), vmem_limit_bytes=32 << 20),
         cost_estimate=cost(2 * groups * rows * keys, 18),
         name="attend_back",
     )(row, x, q, kv, kv, d, logs)
+    return dq, dkv.reshape(kv.shape), lines
 
 
 MAXDIST = 128
@@ -480,10 +482,12 @@
     shares = lax.all_gather(tie(jnp.stack(units), mixed), "batch")
     mixed = tie(mixed.astype(jnp.float32), *units)
     rider = own_cross_x.reshape(-1, rows)
+    own_self = jnp.concatenate([self_query, self_kv], axis=1)
     got = exchange([jnp.concatenate([block_of(mixed, (z + d) % n, rows, 1), rider]) for d in range(n)], n)
     others = got[1:]
     mixed_self = settle(jnp.concatenate([x[:ocols] for x in got])).astype(low)
-    cross_x = jnp.concatenate([x[ocols:] for x in got]).reshape(-1, 8, rows)
+    ridden = ocols + rider.shape[0]
+    cross_x = jnp.concatenate([x[ocols:ridden] for x in got]).reshape(-1, 8, rows)
     own_in = jnp.concatenate([cross_query, cross_kv], axis=1)
     whole_so, whole_co, whole_cq, whole_kv = whole_weights(
         shares, own_in, self_output, cross_output, [mixed_self, cross_x.reshape(-1, rows)]
@@ -493,7 +497,7 @@
     fetched = lax.ppermute(tie(sent, *others), "kv", far_pairs)
     sent = lax.all_gather(tie(fetched, whole_so), "batch", axis=1, tiled=True)
 
-    in_rows = block_of(flat_in, z, rows)
+    in_rows = block_of(inputs.reshape(seq_len, width), z, rows).astype(jnp.float32)
     after_self = in_rows + mm(mixed_self, whole_so, TN)
 
     def into(w, x):
@@ -506,11 +510,6 @@
     place = z.reshape(1).astype(jnp.int32) * (rows // QB)
     mixed_cross, cross_log = attend(place, cross_x, cq, ckv, False)
     after_cross = after_self + mm(mixed_cross, whole_co, TN)
-
-    own_self = jnp.concatenate([self_query, self_kv], axis=1)
-    unit = tie(jnp.concatenate([share(self_query), share(self_kv)], axis=1), fetched)
-    rest_self = lax.all_gather(tie(jnp.stack(exchange([unit] * n, n)[1:]), after_cross), "batch", axis=1, tiled=True)
-    rest_self = settle(rest_self).astype(low)
 
     ffn_in = norm_rows(after_cross, gain_three).astype(low)
     other = settle(lax.ppermute(ffn_in.astype(jnp.float32), "kv", near_pairs)).astype(low)
@@ -546,19 +545,16 @@
     cross_out_grad = own_grad.astype(jnp.float32) + norm_grad
     branch_cross = cross_out_grad.astype(low)
     mixed_grad = mm(whole_co, branch_cross, NT).astype(low)
-    cq_grad, ck_grad, cv_grad, cross_lines = attend_back(
+    cq_grad, ckv_grad, cross_lines = attend_back(
         place, cross_x, cq, ckv, mixed_grad, cross_log, False
     )
-    result = (tie(after_cross, cq_grad) + ffn_out).astype(low).astype(jnp.float32)
-    line = Gather(result, n)
-    first = line.hop(tie)
     cross_in_grad = lax.dot_general(
         cq_grad.reshape(n, qcols, rows), whole_cq, (((0, 1), (0, 2)), ((), ())), preferred_element_type=jnp.float32
     )
     norm_grad, grad_gain_cross = jax.vjp(norm_rows, after_self, gain_two)[1](cross_in_grad)
     self_out_grad = cross_out_grad + norm_grad
     branch_self = self_out_grad.astype(low)
-    mixed_grad = tie(mm(whole_so, branch_self, NT).astype(low).astype(jnp.float32), result)
+    mixed_grad = tie(mm(whole_so, branch_self, NT).astype(low).astype(jnp.float32), ffn_out)
     got = exchange([mixed_grad[d * ocols:(d + 1) * ocols] for d in range(n)], n)
     arrived = got[1:]
     stacked = jnp.stack(got)
@@ -566,43 +562,41 @@
         jnp.concatenate(
             [lax.dynamic_index_in_dim(stacked, (j - z + n) % n, 0, keepdims=False) for j in range(n)], axis=1
         ),
-        *first,
     )
     mixed_grad = settle(mixed_grad).astype(low)
-    ckv_grad = jnp.concatenate(
-        [ck_grad.reshape(n, kcols, -1), cv_grad.reshape(n, kcols, -1)], axis=1
-    ).astype(low)
-    memory_part = [
-        lax.dot_general(ckv_grad, block_of(whole_kv, (z + d) % n, width // n, 1),
-                        (((0, 1), (0, 2)), ((), ())), preferred_element_type=jnp.float32)
-        for d in range(n)
-    ]
-
-    sq_grad, sk_grad, sv_grad, self_lines = attend_back(zero, self_x, sq, skv, mixed_grad, self_log, True)
-    skv_grad = jnp.concatenate([sk_grad, sv_grad]).astype(low)
-    memory_line = Scatter(memory_part, n)
-    second, memory_one = line.hop(tie), memory_line.hop(tie)
+    memory_part = lax.dot_general(
+        ckv_grad.reshape(n, 2 * kcols, -1), whole_kv, (((0, 1), (0, 2)), ((), ())), preferred_element_type=jnp.float32
+    )
+    memory_grad = lax.psum_scatter(tie(memory_part, *arrived), "kv", scatter_dimension=1, tiled=True)
+
+    arriving = exchange([tie(share(own_self), fetched, after_cross)] * n, n)[1:]
+    rest_self = tie(jnp.stack(arriving), cq_grad, ffn_sums)
+    rest_self = settle(lax.all_gather(rest_self, "batch", axis=1, tiled=True)).astype(low)
+
+    sq_grad, skv_grad, self_lines = attend_back(zero, self_x, sq, skv, mixed_grad, self_log, True)
     turned = jnp.concatenate([sq_grad, skv_grad]).astype(jnp.float32)
-    got = exchange([tie(block_of(turned, (z + d) % n, rows, 1), *second, *memory_one) for d in range(n)], n)
+    got = exchange([block_of(turned, (z + d) % n, rows, 1) for d in range(n)], n)
     rest = settle(jnp.stack(got[1:])).astype(low)
     attn_in_grad = mm(got[0].astype(low), own_self, T0) + lax.dot_general(
         rest, rest_self, (((0, 1), (0, 2)), ((), ())), preferred_element_type=jnp.float32
     )
     early = got[1:]
-    third, memory_two = line.hop(tie), memory_line.hop(tie)
     attn_term = mm(sq_grad, self_query, T0) + mm(skv_grad, self_kv, T0)
     norm_grad, _ = jax.vjp(norm_rows, in_rows, gain_one)[1](attn_in_grad)
-    last = tie(self_out_grad + norm_grad, *third, *memory_two)
+    last = self_out_grad + norm_grad
     _, grad_gain_self = jax.vjp(norm_rows, flat_in, gain_one)[1](attn_term)
 
+    result = (tie(after_cross, *early) + ffn_out).astype(low).astype(jnp.float32)
+    line = Gather(result, n)
     ends_line = Gather(last, n)
     one_hop = ends_line.hop(tie)
-    memory_three = memory_line.hop(tie)
     two_hops = ends_line.hop(tie)
-    ends_line.hop(tie)
+    three_hops = ends_line.hop(tie)
+    line.hop(tie)
+    lo_two = line.hop(tie)
+    line.hop(tie)
     layer_out = settle(in_order(line.blocks(), z, n)).astype(low)
     input_grad = in_order(ends_line.blocks(), z, n)
-    memory_grad = memory_line.total()
 
     self_tab = table_gradient(self_lines, False, buckets)
     cross_tab = table_gradient(cross_lines, True, buckets)
@@ -614,12 +608,12 @@
             tabs, cross_tab[:, d * heads:(d + 1) * heads].reshape(1, 1, -1), (1, spots[d], 0)
         )
     small = jnp.stack([grad_gain_self, grad_gain_cross, grad_gain_ffn, jnp.pad(tabs.reshape(-1), (0, width - tabs.size))], axis=1)
-    small = jnp.pad(small, ((0, 0), (0, 124)))
+    small = jnp.pad(tie(small, *early), ((0, 0), (0, 124)))
     sums = jnp.concatenate(
         [
             mm(branch_cross, mixed_cross, T0),
             mm(cross_in, cq_grad, T0),
-            mm(flat_mem, ckv_grad.reshape(-1, flat_mem.shape[0]), T0),
+            mm(flat_mem, ckv_grad, T0),
             mm(branch_self, mixed_self, T0),
             mm(attn_in, sq_grad, T0),
             mm(attn_in, skv_grad, T0),
@@ -629,24 +623,18 @@
     )
     sums = lax.psum_scatter(sums, "batch", tiled=True)
     self_sums, small = sums[:, 4 * width:-128], sums[:, -128:]
-    attn_line = Scatter(
-        [
-            jnp.concatenate(
-                [sums[:, at * width + d * size:at * width + (d + 1) * size]
-                 for at, size in enumerate((ocols, qcols, 2 * kcols, ocols))] + [small],
-                axis=1,
-            )
-            for d in range(n)
-        ],
-        n,
-    )
-    attn_line.hop(tie, *one_hop)
-    attn_line.hop(tie)
-    attn_line.hop(tie)
-    attn_sums = attn_line.total()
-    ffn_sums = ffn_sums[:3] + lax.ppermute(tie(ffn_sums[3:], sq_grad), "kv", far_pairs)
-    ffn_sums = lax.all_gather(tie(ffn_sums, last), "batch", axis=1, tiled=True)
-    attn_sums = lax.all_gather(tie(jnp.concatenate([attn_sums, self_sums], axis=1), *memory_three), "batch", tiled=True)
+    parts = [
+        jnp.concatenate(
+            [sums[:, at * width + d * size:at * width + (d + 1) * size]
+             for at, size in enumerate((ocols, qcols, 2 * kcols, ocols))] + [small],
+            axis=1,
+        )
+        for d in range(n)
+    ]
+    attn_sums = sum(exchange([tie(x, *three_hops) for x in parts], n))
+    ffn_sums = ffn_sums[:3] + lax.ppermute(tie(ffn_sums[3:], *arrived), "kv", far_pairs)
+    ffn_sums = lax.all_gather(tie(ffn_sums, last, memory_grad), "batch", axis=1, tiled=True)
+    attn_sums = lax.all_gather(tie(jnp.concatenate([attn_sums, self_sums], axis=1), *lo_two), "batch", tiled=True)
 
     def columns(x, sizes):
         at = 0

time: 836 us -> 806 us (0.964)
  starting transfers between devices: 148 us -> 101 us
  waiting for transfers between devices: 273 us -> 311 us
  matrix products: 104 us -> 90.7 us
  other arithmetic: 72.4 us -> 61.4 us
    ppermute x13 -> x1, starting transfers between devices: 85.3 us -> 5.12 us  [on_device(): lax.ppermute(tie(ffn_sums[3:], *arrived), 'kv', far_pairs)]
    ppermute x6, waiting for transfers between devices: 34.3 us -> 95.1 us  [hop(): lax.ppermute(tie(self.left, *others), 'kv', [(i + 1, i) for i in range(n...]
    ppermute x13 -> x1, waiting for transfers between devices: 64.5 us -> 17.3 us  [on_device(): lax.ppermute(tie(ffn_sums[3:], *arrived), 'kv', far_pairs)]
    ppermute x15 -> x18, starting transfers between devices: 33.8 us -> 62.6 us  [exchange(): lax.ppermute(blocks[n - d], 'kv', [((i + d) % n, i) for i in range(n)])]
    reduce_scatter x1, waiting for transfers between devices: 0.02 us -> 26.9 us  [on_device(): sums = lax.psum_scatter(sums, 'batch', tiled=True)]
    ppermute x6, waiting for transfers between devices: 18.2 us -> 0.3 us  [hop(): lax.ppermute(tie(self.right, *others), 'kv', [(i, i + 1) for i in range(d...]
    all_gather x3, waiting for transfers between devices: 0.01 us -> 17.6 us  [the longest x1 17.6 us: on_device(): lax.all_gather(rest_self, 'batch', axis=1, tiled=True)]
    unnamed x241 -> x258, local copies, waits for them, and re-layouts: 42 us -> 46.8 us
  transfers between devices with their start and end apart: 51 -> 43, of which waited for: 23 -> 24; matrix products, arithmetic and copies ran while one was open for 26% -> 24% of each run, Pallas kernels for 10% -> 10%
where the time goes in v3:
time: 806 us; the launch traced here: 794 us
  waiting for transfers between devices  311 us (39%)
  local copies, waits for them, and re-layouts  116 us (14%)
  starting transfers between devices  101 us (13%)
  matrix products  90.7 us (11%)
  Pallas kernels  79.3 us (10%)
  other arithmetic  61.4 us (8%)
  between operations  34.2 us (4%)
    ppermute x6, waiting for transfers between devices, hop(): lax.ppermute(tie(self.left, *others), 'kv', [(i + 1, i) for i in range(n...  95.1 us
    ppermute x18, waiting for transfers between devices, exchange(): lax.ppermute(blocks[n - d], 'kv', [((i + d) % n, i) for i in range(n)])  90 us
    dot_general x45, matrix products, mm(): lax.dot_general(a, b, (dims, ((), ())), preferred_element_type=jnp.float32)  71.9 us
    ppermute x18, starting transfers between devices, exchange(): lax.ppermute(blocks[n - d], 'kv', [((i + d) % n, i) for i in range(n)])  62.6 us
    unnamed x258, local copies, waits for them, and re-layouts  46.8 us
    pallas_call x2, Pallas kernels, attend_back(): pl.pallas_call(functools.partial(bwd_kernel, causal), out_shape=[jax.Shap...  43 us
    pallas_call x2, Pallas kernels, attend(): pl.pallas_call(functools.partial(fwd_kernel, causal), out_shape=(jax.Shap...  29.1 us
    reduce_scatter x1, waiting for transfers between devices, on_device(): sums = lax.psum_scatter(sums, 'batch', tiled=True)  26.9 us
  transfers between devices with their start and end apart: 43, of which 24 were waited for; matrix products, arithmetic and copies ran while one was open for 24% of the time, Pallas kernels for 10%

profile of v3, /device:TPU:0, one launch (start us, length us, event | category | flops | bytes accessed | tf_op | source)
XLA Modules:
  0.0 794.1 jit_solution(15101398188045510310)
XLA Ops:
  28.4 16.6 %attend.2 = (bf16[256,1024]{1,0:T(8,128)(2,1)S(1)}, f32[2,2,1024]{2,1,0:T(2,128)S(1)}) custom-call(s32[1]{0:T(128)} %constant.172.clone.1.row_ref, f32[2,8,256]{2,1,0:T(8,128)S(1)} %pad_maximum_fusion.12.x_ref, bf16[256,1024]{1,0:T(8,128)(2,1)S(1)} %fusion.36.q_ref, bf16[256,1024]{1,0:T(8,128)(2,1)S(1)} %convolution_convert_fusion.3.k_ref.v_ref, ...), custom_call_target="tpu_custom_call" | custom-call | bytes 46137344 | tf_op jit(solution)/shard_map/attend/pallas_call | solution.py:192
  64.4 11.7 %collective-permute-start.5 = (f32[272,256]{1,0:T(8,128)}, f32[272,256]{1,0:T(8,128)}, u32[]{:S(2)}, u32[]{:S(2)}) collective-permute-start(f32[272,256]{1,0:T(8,128)} %get-tuple-element.196), channel_id=1, source_target_pairs={{3,0},{0,1},{1,2},{2,3},{7,4},{4,5},{5,6},{6,7},{11,8},{8,9},{9,10... | collective-permute-start | bytes 835592 | tf_op jit(solution)/shard_map/ppermute | solution.py:353
  87.0 8.3 %collective-permute-done.4 = f32[272,256]{1,0:T(8,128)} collective-permute-done((f32[272,256]{1,0:T(8,128)}, f32[272,256]{1,0:T(8,128)}, u32[]{:S(2)}, u32[]{:S(2)}) %collective-permute-start.4) | collective-permute-done | bytes 278560 | tf_op jit(solution)/shard_map/ppermute | solution.py:353
  112.4 25.4 %all-gather.6.cloned.1.call-done.shares_ref = f32[8,3,256,512]{3,2,1,0:T(8,128)} async-done(((f32[1,3,256,512]{3,2,1,0:T(8,128)}), f32[8,3,256,512]{3,2,1,0:T(8,128)}) %all-gather.6.cloned.1.call-update) | async-done | bytes 12582928 | tf_op jit(solution)/shard_map/all_gather | solution.py:482
  141.1 7.2 whole_weights.1
  166.1 12.5 %attend.3 = (bf16[1024,256]{1,0:T(8,128)(2,1)S(1)}, f32[8,2,256]{2,1,0:T(2,128)S(1)}) custom-call(s32[1]{0:T(128)} %bitcast.18.row_ref, f32[8,8,256]{2,1,0:T(8,128)S(1)} %get-tuple-element.188.x_ref, bf16[1024,256]{1,0:T(8,128)(2,1)S(1)} %bitcast.303, bf16[1024,1024]{1,0:T(8,128)(2,1)S(1)} %bitcast.295, bf16[1024,1024]{1,0:T(8,128)(2,1)S(1)} %bitcast.296), custom_call_target="tpu_custom_call" | custom-call | bytes 46137344 | tf_op jit(solution)/shard_map/attend/pallas_call | solution.py:192
  184.6 20.6 %collective-permute-done.7 = f32[256,1024]{1,0:T(8,128)S(1)} collective-permute-done((f32[256,1024]{1,0:T(8,128)S(1)}, f32[256,1024]{1,0:T(8,128)S(1)}, u32[]{:S(2)}, u32[]{:S(2)}) %collective-permute-start.7) | collective-permute-done | bytes 1048608 | tf_op jit(solution)/shard_map/ppermute | solution.py:515
  248.2 18.1 %collective-permute-done.8 = f32[256,1024]{1,0:T(8,128)S(1)} collective-permute-done((f32[256,1024]{1,0:T(8,128)S(1)}, f32[256,1024]{1,0:T(8,128)S(1)}, u32[]{:S(2)}, u32[]{:S(2)}) %collective-permute-start.8) | collective-permute-done | bytes 1048608 | tf_op jit(solution)/shard_map/ppermute | solution.py:533
  276.2 21.3 %attend_back.2 = (bf16[1024,256]{1,0:T(8,128)(2,1)S(1)}, bf16[4,2,2,64,1024]{4,3,2,1,0:T(8,128)(2,1)S(1)}, f32[8,10,256]{2,1,0:T(8,128)S(1)}) custom-call(s32[1]{0:T(128)} %bitcast.18.row_ref, f32[8,8,256]{2,1,0:T(8,128)S(1)} %get-tuple-element.188.x_ref, bf16[1024,256]{1,0:T(8,128)(2,1)S(1)} %bitcast.304, bf16[1024,1024]{1,0:T(8,128)(2,1)S(1)} %bitcast.297, ...), custom_call_target="tpu_custom_call" | custom-call | bytes 75497472 | tf_op jit(solution)/shard_map/attend_back/pallas_call | solution.py:210
  358.1 11.1 %collective-permute-done.23 = f32[128,512]{1,0:T(8,128)} collective-permute-done((f32[128,512]{1,0:T(8,128)}, f32[128,512]{1,0:T(8,128)}, u32[]{:S(2)}, u32[]{:S(2)}) %collective-permute-start.23) | collective-permute-done | bytes 262176 | tf_op jit(solution)/shard_map/ppermute | solution.py:353
  398.1 21.7 %attend_back.3 = (bf16[256,1024]{1,0:T(8,128)(2,1)S(1)}, bf16[1,2,2,64,1024]{4,3,2,1,0:T(8,128)(2,1)S(1)}, f32[2,10,256]{2,1,0:T(8,128)S(1)}) custom-call(s32[1]{0:T(128)} %constant.172.clone.1.row_ref, f32[2,8,256]{2,1,0:T(8,128)S(1)} %pad_maximum_fusion.12.x_ref, bf16[256,1024]{1,0:T(8,128)(2,1)S(1)} %copy-done.10, ...), custom_call_target="tpu_custom_call" | custom-call | bytes 75497472 | tf_op jit(solution)/shard_map/attend_back/pallas_call | solution.py:210
  422.0 21.7 %collective-permute-start.15 = (f32[512,256]{1,0:T(8,128)}, f32[512,256]{1,0:T(8,128)}, u32[]{:S(2)}, u32[]{:S(2)}) collective-permute-start(f32[512,256]{1,0:T(8,128)} %get-tuple-element.156), channel_id=1, source_target_pairs={{3,0},{0,1},{1,2},{2,3},{7,4},{4,5},{5,6},{6,7},{11,8},{8,9},{9,10... | collective-permute-start | bytes 1572872 | tf_op jit(solution)/shard_map/ppermute | solution.py:353
  461.4 10.6 %collective-permute-done.14 = f32[512,256]{1,0:T(8,128)} collective-permute-done((f32[512,256]{1,0:T(8,128)}, f32[512,256]{1,0:T(8,128)}, u32[]{:S(2)}, u32[]{:S(2)}) %collective-permute-start.14) | collective-permute-done | bytes 524320 | tf_op jit(solution)/shard_map/ppermute | solution.py:353
  492.7 17.6 %all-gather.10.cloned.1.call-done = f32[3,1024,512]{2,1,0:T(8,128)} async-done(((f32[3,128,512]{2,1,0:T(8,128)}), f32[3,1024,512]{2,1,0:T(8,128)}) %all-gather.10.cloned.1.call-update) | async-done | bytes 6291472 | tf_op jit(solution)/shard_map/all_gather | solution.py:574
  518.7 17.3 %collective-permute-done.34 = f32[3,88,1024]{2,1,0:T(8,128)} collective-permute-done((f32[3,88,1024]{2,1,0:T(8,128)}, f32[3,88,1024]{2,1,0:T(8,128)}, u32[]{:S(2)}, u32[]{:S(2)}) %collective-permute-start.34) | collective-permute-done | bytes 1081376 | tf_op jit(solution)/shard_map/ppermute | solution.py:635
  553.8 13.7 %collective-permute-done.25 = f32[256,1024]{1,0:T(8,128)S(1)} collective-permute-done((f32[256,1024]{1,0:T(8,128)}, f32[256,1024]{1,0:T(8,128)S(1)}, u32[]{:S(2)}, u32[]{:S(2)}) %collective-permute-start.25) | collective-permute-done | bytes 1048608 | tf_op jit(solution)/shard_map/ppermute | solution.py:314
  570.6 19.4 %collective-permute-done.16 = f32[256,1024]{1,0:T(8,128)} collective-permute-done((f32[256,1024]{1,0:T(8,128)S(1)}, f32[256,1024]{1,0:T(8,128)}, u32[]{:S(2)}, u32[]{:S(2)}) %collective-permute-start.16) | collective-permute-done | bytes 1048608 | tf_op jit(solution)/shard_map/ppermute | solution.py:314
  593.0 19.5 %collective-permute-done.29 = f32[256,1024]{1,0:T(8,128)} collective-permute-done((f32[256,1024]{1,0:T(8,128)S(1)}, f32[256,1024]{1,0:T(8,128)}, u32[]{:S(2)}, u32[]{:S(2)}) %collective-permute-start.29) | collective-permute-done | bytes 1048608 | tf_op jit(solution)/shard_map/ppermute | solution.py:314
  615.4 26.9 %reduce-scatter.8.cloned.1.call-done = f32[128,4736]{0,1:T(8,128)} async-done(((f32[1024,4736]{0,1:T(8,128)}), f32[128,4736]{0,1:T(8,128)}) %reduce-scatter.8.cloned.1.call-update) | async-done | bytes 2424848 | tf_op jit(solution)/shard_map/reduce_scatter | solution.py:624
  646.8 9.2 %collective-permute-done.30 = f32[256,1024]{1,0:T(8,128)} collective-permute-done((f32[256,1024]{1,0:T(8,128)}, f32[256,1024]{1,0:T(8,128)}, u32[]{:S(2)}, u32[]{:S(2)}) %collective-permute-start.30) | collective-permute-done | bytes 1048608 | tf_op jit(solution)/shard_map/ppermute | solution.py:314
  671.6 7.4 collective-permute-done.33
  679.1 23.6 %collective-permute-done.32 = f32[128,1152]{0,1:T(8,128)} collective-permute-done((f32[128,1152]{0,1:T(8,128)}, f32[128,1152]{0,1:T(8,128)}, u32[]{:S(2)}, u32[]{:S(2)}) %collective-permute-start.32) | collective-permute-done | bytes 589856 | tf_op jit(solution)/shard_map/ppermute | solution.py:353
  709.9 33.4 %collective-permute-done.21 = f32[256,1024]{1,0:T(8,128)} collective-permute-done((f32[256,1024]{1,0:T(8,128)}, f32[256,1024]{1,0:T(8,128)}, u32[]{:S(2)}, u32[]{:S(2)}) %collective-permute-start.21) | collective-permute-done | bytes 1048608 | tf_op jit(solution)/shard_map/ppermute | solution.py:314
  758.3 7.4 slice_bitcast_fusion
  (535 shorter events, 357.7 us)
Async XLA Ops:
  7.2 130.6 %all-gather.6.cloned.1.call-start = ((), (), s32[]{:S(2)}) async-start(), calls=%async_computation.3 | async-start | bytes 14155776 | tf_op jit(solution)/shard_map/all_gather | solution.py:482
  15.5 36.9 %collective-permute-start.1 = (f32[256,512]{1,0:T(8,128)}, f32[256,512]{1,0:T(8,128)}, u32[]{:S(2)}, u32[]{:S(2)}) collective-permute-start(f32[256,512]{1,0:T(8,128)} %constant_dynamic-update-slice_fusion.2), channel_id=1, source_target_pairs={{2,0},{3,1},{0,2},{1,3},{6,4},{7,5},{4,6},{5,7},{10,8},{11,9},{8,1... | collective-permute-start | bytes 1572872 | tf_op jit(solution)/shard_map/ppermute | solution.py:353
  55.1 159.5 %all-gather.8.cloned.1.call-start = ((), (), s32[]{:S(2)}) async-start(), calls=%async_computation.4 | async-start | bytes 9732096 | tf_op jit(solution)/shard_map/all_gather | solution.py:498
  101.5 53.3 %collective-permute-start.6 = (f32[3,88,1024]{2,1,0:T(8,128)}, f32[3,88,1024]{2,1,0:T(8,128)}, u32[]{:S(2)}, u32[]{:S(2)}) collective-permute-start(f32[3,88,1024]{2,1,0:T(8,128)} %add_add_fusion.3), channel_id=1, source_target_pairs={{0,2},{1,3},{2,0},{3,1},{4,6},{5,7},{6,4},{7,5},{8,10},{9,11},{10,... | collective-permute-start | bytes 3244040 | tf_op jit(solution)/shard_map/ppermute | solution.py:497
  157.2 196.3 %reduce-scatter.4.cloned.1.call-start = ((), (), s32[]{:S(2)}) async-start(), calls=%async_computation.5 | async-start | bytes 19464192 | tf_op jit(solution)/shard_map/reduce_scatter | solution.py:541
  233.6 257.2 %reduce-scatter.6.cloned.1.call-start = ((), (), s32[]{:S(2)}) async-start(), calls=%async_computation.7 | async-start | bytes 5242880 | tf_op jit(solution)/shard_map/reduce_scatter | solution.py:570
  338.4 171.9 %all-gather.10.cloned.1.call-start = ((), (), s32[]{:S(2)}) async-start(), calls=%async_computation.6 | async-start | bytes 7077888 | tf_op jit(solution)/shard_map/all_gather | solution.py:574
  372.5 269.8 %reduce-scatter.8.cloned.1.call-start = ((), (), s32[]{:S(2)}) async-start(), calls=%async_computation.8 | async-start | bytes 21823488 | tf_op jit(solution)/shard_map/reduce_scatter | solution.py:624
  422.0 37.6 %collective-permute-start.15 = (f32[512,256]{1,0:T(8,128)}, f32[512,256]{1,0:T(8,128)}, u32[]{:S(2)}, u32[]{:S(2)}) collective-permute-start(f32[512,256]{1,0:T(8,128)} %get-tuple-element.156), channel_id=1, source_target_pairs={{3,0},{0,1},{1,2},{2,3},{7,4},{4,5},{5,6},{6,7},{11,8},{8,9},{9,10... | collective-permute-start | bytes 1572872 | tf_op jit(solution)/shard_map/ppermute | solution.py:353
  480.4 277.9 %all-gather.14.cloned.1.call-start = ((), (), s32[]{:S(2)}) async-start(), calls=%async_computation.10 | async-start | bytes 9732096 | tf_op jit(solution)/shard_map/all_gather | solution.py:636
  483.2 52.7 %collective-permute-start.34 = (f32[3,88,1024]{2,1,0:T(8,128)}, f32[3,88,1024]{2,1,0:T(8,128)}, u32[]{:S(2)}, u32[]{:S(2)}) collective-permute-start(f32[3,88,1024]{2,1,0:T(8,128)} %fusion.38), channel_id=1, source_target_pairs={{0,2},{1,3},{2,0},{3,1},{4,6},{5,7},{6,4},{7,5},{8,10},{9,11},{10,... | collective-permute-start | bytes 3244040 | tf_op jit(solution)/shard_map/ppermute | solution.py:635
  539.2 226.5 %all-gather.12.cloned.1.call-start = ((), (), s32[]{:S(2)}) async-start(), calls=%async_computation.9 | async-start | bytes 7667712 | tf_op jit(solution)/shard_map/all_gather | solution.py:637
  546.9 43.1 %collective-permute-start.16 = (f32[256,1024]{1,0:T(8,128)S(1)}, f32[256,1024]{1,0:T(8,128)}, u32[]{:S(2)}, u32[]{:S(2)}) collective-permute-start(f32[256,1024]{1,0:T(8,128)S(1)} %fusion.104), channel_id=1, source_target_pairs={{1,0},{2,1},{3,2},{5,4},{6,5},{7,6},{9,8},{10,9},{11,10},{13,12},{... | collective-permute-start | bytes 3145736 | tf_op jit(solution)/shard_map/ppermute | solution.py:314
  548.2 43.1 %collective-permute-start.17 = (f32[256,1024]{1,0:T(8,128)S(1)}, f32[256,1024]{1,0:T(8,128)}, u32[]{:S(2)}, u32[]{:S(2)}) collective-permute-start(f32[256,1024]{1,0:T(8,128)S(1)} %fusion.104), channel_id=1, source_target_pairs={{0,1},{1,2},{2,3},{4,5},{5,6},{6,7},{8,9},{9,10},{10,11},{12,13},{... | collective-permute-start | bytes 3145736 | tf_op jit(solution)/shard_map/ppermute | solution.py:313
  567.4 45.0 %collective-permute-start.29 = (f32[256,1024]{1,0:T(8,128)S(1)}, f32[256,1024]{1,0:T(8,128)}, u32[]{:S(2)}, u32[]{:S(2)}) collective-permute-start(f32[256,1024]{1,0:T(8,128)S(1)} %collective-permute-done.25), channel_id=1, source_target_pairs={{1,0},{2,1},{5,4},{6,5},{9,8},{10,9},{13,12},{14,13},{17,16},{18,1... | collective-permute-start | bytes 3145736 | tf_op jit(solution)/shard_map/ppermute | solution.py:314
  569.0 44.8 %collective-permute-start.27 = (f32[256,1024]{1,0:T(8,128)S(1)}, f32[256,1024]{1,0:T(8,128)}, u32[]{:S(2)}, u32[]{:S(2)}) collective-permute-start(f32[256,1024]{1,0:T(8,128)S(1)} %collective-permute-done.26), channel_id=1, source_target_pairs={{1,2},{2,3},{5,6},{6,7},{9,10},{10,11},{13,14},{14,15},{17,18},{18... | collective-permute-start | bytes 3145736 | tf_op jit(solution)/shard_map/ppermute | solution.py:313
  590.0 78.0 %collective-permute-start.20 = (f32[256,1024]{1,0:T(8,128)}, f32[256,1024]{1,0:T(8,128)}, u32[]{:S(2)}, u32[]{:S(2)}) collective-permute-start(f32[256,1024]{1,0:T(8,128)} %collective-permute-done.16), channel_id=1, source_target_pairs={{1,0},{2,1},{5,4},{6,5},{9,8},{10,9},{13,12},{14,13},{17,16},{18,1... | collective-permute-start | bytes 3145736 | tf_op jit(solution)/shard_map/ppermute | solution.py:314
  591.3 78.5 %collective-permute-start.18 = (f32[256,1024]{1,0:T(8,128)}, f32[256,1024]{1,0:T(8,128)}, u32[]{:S(2)}, u32[]{:S(2)}) collective-permute-start(f32[256,1024]{1,0:T(8,128)} %collective-permute-done.17), channel_id=1, source_target_pairs={{1,2},{2,3},{5,6},{6,7},{9,10},{10,11},{13,14},{14,15},{17,18},{18... | collective-permute-start | bytes 3145736 | tf_op jit(solution)/shard_map/ppermute | solution.py:313
  612.5 43.5 %collective-permute-start.30 = (f32[256,1024]{1,0:T(8,128)}, f32[256,1024]{1,0:T(8,128)}, u32[]{:S(2)}, u32[]{:S(2)}) collective-permute-start(f32[256,1024]{1,0:T(8,128)} %collective-permute-done.29), channel_id=1, source_target_pairs={{1,0},{5,4},{9,8},{13,12},{17,16},{21,20},{25,24},{29,28}} | collective-permute-start | bytes 3145736 | tf_op jit(solution)/shard_map/ppermute | solution.py:314
  613.8 44.1 %collective-permute-start.28 = (f32[256,1024]{1,0:T(8,128)}, f32[256,1024]{1,0:T(8,128)}, u32[]{:S(2)}, u32[]{:S(2)}) collective-permute-start(f32[256,1024]{1,0:T(8,128)} %collective-permute-done.27), channel_id=1, source_target_pairs={{2,3},{6,7},{10,11},{14,15},{18,19},{22,23},{26,27},{30,31}} | collective-permute-start | bytes 3145736 | tf_op jit(solution)/shard_map/ppermute | solution.py:313
  662.5 40.1 %collective-permute-start.32 = (f32[128,1152]{0,1:T(8,128)}, f32[128,1152]{0,1:T(8,128)}, u32[]{:S(2)}, u32[]{:S(2)}) collective-permute-start(f32[128,1152]{0,1:T(8,128)} %add_add_fusion.7), channel_id=1, source_target_pairs={{2,0},{3,1},{0,2},{1,3},{6,4},{7,5},{4,6},{5,7},{10,8},{11,9},{8,1... | collective-permute-start | bytes 1769480 | tf_op jit(solution)/shard_map/ppermute | solution.py:353
  667.5 35.2 %collective-permute-start.31 = (f32[128,1152]{0,1:T(8,128)}, f32[128,1152]{0,1:T(8,128)}, u32[]{:S(2)}, u32[]{:S(2)}) collective-permute-start(f32[128,1152]{0,1:T(8,128)} %add_add_fusion.8), channel_id=1, source_target_pairs={{1,0},{2,1},{3,2},{0,3},{5,4},{6,5},{7,6},{4,7},{9,8},{10,9},{11,1... | collective-permute-start | bytes 1769480 | tf_op jit(solution)/shard_map/ppermute | solution.py:353
  705.3 38.0 %collective-permute-start.21 = (f32[256,1024]{1,0:T(8,128)}, f32[256,1024]{1,0:T(8,128)}, u32[]{:S(2)}, u32[]{:S(2)}) collective-permute-start(f32[256,1024]{1,0:T(8,128)} %collective-permute-done.20), channel_id=1, source_target_pairs={{1,0},{5,4},{9,8},{13,12},{17,16},{21,20},{25,24},{29,28}} | collective-permute-start | bytes 3145736 | tf_op jit(solution)/shard_map/ppermute | solution.py:314
  706.6 38.5 %collective-permute-start.19 = (f32[256,1024]{1,0:T(8,128)}, f32[256,1024]{1,0:T(8,128)}, u32[]{:S(2)}, u32[]{:S(2)}) collective-permute-start(f32[256,1024]{1,0:T(8,128)} %collective-permute-done.18), channel_id=1, source_target_pairs={{2,3},{6,7},{10,11},{14,15},{18,19},{22,23},{26,27},{30,31}} | collective-permute-start | bytes 3145736 | tf_op jit(solution)/shard_map/ppermute | solution.py:313
  (140 other events, 1522.3 us)
Sparse Core Ops, SparseCore 0:
  55.3 82.4 all-gather.5
  157.3 55.4 all-gather.7
  233.8 118.5 reduce-scatter.3
  355.2 80.1 reduce-scatter.5
  437.7 72.5 all-gather.9
  513.8 128.4 reduce-scatter.7
  645.0 55.4 all-gather.13
  705.4 59.2 all-gather.11

commit v4 on v3

--- a/solution.py
+++ b/solution.py
@@ -47,11 +47,17 @@
 
 
 def over_chunks(count, body, init):
-    if isinstance(count, int):
-        for c in range(count):
-            init = body(c, init)
-        return init
-    return lax.fori_loop(0, count, body, init)
+    for c in range(count):
+        init = body(c, init)
+    return init
+
+
+def by_length(causal, block, total_chunks, work):
+    if not causal:
+        work(total_chunks)
+        return
+    for k in range(total_chunks):
+        pl.when(block == k)(functools.partial(work, k + 1))
 
 
 def ds(c):
@@ -73,34 +79,36 @@
             make_band(x_ref, h, band)
         keys[...] = k_ref[...].T
 
-    count = block + 1 if causal else total_chunks
-    for h in range(2):
-        q = q_ref[h * DH:(h + 1) * DH, :]
-
-        def scores(c, top):
-            s = mm(keys[ds(c), :], q, NN) + band[h, pl.ds(band_at(c, block), QB), :]
-            s_ref[ds(c), :] = s
-            return jnp.maximum(top, part_sum(s, jnp.max))
-
-        top = over_chunks(count, scores, jnp.full((8, QB), NEG, jnp.float32))
-        top = jnp.max(top, axis=0, keepdims=True)
-
-        def weigh(c, tot):
-            e = jnp.exp(s_ref[ds(c), :] - top)
-            s_ref[ds(c), :] = e
-            return tot + part_sum(e, jnp.sum)
-
-        tot = over_chunks(count, weigh, jnp.zeros((8, QB), jnp.float32))
-        tot = jnp.sum(tot, axis=0, keepdims=True)
-        inv = 1.0 / tot
-
-        def mix(c, acc):
-            p = (s_ref[ds(c), :] * inv).astype(jnp.bfloat16)
-            return acc + mm(v_ref[:, ds(c)], p, NN)
-
-        acc = over_chunks(count, mix, jnp.zeros((DH, QB), jnp.float32))
-        o_ref[h * DH:(h + 1) * DH, :] = acc.astype(jnp.bfloat16)
-        l_ref[0, h:h + 1, :] = top + jnp.log(tot)
+    def work(count):
+        for h in range(2):
+            q = q_ref[h * DH:(h + 1) * DH, :]
+
+            def scores(c, top):
+                s = mm(keys[ds(c), :], q, NN) + band[h, pl.ds(band_at(c, block), QB), :]
+                s_ref[ds(c), :] = s
+                return jnp.maximum(top, part_sum(s, jnp.max))
+
+            top = over_chunks(count, scores, jnp.full((8, QB), NEG, jnp.float32))
+            top = jnp.max(top, axis=0, keepdims=True)
+
+            def weigh(c, tot):
+                e = jnp.exp(s_ref[ds(c), :] - top)
+                s_ref[ds(c), :] = e
+                return tot + part_sum(e, jnp.sum)
+
+            tot = over_chunks(count, weigh, jnp.zeros((8, QB), jnp.float32))
+            tot = jnp.sum(tot, axis=0, keepdims=True)
+            inv = 1.0 / tot
+
+            def mix(c, acc):
+                p = (s_ref[ds(c), :] * inv).astype(jnp.bfloat16)
+                return acc + mm(v_ref[:, ds(c)], p, NN)
+
+            acc = over_chunks(count, mix, jnp.zeros((DH, QB), jnp.float32))
+            o_ref[h * DH:(h + 1) * DH, :] = acc.astype(jnp.bfloat16)
+            l_ref[0, h:h + 1, :] = top + jnp.log(tot)
+
+    by_length(causal, block, total_chunks, work)
 
 
 def bwd_kernel(causal, row_ref, x_ref, q_ref, k_ref, v_ref, d_ref, l_ref,
@@ -119,34 +127,36 @@
         dv_ref[...] = jnp.zeros_like(dv_ref)
         near[...] = jnp.zeros_like(near)
 
-    count = block + 1 if causal else total_chunks
-    for h in range(2):
-        q = q_ref[h * DH:(h + 1) * DH, :]
-        d = d_ref[h * DH:(h + 1) * DH, :]
-        log_total = l_ref[0, h:h + 1, :]
-
-        def weigh(c, dot):
-            s = mm(keys[ds(c), :], q, NN) + band[h, pl.ds(band_at(c, block), QB), :]
-            p = jnp.exp(s - log_total)
-            dp = mm(values[ds(c), :], d, NN)
-            p_ref[ds(c), :] = p
-            g_ref[ds(c), :] = dp
-            return dot + part_sum(p * dp, jnp.sum)
-
-        dot = over_chunks(count, weigh, jnp.zeros((8, QB), jnp.float32))
-        dot = jnp.sum(dot, axis=0, keepdims=True)
-
-        def back(c, acc):
-            p = p_ref[ds(c), :]
-            low = (p * (g_ref[ds(c), :] - dot)).astype(jnp.bfloat16)
-            dk_ref[:, ds(c)] += mm(q, low, NT)
-            dv_ref[:, ds(c)] += mm(d, p.astype(jnp.bfloat16), NT)
-            at = pl.ds(band_at(c, block), QB)
-            near[h, at, :] += low.astype(jnp.float32)
-            return acc + mm(k_ref[:, ds(c)], low, NN)
-
-        acc = over_chunks(count, back, jnp.zeros((DH, QB), jnp.float32))
-        dq_ref[h * DH:(h + 1) * DH, :] = acc.astype(jnp.bfloat16)
+    def work(count):
+        for h in range(2):
+            q = q_ref[h * DH:(h + 1) * DH, :]
+            d = d_ref[h * DH:(h + 1) * DH, :]
+            log_total = l_ref[0, h:h + 1, :]
+
+            def weigh(c, dot):
+                s = mm(keys[ds(c), :], q, NN) + band[h, pl.ds(band_at(c, block), QB), :]
+                p = jnp.exp(s - log_total)
+                dp = mm(values[ds(c), :], d, NN)
+                p_ref[ds(c), :] = p
+                g_ref[ds(c), :] = dp
+                return dot + part_sum(p * dp, jnp.sum)
+
+            dot = over_chunks(count, weigh, jnp.zeros((8, QB), jnp.float32))
+            dot = jnp.sum(dot, axis=0, keepdims=True)
+
+            def back(c, acc):
+                p = p_ref[ds(c), :]
+                low = (p * (g_ref[ds(c), :] - dot)).astype(jnp.bfloat16)
+                dk_ref[:, ds(c)] += mm(q, low, NT)
+                dv_ref[:, ds(c)] += mm(d, p.astype(jnp.bfloat16), NT)
+                at = pl.ds(band_at(c, block), QB)
+                near[h, at, :] += low.astype(jnp.float32)
+                return acc + mm(k_ref[:, ds(c)], low, NN)
+
+            acc = over_chunks(count, back, jnp.zeros((DH, QB), jnp.float32))
+            dq_ref[h * DH:(h + 1) * DH, :] = acc.astype(jnp.bfloat16)
+
+    by_length(causal, block, total_chunks, work)
 
     @pl.when(r == pl.num_programs(1) - 1)
     def _():

time: 806 us -> 804 us (level)
  Pallas kernels: 79.3 us -> 64.3 us
  waiting for transfers between devices: 311 us -> 321 us
    ppermute x18, waiting for transfers between devices: 90 us -> 101 us  [exchange(): lax.ppermute(blocks[n - d], 'kv', [((i + d) % n, i) for i in range(n)])]
  transfers between devices with their start and end apart: 43 -> 43, of which waited for: 24 -> 23; matrix products, arithmetic and copies ran while one was open for 24% -> 24% of each run, Pallas kernels for 10% -> 8%
where the time goes in v4:
time: 804 us; the launch traced here: 794 us
  waiting for transfers between devices  321 us (40%)
  local copies, waits for them, and re-layouts  116 us (14%)
  starting transfers between devices  105 us (13%)
  matrix products  90.7 us (11%)
  Pallas kernels  64.3 us (8%)
  other arithmetic  61.7 us (8%)
  between operations  34.3 us (4%)
    ppermute x18, waiting for transfers between devices, exchange(): lax.ppermute(blocks[n - d], 'kv', [((i + d) % n, i) for i in range(n)])  101 us
    ppermute x6, waiting for transfers between devices, hop(): lax.ppermute(tie(self.left, *others), 'kv', [(i + 1, i) for i in range(n...  91 us
    dot_general x45, matrix products, mm(): lax.dot_general(a, b, (dims, ((), ())), preferred_element_type=jnp.float32)  71.9 us
    ppermute x18, starting transfers between devices, exchange(): lax.ppermute(blocks[n - d], 'kv', [((i + d) % n, i) for i in range(n)])  62.8 us
    unnamed x258, local copies, waits for them, and re-layouts  46.9 us
    pallas_call x2, Pallas kernels, attend_back(): pl.pallas_call(functools.partial(bwd_kernel, causal), out_shape=[jax.Shap...  35.2 us
    reduce_scatter x1, waiting for transfers between devices, on_device(): sums = lax.psum_scatter(sums, 'batch', tiled=True)  30.5 us
    slice x26, local copies, waits for them, and re-layouts, tie(): x = x + other[(0,) * other.ndim].astype(jnp.float32) * (one - 1.0)  26.8 us
  transfers between devices with their start and end apart: 43, of which 23 were waited for; matrix products, arithmetic and copies ran while one was open for 24% of the time, Pallas kernels for 8%

profile of v4, /device:TPU:0, one launch (start us, length us, event | category | flops | bytes accessed | tf_op | source)
XLA Modules:
  0.0 793.7 jit_solution(7207779618895582858)
XLA Ops:
  28.4 9.6 %attend.2 = (bf16[256,1024]{1,0:T(8,128)(2,1)S(1)}, f32[2,2,1024]{2,1,0:T(2,128)S(1)}) custom-call(s32[1]{0:T(128)} %constant.172.clone.1.row_ref, f32[2,8,256]{2,1,0:T(8,128)S(1)} %pad_maximum_fusion.12.x_ref, bf16[256,1024]{1,0:T(8,128)(2,1)S(1)} %fusion.36.q_ref, bf16[256,1024]{1,0:T(8,128)(2,1)S(1)} %convolution_convert_fusion.3.k_ref.v_ref, ...), custom_call_target="tpu_custom_call" | custom-call | bytes 46137344 | tf_op jit(solution)/shard_map/attend/pallas_call | solution.py:202
  39.9 12.5 %collective-permute-done.1 = f32[256,512]{1,0:T(8,128)} collective-permute-done((f32[256,512]{1,0:T(8,128)}, f32[256,512]{1,0:T(8,128)}, u32[]{:S(2)}, u32[]{:S(2)}) %collective-permute-start.1) | collective-permute-done | bytes 524320 | tf_op jit(solution)/shard_map/ppermute | solution.py:363
  64.4 11.7 %collective-permute-start.5 = (f32[272,256]{1,0:T(8,128)}, f32[272,256]{1,0:T(8,128)}, u32[]{:S(2)}, u32[]{:S(2)}) collective-permute-start(f32[272,256]{1,0:T(8,128)} %get-tuple-element.196), channel_id=1, source_target_pairs={{3,0},{0,1},{1,2},{2,3},{7,4},{4,5},{5,6},{6,7},{11,8},{8,9},{9,10... | collective-permute-start | bytes 835592 | tf_op jit(solution)/shard_map/ppermute | solution.py:363
  87.0 8.3 %collective-permute-done.4 = f32[272,256]{1,0:T(8,128)} collective-permute-done((f32[272,256]{1,0:T(8,128)}, f32[272,256]{1,0:T(8,128)}, u32[]{:S(2)}, u32[]{:S(2)}) %collective-permute-start.4) | collective-permute-done | bytes 278560 | tf_op jit(solution)/shard_map/ppermute | solution.py:363
  112.4 25.4 %all-gather.6.cloned.1.call-done.shares_ref = f32[8,3,256,512]{3,2,1,0:T(8,128)} async-done(((f32[1,3,256,512]{3,2,1,0:T(8,128)}), f32[8,3,256,512]{3,2,1,0:T(8,128)}) %all-gather.6.cloned.1.call-update) | async-done | bytes 12582928 | tf_op jit(solution)/shard_map/all_gather | solution.py:492
  166.4 12.3 %attend.3 = (bf16[1024,256]{1,0:T(8,128)(2,1)S(1)}, f32[8,2,256]{2,1,0:T(2,128)S(1)}) custom-call(s32[1]{0:T(128)} %bitcast.18.row_ref, f32[8,8,256]{2,1,0:T(8,128)S(1)} %get-tuple-element.188.x_ref, bf16[1024,256]{1,0:T(8,128)(2,1)S(1)} %bitcast.303, bf16[1024,1024]{1,0:T(8,128)(2,1)S(1)} %bitcast.295, bf16[1024,1024]{1,0:T(8,128)(2,1)S(1)} %bitcast.296), custom_call_target="tpu_custom_call" | custom-call | bytes 46137344 | tf_op jit(solution)/shard_map/attend/pallas_call | solution.py:202
  184.6 20.6 %collective-permute-done.7 = f32[256,1024]{1,0:T(8,128)S(1)} collective-permute-done((f32[256,1024]{1,0:T(8,128)S(1)}, f32[256,1024]{1,0:T(8,128)S(1)}, u32[]{:S(2)}, u32[]{:S(2)}) %collective-permute-start.7) | collective-permute-done | bytes 1048608 | tf_op jit(solution)/shard_map/ppermute | solution.py:525
  248.2 18.1 %collective-permute-done.8 = f32[256,1024]{1,0:T(8,128)S(1)} collective-permute-done((f32[256,1024]{1,0:T(8,128)S(1)}, f32[256,1024]{1,0:T(8,128)S(1)}, u32[]{:S(2)}, u32[]{:S(2)}) %collective-permute-start.8) | collective-permute-done | bytes 1048608 | tf_op jit(solution)/shard_map/ppermute | solution.py:543
  276.2 21.3 %attend_back.2 = (bf16[1024,256]{1,0:T(8,128)(2,1)S(1)}, bf16[4,2,2,64,1024]{4,3,2,1,0:T(8,128)(2,1)S(1)}, f32[8,10,256]{2,1,0:T(8,128)S(1)}) custom-call(s32[1]{0:T(128)} %bitcast.18.row_ref, f32[8,8,256]{2,1,0:T(8,128)S(1)} %get-tuple-element.188.x_ref, bf16[1024,256]{1,0:T(8,128)(2,1)S(1)} %bitcast.304, bf16[1024,1024]{1,0:T(8,128)(2,1)S(1)} %bitcast.297, ...), custom_call_target="tpu_custom_call" | custom-call | bytes 75497472 | tf_op jit(solution)/shard_map/attend_back/pallas_call | solution.py:220
  358.0 11.2 %collective-permute-done.23 = f32[128,512]{1,0:T(8,128)} collective-permute-done((f32[128,512]{1,0:T(8,128)}, f32[128,512]{1,0:T(8,128)}, u32[]{:S(2)}, u32[]{:S(2)}) %collective-permute-start.23) | collective-permute-done | bytes 262176 | tf_op jit(solution)/shard_map/ppermute | solution.py:363
  398.2 13.9 %attend_back.3 = (bf16[256,1024]{1,0:T(8,128)(2,1)S(1)}, bf16[1,2,2,64,1024]{4,3,2,1,0:T(8,128)(2,1)S(1)}, f32[2,10,256]{2,1,0:T(8,128)S(1)}) custom-call(s32[1]{0:T(128)} %constant.172.clone.1.row_ref, f32[2,8,256]{2,1,0:T(8,128)S(1)} %pad_maximum_fusion.12.x_ref, bf16[256,1024]{1,0:T(8,128)(2,1)S(1)} %copy-done.10, ...), custom_call_target="tpu_custom_call" | custom-call | bytes 75497472 | tf_op jit(solution)/shard_map/attend_back/pallas_call | solution.py:220
  414.3 21.7 %collective-permute-start.15 = (f32[512,256]{1,0:T(8,128)}, f32[512,256]{1,0:T(8,128)}, u32[]{:S(2)}, u32[]{:S(2)}) collective-permute-start(f32[512,256]{1,0:T(8,128)} %get-tuple-element.156), channel_id=1, source_target_pairs={{3,0},{0,1},{1,2},{2,3},{7,4},{4,5},{5,6},{6,7},{11,8},{8,9},{9,10... | collective-permute-start | bytes 1572872 | tf_op jit(solution)/shard_map/ppermute | solution.py:363
  453.9 18.2 %collective-permute-done.14 = f32[512,256]{1,0:T(8,128)} collective-permute-done((f32[512,256]{1,0:T(8,128)}, f32[512,256]{1,0:T(8,128)}, u32[]{:S(2)}, u32[]{:S(2)}) %collective-permute-start.14) | collective-permute-done | bytes 524320 | tf_op jit(solution)/shard_map/ppermute | solution.py:363
  479.3 8.8 %collective-permute-start.34 = (f32[3,88,1024]{2,1,0:T(8,128)}, f32[3,88,1024]{2,1,0:T(8,128)}, u32[]{:S(2)}, u32[]{:S(2)}) collective-permute-start(f32[3,88,1024]{2,1,0:T(8,128)} %fusion.38), channel_id=1, source_target_pairs={{0,2},{1,3},{2,0},{3,1},{4,6},{5,7},{6,4},{7,5},{8,10},{9,11},{10,... | collective-permute-start | bytes 3244040 | tf_op jit(solution)/shard_map/ppermute | solution.py:645
  492.5 21.1 %all-gather.10.cloned.1.call-done = f32[3,1024,512]{2,1,0:T(8,128)} async-done(((f32[3,128,512]{2,1,0:T(8,128)}), f32[3,1024,512]{2,1,0:T(8,128)}) %all-gather.10.cloned.1.call-update) | async-done | bytes 6291472 | tf_op jit(solution)/shard_map/all_gather | solution.py:584
  521.9 13.7 %collective-permute-done.34 = f32[3,88,1024]{2,1,0:T(8,128)} collective-permute-done((f32[3,88,1024]{2,1,0:T(8,128)}, f32[3,88,1024]{2,1,0:T(8,128)}, u32[]{:S(2)}, u32[]{:S(2)}) %collective-permute-start.34) | collective-permute-done | bytes 1081376 | tf_op jit(solution)/shard_map/ppermute | solution.py:645
  553.5 13.6 %collective-permute-done.25 = f32[256,1024]{1,0:T(8,128)S(1)} collective-permute-done((f32[256,1024]{1,0:T(8,128)}, f32[256,1024]{1,0:T(8,128)S(1)}, u32[]{:S(2)}, u32[]{:S(2)}) %collective-permute-start.25) | collective-permute-done | bytes 1048608 | tf_op jit(solution)/shard_map/ppermute | solution.py:324
  570.3 19.4 %collective-permute-done.16 = f32[256,1024]{1,0:T(8,128)} collective-permute-done((f32[256,1024]{1,0:T(8,128)S(1)}, f32[256,1024]{1,0:T(8,128)}, u32[]{:S(2)}, u32[]{:S(2)}) %collective-permute-start.16) | collective-permute-done | bytes 1048608 | tf_op jit(solution)/shard_map/ppermute | solution.py:324
  592.7 19.5 %collective-permute-done.29 = f32[256,1024]{1,0:T(8,128)} collective-permute-done((f32[256,1024]{1,0:T(8,128)S(1)}, f32[256,1024]{1,0:T(8,128)}, u32[]{:S(2)}, u32[]{:S(2)}) %collective-permute-start.29) | collective-permute-done | bytes 1048608 | tf_op jit(solution)/shard_map/ppermute | solution.py:324
  615.1 30.5 %reduce-scatter.8.cloned.1.call-done = f32[128,4736]{0,1:T(8,128)} async-done(((f32[1024,4736]{0,1:T(8,128)}), f32[128,4736]{0,1:T(8,128)}) %reduce-scatter.8.cloned.1.call-update) | async-done | bytes 2424848 | tf_op jit(solution)/shard_map/reduce_scatter | solution.py:634
  671.2 7.5 collective-permute-done.33
  678.7 23.5 %collective-permute-done.32 = f32[128,1152]{0,1:T(8,128)} collective-permute-done((f32[128,1152]{0,1:T(8,128)}, f32[128,1152]{0,1:T(8,128)}, u32[]{:S(2)}, u32[]{:S(2)}) %collective-permute-start.32) | collective-permute-done | bytes 589856 | tf_op jit(solution)/shard_map/ppermute | solution.py:363
  709.7 33.0 %collective-permute-done.21 = f32[256,1024]{1,0:T(8,128)} collective-permute-done((f32[256,1024]{1,0:T(8,128)}, f32[256,1024]{1,0:T(8,128)}, u32[]{:S(2)}, u32[]{:S(2)}) %collective-permute-start.21) | collective-permute-done | bytes 1048608 | tf_op jit(solution)/shard_map/ppermute | solution.py:324
  757.8 7.4 slice_bitcast_fusion
  (535 shorter events, 356.7 us)
Async XLA Ops:
  7.2 130.6 %all-gather.6.cloned.1.call-start = ((), (), s32[]{:S(2)}) async-start(), calls=%async_computation.3 | async-start | bytes 14155776 | tf_op jit(solution)/shard_map/all_gather | solution.py:492
  15.5 36.9 %collective-permute-start.1 = (f32[256,512]{1,0:T(8,128)}, f32[256,512]{1,0:T(8,128)}, u32[]{:S(2)}, u32[]{:S(2)}) collective-permute-start(f32[256,512]{1,0:T(8,128)} %constant_dynamic-update-slice_fusion.2), channel_id=1, source_target_pairs={{2,0},{3,1},{0,2},{1,3},{6,4},{7,5},{4,6},{5,7},{10,8},{11,9},{8,1... | collective-permute-start | bytes 1572872 | tf_op jit(solution)/shard_map/ppermute | solution.py:363
  55.1 159.5 %all-gather.8.cloned.1.call-start = ((), (), s32[]{:S(2)}) async-start(), calls=%async_computation.4 | async-start | bytes 9732096 | tf_op jit(solution)/shard_map/all_gather | solution.py:508
  101.5 53.3 %collective-permute-start.6 = (f32[3,88,1024]{2,1,0:T(8,128)}, f32[3,88,1024]{2,1,0:T(8,128)}, u32[]{:S(2)}, u32[]{:S(2)}) collective-permute-start(f32[3,88,1024]{2,1,0:T(8,128)} %add_add_fusion.3), channel_id=1, source_target_pairs={{0,2},{1,3},{2,0},{3,1},{4,6},{5,7},{6,4},{7,5},{8,10},{9,11},{10,... | collective-permute-start | bytes 3244040 | tf_op jit(solution)/shard_map/ppermute | solution.py:507
  157.2 196.3 %reduce-scatter.4.cloned.1.call-start = ((), (), s32[]{:S(2)}) async-start(), calls=%async_computation.5 | async-start | bytes 19464192 | tf_op jit(solution)/shard_map/reduce_scatter | solution.py:551
  233.6 257.0 %reduce-scatter.6.cloned.1.call-start = ((), (), s32[]{:S(2)}) async-start(), calls=%async_computation.7 | async-start | bytes 5242880 | tf_op jit(solution)/shard_map/reduce_scatter | solution.py:580
  338.4 175.1 %all-gather.10.cloned.1.call-start = ((), (), s32[]{:S(2)}) async-start(), calls=%async_computation.6 | async-start | bytes 7077888 | tf_op jit(solution)/shard_map/all_gather | solution.py:584
  372.6 273.0 %reduce-scatter.8.cloned.1.call-start = ((), (), s32[]{:S(2)}) async-start(), calls=%async_computation.8 | async-start | bytes 21823488 | tf_op jit(solution)/shard_map/reduce_scatter | solution.py:634
  414.3 37.8 %collective-permute-start.15 = (f32[512,256]{1,0:T(8,128)}, f32[512,256]{1,0:T(8,128)}, u32[]{:S(2)}, u32[]{:S(2)}) collective-permute-start(f32[512,256]{1,0:T(8,128)} %get-tuple-element.156), channel_id=1, source_target_pairs={{3,0},{0,1},{1,2},{2,3},{7,4},{4,5},{5,6},{6,7},{11,8},{8,9},{9,10... | collective-permute-start | bytes 1572872 | tf_op jit(solution)/shard_map/ppermute | solution.py:363
  436.0 38.0 %collective-permute-start.13 = (f32[512,256]{1,0:T(8,128)}, f32[512,256]{1,0:T(8,128)}, u32[]{:S(2)}, u32[]{:S(2)}) collective-permute-start(f32[512,256]{1,0:T(8,128)} %get-tuple-element.155), channel_id=1, source_target_pairs={{1,0},{2,1},{3,2},{0,3},{5,4},{6,5},{7,6},{4,7},{9,8},{10,9},{11,1... | collective-permute-start | bytes 1572872 | tf_op jit(solution)/shard_map/ppermute | solution.py:363
  476.7 281.1 %all-gather.14.cloned.1.call-start = ((), (), s32[]{:S(2)}) async-start(), calls=%async_computation.10 | async-start | bytes 9732096 | tf_op jit(solution)/shard_map/all_gather | solution.py:646
  479.3 56.4 %collective-permute-start.34 = (f32[3,88,1024]{2,1,0:T(8,128)}, f32[3,88,1024]{2,1,0:T(8,128)}, u32[]{:S(2)}, u32[]{:S(2)}) collective-permute-start(f32[3,88,1024]{2,1,0:T(8,128)} %fusion.38), channel_id=1, source_target_pairs={{0,2},{1,3},{2,0},{3,1},{4,6},{5,7},{6,4},{7,5},{8,10},{9,11},{10,... | collective-permute-start | bytes 3244040 | tf_op jit(solution)/shard_map/ppermute | solution.py:645
  538.9 226.4 %all-gather.12.cloned.1.call-start = ((), (), s32[]{:S(2)}) async-start(), calls=%async_computation.9 | async-start | bytes 7667712 | tf_op jit(solution)/shard_map/all_gather | solution.py:647
  546.7 43.0 %collective-permute-start.16 = (f32[256,1024]{1,0:T(8,128)S(1)}, f32[256,1024]{1,0:T(8,128)}, u32[]{:S(2)}, u32[]{:S(2)}) collective-permute-start(f32[256,1024]{1,0:T(8,128)S(1)} %fusion.104), channel_id=1, source_target_pairs={{1,0},{2,1},{3,2},{5,4},{6,5},{7,6},{9,8},{10,9},{11,10},{13,12},{... | collective-permute-start | bytes 3145736 | tf_op jit(solution)/shard_map/ppermute | solution.py:324
  548.0 43.0 %collective-permute-start.17 = (f32[256,1024]{1,0:T(8,128)S(1)}, f32[256,1024]{1,0:T(8,128)}, u32[]{:S(2)}, u32[]{:S(2)}) collective-permute-start(f32[256,1024]{1,0:T(8,128)S(1)} %fusion.104), channel_id=1, source_target_pairs={{0,1},{1,2},{2,3},{4,5},{5,6},{6,7},{8,9},{9,10},{10,11},{12,13},{... | collective-permute-start | bytes 3145736 | tf_op jit(solution)/shard_map/ppermute | solution.py:323
  567.1 45.0 %collective-permute-start.29 = (f32[256,1024]{1,0:T(8,128)S(1)}, f32[256,1024]{1,0:T(8,128)}, u32[]{:S(2)}, u32[]{:S(2)}) collective-permute-start(f32[256,1024]{1,0:T(8,128)S(1)} %collective-permute-done.25), channel_id=1, source_target_pairs={{1,0},{2,1},{5,4},{6,5},{9,8},{10,9},{13,12},{14,13},{17,16},{18,1... | collective-permute-start | bytes 3145736 | tf_op jit(solution)/shard_map/ppermute | solution.py:324
  568.7 44.8 %collective-permute-start.27 = (f32[256,1024]{1,0:T(8,128)S(1)}, f32[256,1024]{1,0:T(8,128)}, u32[]{:S(2)}, u32[]{:S(2)}) collective-permute-start(f32[256,1024]{1,0:T(8,128)S(1)} %collective-permute-done.26), channel_id=1, source_target_pairs={{1,2},{2,3},{5,6},{6,7},{9,10},{10,11},{13,14},{14,15},{17,18},{18... | collective-permute-start | bytes 3145736 | tf_op jit(solution)/shard_map/ppermute | solution.py:323
  589.7 77.9 %collective-permute-start.20 = (f32[256,1024]{1,0:T(8,128)}, f32[256,1024]{1,0:T(8,128)}, u32[]{:S(2)}, u32[]{:S(2)}) collective-permute-start(f32[256,1024]{1,0:T(8,128)} %collective-permute-done.16), channel_id=1, source_target_pairs={{1,0},{2,1},{5,4},{6,5},{9,8},{10,9},{13,12},{14,13},{17,16},{18,1... | collective-permute-start | bytes 3145736 | tf_op jit(solution)/shard_map/ppermute | solution.py:324
  591.0 78.4 %collective-permute-start.18 = (f32[256,1024]{1,0:T(8,128)}, f32[256,1024]{1,0:T(8,128)}, u32[]{:S(2)}, u32[]{:S(2)}) collective-permute-start(f32[256,1024]{1,0:T(8,128)} %collective-permute-done.17), channel_id=1, source_target_pairs={{1,2},{2,3},{5,6},{6,7},{9,10},{10,11},{13,14},{14,15},{17,18},{18... | collective-permute-start | bytes 3145736 | tf_op jit(solution)/shard_map/ppermute | solution.py:323
  612.1 43.4 %collective-permute-start.30 = (f32[256,1024]{1,0:T(8,128)}, f32[256,1024]{1,0:T(8,128)}, u32[]{:S(2)}, u32[]{:S(2)}) collective-permute-start(f32[256,1024]{1,0:T(8,128)} %collective-permute-done.29), channel_id=1, source_target_pairs={{1,0},{5,4},{9,8},{13,12},{17,16},{21,20},{25,24},{29,28}} | collective-permute-start | bytes 3145736 | tf_op jit(solution)/shard_map/ppermute | solution.py:324
  613.4 44.0 %collective-permute-start.28 = (f32[256,1024]{1,0:T(8,128)}, f32[256,1024]{1,0:T(8,128)}, u32[]{:S(2)}, u32[]{:S(2)}) collective-permute-start(f32[256,1024]{1,0:T(8,128)} %collective-permute-done.27), channel_id=1, source_target_pairs={{2,3},{6,7},{10,11},{14,15},{18,19},{22,23},{26,27},{30,31}} | collective-permute-start | bytes 3145736 | tf_op jit(solution)/shard_map/ppermute | solution.py:323
  662.1 40.0 %collective-permute-start.32 = (f32[128,1152]{0,1:T(8,128)}, f32[128,1152]{0,1:T(8,128)}, u32[]{:S(2)}, u32[]{:S(2)}) collective-permute-start(f32[128,1152]{0,1:T(8,128)} %add_add_fusion.7), channel_id=1, source_target_pairs={{2,0},{3,1},{0,2},{1,3},{6,4},{7,5},{4,6},{5,7},{10,8},{11,9},{8,1... | collective-permute-start | bytes 1769480 | tf_op jit(solution)/shard_map/ppermute | solution.py:363
  704.8 37.9 %collective-permute-start.21 = (f32[256,1024]{1,0:T(8,128)}, f32[256,1024]{1,0:T(8,128)}, u32[]{:S(2)}, u32[]{:S(2)}) collective-permute-start(f32[256,1024]{1,0:T(8,128)} %collective-permute-done.20), channel_id=1, source_target_pairs={{1,0},{5,4},{9,8},{13,12},{17,16},{21,20},{25,24},{29,28}} | collective-permute-start | bytes 3145736 | tf_op jit(solution)/shard_map/ppermute | solution.py:324
  706.1 38.4 %collective-permute-start.19 = (f32[256,1024]{1,0:T(8,128)}, f32[256,1024]{1,0:T(8,128)}, u32[]{:S(2)}, u32[]{:S(2)}) collective-permute-start(f32[256,1024]{1,0:T(8,128)} %collective-permute-done.18), channel_id=1, source_target_pairs={{2,3},{6,7},{10,11},{14,15},{18,19},{22,23},{26,27},{30,31}} | collective-permute-start | bytes 3145736 | tf_op jit(solution)/shard_map/ppermute | solution.py:323
  (140 other events, 1520.4 us)
Sparse Core Ops, SparseCore 0:
  55.3 82.4 all-gather.5
  157.3 55.4 all-gather.7
  233.8 118.5 reduce-scatter.3
  355.2 85.2 reduce-scatter.5
  442.9 70.6 all-gather.9
  517.1 128.4 reduce-scatter.7
  648.2 55.4 all-gather.13
  705.8 58.7 all-gather.11
